TPU v7x, 128 devices: a whole 4x4x4 slice. The times are simulated.
128 devices in a mesh: row: 8 (over x_hi, y), col: 16 (over z, x_lo, core).
Axes of the slice: x: 4 (x_hi: 2, x_lo: 2; x = x_hi * 2 + x_lo), y: 4, z: 4, core: 2. Of those that a mesh axis runs over, the one named last changes fastest.
Arguments:
- object_one: float32 [2, 2048, 4096], P(None, 'row', 'col'), may hold values from -5 to 5
- object_two: float32 [2, 2048, 4096], P(None, 'row', 'col'), may hold values from -5 to 5
- probe: float32 [2, 256, 256], replicated, may hold values from -6 to 6
- scan_pos: int32 [8, 16, 8, 2], P('row', 'col'), may hold values from 0 to 255
- pattern_index: int32 [8, 16, 8], P('row', 'col'), may hold values from 0 to 7, each once within a row
- measured: float32 [8, 16, 8, 256, 256], P('row', 'col'), may hold values from 0 to 3
Outputs:
- grad_one: float32 [2, 2048, 4096], P(None, 'row', 'col')
- grad_two: float32 [2, 2048, 4096], P(None, 'row', 'col')
- probe_step: float32 [2, 256, 256], replicated
Inputs may be any that keep to these rules, and one draw needn't show every extreme that they name: For each tile (r, c), pattern_index[r, c] names each of that tile's 8 patterns exactly once.
All inputs are finite; a program needn't handle non-finite values.
Results may differ from a plain program's by a relative error of at most 0.00015.
Values sent between devices are 32-bit elements; how exact they have to be, the bound alone decides.
No kernel may reach another device: no remote copies, remote signals or barrier semaphores. Data moves between devices by JAX's collectives and lax.ppermute only.
A program may use at most 128 MiB of HBM per device.

v0:
```python
import math

import jax
import jax.numpy as jnp
from jax import lax
from jax.sharding import PartitionSpec as P

phase_rate = 0.002


def padded(shard, sides, width):
    for axis, dim in sides:
        size, length = (lax.axis_size(axis), shard.shape[dim])
        up = [(i, (i + 1) % size) for i in range(size - 1)]
        down = [(j, i) for i, j in up]
        last = lax.slice_in_dim(shard, length - width, length, axis=dim)
        leading = lax.slice_in_dim(shard, 0, width, axis=dim)
        before = lax.ppermute(last, axis, up)
        after = lax.ppermute(leading, axis, down)
        shard = jnp.concatenate([before, shard, after], axis=dim)
    return shard


def passed_along(block, axis, distance):
    devices = range(lax.axis_size(axis))
    route = [(i - distance, i) for i in devices if i - distance in devices]
    return lax.ppermute(block, axis, route)


def dft_tables(window, float_type):
    counter = jnp.arange(window, dtype=jnp.int32)
    turn_count = counter[:, None] * counter[None, :] % window
    angles = -2.0 * math.pi / window * turn_count.astype(float_type)
    weight = 1.0 / math.sqrt(window)
    return (jnp.cos(angles) * weight, jnp.sin(angles) * weight)


def fresnel(window, float_type):
    counter = jnp.arange(window, dtype=jnp.int32)
    frequency = jnp.where(counter < window // 2, counter, counter - window).astype(float_type)
    phases = -phase_rate * (frequency[:, None] ** 2 + frequency[None, :] ** 2)
    return (jnp.cos(phases), jnp.sin(phases))


def left_product(table, field):
    return jnp.einsum("aj,njk->nak", table, field, precision=lax.Precision.HIGHEST)


def right_product(field, table):
    return jnp.einsum("nak,kb->nab", field, table, precision=lax.Precision.HIGHEST)


def transform(real_part, imag_part, table_re, table_im):
    upper_re = left_product(table_re, real_part) - left_product(table_im, imag_part)
    upper_im = left_product(table_re, imag_part) + left_product(table_im, real_part)
    return (
        right_product(upper_re, table_re) - right_product(upper_im, table_im),
        right_product(upper_re, table_im) + right_product(upper_im, table_re),
    )


def complex_mul(left_re, left_im, right_re, right_im):
    return (left_re * right_re - left_im * right_im, left_re * right_im + left_im * right_re)


def widen(plane, rim_width):
    return padded(plane, (("row", 1), ("col", 2)), rim_width)


def windows_of(plane, starts, window):
    zero_index = jnp.zeros((), jnp.int32)

    def take_window(anchor):
        return lax.dynamic_slice(plane, (zero_index, anchor[0], anchor[1]), (2, window, window))

    windows = jax.vmap(take_window)(starts)
    return (windows[:, 0], windows[:, 1])


def spread(term_re, term_im, starts, tile_size, window):
    extent = tile_size + window
    initial = jnp.zeros((2, extent, extent), term_re.dtype)
    zero_index = jnp.zeros((), jnp.int32)

    def add_piece(position, accumulated):
        anchor = starts[position]
        place = (zero_index, anchor[0], anchor[1])
        current = lax.dynamic_slice(accumulated, place, (2, window, window))
        addend = jnp.stack([term_re[position], term_im[position]])
        return lax.dynamic_update_slice(accumulated, current + addend, place)

    return lax.fori_loop(0, term_re.shape[0], add_piece, initial)


def fold_back(gradient, tile_size, rim_width):
    inner_end = tile_size + rim_width
    interior = gradient[:, rim_width:inner_end, rim_width:inner_end]
    top_edge = gradient[:, :rim_width, rim_width:inner_end]
    bottom_edge = gradient[:, inner_end:, rim_width:inner_end]
    left_edge = gradient[:, rim_width:inner_end, :rim_width]
    right_edge = gradient[:, rim_width:inner_end, inner_end:]
    edge_below = passed_along(top_edge, "row", -1)
    edge_above = passed_along(bottom_edge, "row", 1)
    edge_after = passed_along(left_edge, "col", -1)
    edge_before = passed_along(right_edge, "col", 1)
    upper_left = gradient[:, :rim_width, :rim_width]
    upper_right = gradient[:, :rim_width, inner_end:]
    lower_left = gradient[:, inner_end:, :rim_width]
    lower_right = gradient[:, inner_end:, inner_end:]
    upper_left, upper_right = passed_along((upper_left, upper_right), "row", -1)
    lower_left, lower_right = passed_along((lower_left, lower_right), "row", 1)
    upper_left, lower_left = passed_along((upper_left, lower_left), "col", -1)
    upper_right, lower_right = passed_along((upper_right, lower_right), "col", 1)
    low_start = tile_size - rim_width
    interior = interior.at[:, low_start:, :].add(edge_below)
    interior = interior.at[:, :rim_width, :].add(edge_above)
    interior = interior.at[:, :, low_start:].add(edge_after)
    interior = interior.at[:, :, :rim_width].add(edge_before)
    interior = interior.at[:, low_start:, low_start:].add(upper_left)
    interior = interior.at[:, low_start:, :rim_width].add(upper_right)
    interior = interior.at[:, :rim_width, low_start:].add(lower_left)
    interior = interior.at[:, :rim_width, :rim_width].add(lower_right)
    return interior


def body(object_one, object_two, probe, scan_pos, pattern_index, measured):
    tile_size = object_one.shape[1]
    window = probe.shape[-1]
    rim_width = window // 2
    float_type = probe.dtype
    table_re, table_im = dft_tables(window, float_type)
    kernel_re, kernel_im = fresnel(window, float_type)
    starts = scan_pos[0, 0]
    wide_one = widen(object_one, rim_width)
    wide_two = widen(object_two, rim_width)
    one_re, one_im = windows_of(wide_one, starts, window)
    wave_re, wave_im = complex_mul(probe[0], probe[1], one_re, one_im)
    spec_re, spec_im = transform(wave_re, wave_im, table_re, table_im)
    spec_re, spec_im = complex_mul(spec_re, spec_im, kernel_re, kernel_im)
    prop_re, prop_im = transform(spec_re, spec_im, table_re, -table_im)
    two_re, two_im = windows_of(wide_two, starts, window)
    exit_re, exit_im = complex_mul(prop_re, prop_im, two_re, two_im)
    far_re, far_im = transform(exit_re, exit_im, table_re, table_im)
    amplitude = jnp.take(measured[0, 0], pattern_index[0, 0], axis=0)
    magnitude = jnp.sqrt(far_re * far_re + far_im * far_im + 1.0)
    factor = (magnitude - amplitude) / magnitude
    back_re, back_im = transform(factor * far_re, factor * far_im, table_re, -table_im)
    term_re, term_im = complex_mul(prop_re, -prop_im, back_re, back_im)
    spread_two = spread(term_re, term_im, starts, tile_size, window)
    inner_re, inner_im = complex_mul(two_re, -two_im, back_re, back_im)
    spec_re, spec_im = transform(inner_re, inner_im, table_re, table_im)
    spec_re, spec_im = complex_mul(spec_re, spec_im, kernel_re, -kernel_im)
    entry_re, entry_im = transform(spec_re, spec_im, table_re, -table_im)
    term_re, term_im = complex_mul(probe[0], -probe[1], entry_re, entry_im)
    spread_one = spread(term_re, term_im, starts, tile_size, window)
    grad_two = fold_back(spread_two, tile_size, rim_width)
    grad_one = fold_back(spread_one, tile_size, rim_width)
    share_re, share_im = complex_mul(one_re, -one_im, entry_re, entry_im)
    numerator = jnp.stack([jnp.sum(share_re, 0), jnp.sum(share_im, 0)])
    illumination = jnp.sum(one_re * one_re + one_im * one_im, 0)
    numerator, illumination = lax.psum((numerator, illumination), ("row", "col"))
    probe_step = numerator * lax.rsqrt(illumination + 1.0)
    return (grad_one, grad_two, probe_step)


def solution(mesh):
    placed = (
        P(None, "row", "col"),
        P(None, "row", "col"),
        P(),
        P("row", "col", None, None),
        P("row", "col", None),
        P("row", "col", None, None, None),
    )
    return jax.shard_map(
        body,
        mesh=mesh,
        in_specs=placed,
        out_specs=(P(None, "row", "col"), P(None, "row", "col"), P()),
        check_vma=False,
    )
```

profile of v0, /device:TPU:7, one launch (start us, length us, event | category | flops | bytes accessed | tf_op | source)
XLA Modules:
  0.0 774.8 jit_solution(1358459712921081292)
XLA Ops:
  22.0 7.0 collective-permute-start.1
  61.0 24.5 %while.47 = (s32[]{:T(128)}, f32[2,512,512]{2,1,0:T(8,128)S(1)}, s32[8,3]{0,1:T(4,128)S(1)}, f32[8,2,256,256]{3,2,0,1:T(8,128)}, s32[]{:T(128)}) while((s32[]{:T(128)}, f32[2,512,512]{2,1,0:T(8,128)S(1)}, s32[8,3]{0,1:T(4,128)S(1)}, f32[8,2,256,256]{3,2,0,1:T(8,128)}, s32[]{:T(128)}) %tuple.191), condition=%wide.while_cond.17, body=%wide.while_body.17.sunk | while | flops 2 | bytes 1050217 | solution.py:74
  85.5 6.9 fusion.167
  150.7 6.0 convolution_subtract_fusion.4
  161.9 32.6 %while.46 = (s32[]{:T(128)}, f32[2,512,512]{2,1,0:T(8,128)}, s32[8,3]{0,1:T(4,128)S(1)}, f32[8,2,256,256]{3,2,0,1:T(8,128)}, s32[]{:T(128)}) while((s32[]{:T(128)}, f32[2,512,512]{2,1,0:T(8,128)}, s32[8,3]{0,1:T(4,128)S(1)}, f32[8,2,256,256]{3,2,0,1:T(8,128)}, s32[]{:T(128)}) %tuple.206), condition=%wide.while_cond.16, body=%wide.while_body.16.sunk | while | flops 2 | bytes 1050217 | solution.py:74
  194.5 6.2 fusion.66
  276.2 7.5 multiply_add_fusion
  320.6 6.1 fusion.104
  335.9 6.1 fusion
  349.4 106.6 %while.45 = (s32[]{:T(128)}, f32[2,512,512]{2,1,0:T(8,128)}, s32[8,2]{0,1:T(2,128)S(1)}, f32[8,256,256]{2,1,0:T(8,128)}, f32[8,256,256]{2,1,0:T(8,128)}, /*index=5*/s32[]{:T(128)}, s32[]{:T(128)}, s32[]{:T(128)}) while((s32[]{:T(128)}, f32[2,512,512]{2,1,0:T(8,128)}, s32[8,2]{0,1:T(2,128)S(1)}, f32[8,256,256]{2,1,0:T(8,128)}, ...), condition=%wide.region_4.5_spmd, body=%wide.region_3.4_spmd.sunk | while | flops 262152 | bytes 3670221 | solution.py:92
  356.3 6.6 dynamic_update_slice.17
  369.8 6.5 dynamic_update_slice.17
  383.3 6.3 dynamic_update_slice.17
  396.5 6.6 dynamic_update_slice.17
  410.0 6.3 dynamic_update_slice.17
  423.2 6.2 dynamic_update_slice.17
  436.4 6.4 dynamic_update_slice.17
  449.7 6.0 dynamic_update_slice.17
  460.7 6.2 convolution_subtract_fusion
  471.3 10.9 %fusion.55 = (f32[256,256]{1,0:T(8,128)S(1)}, f32[256,256]{1,0:T(8,128)}, f32[256,256]{1,0:T(8,128)}, f32[8,256,256]{2,1,0:T(8,128)}, f32[8,256,256]{2,1,0:T(8,128)}) fusion(f32[8,256,256]{2,1,0:T(8,128)S(1)} %fusion.93, f32[8,2,256,256]{3,2,0,1:T(8,128)S(1)} %copy-done.5, f32[256,256]{1,0:T(8,128)S(1)} %copy-done.19, ...), kind=kOutput, calls=%fused_computation.83 | convolution fusion | flops 1621884928 | bytes 15990784 | tf_op jit(solution)/shard_map/nak,kb->nab/dot_general | solution.py:50
  483.8 106.3 %while.44 = (s32[]{:T(128)}, f32[2,512,512]{2,1,0:T(8,128)}, s32[8,2]{0,1:T(2,128)S(1)}, f32[8,256,256]{2,1,0:T(8,128)}, f32[8,256,256]{2,1,0:T(8,128)}, /*index=5*/s32[]{:T(128)}, s32[]{:T(128)}, s32[]{:T(128)}) while((s32[]{:T(128)}, f32[2,512,512]{2,1,0:T(8,128)}, s32[8,2]{0,1:T(2,128)S(1)}, f32[8,256,256]{2,1,0:T(8,128)}, ...), condition=%wide.region_1.2_spmd, body=%wide.region_0.1_spmd.sunk | while | flops 262152 | bytes 3670221 | solution.py:92
  490.8 6.6 dynamic_update_slice.16
  504.2 6.5 dynamic_update_slice.16
  517.7 6.3 dynamic_update_slice.16
  530.9 6.6 dynamic_update_slice.16
  544.4 6.3 dynamic_update_slice.16
  557.6 6.2 dynamic_update_slice.16
  570.7 6.4 dynamic_update_slice.16
  584.1 6.0 dynamic_update_slice.16
  601.3 6.2 collective-permute-start.23
  636.9 6.3 collective-permute-done.9
  696.9 67.9 %all-reduce.3.cloned.1.call-done = (f32[2,256,256]{2,1,0:T(8,128)}, f32[256,256]{1,0:T(8,128)}) async-done(((f32[2,256,256]{2,1,0:T(8,128)}, f32[256,256]{1,0:T(8,128)}), (f32[2,256,256]{2,1,0:T(8,128)}, f32[256,256]{1,0:T(8,128)})) %all-reduce.3.cloned.1.call-update) | async-done | bytes 786448 | tf_op jit(solution)/shard_map/psum | solution.py:161
  (323 shorter events, 451.6 us)
Async XLA Ops:
  7.2 757.6 %all-reduce.3.cloned.1.call-start = ((), (), s32[]{:S(2)}) async-start(), calls=%async_computation | async-start | bytes 1572864 | tf_op jit(solution)/shard_map/psum | solution.py:161
  9.3 25.0 %collective-permute-start.4 = (f32[2,128,256]{2,1,0:T(8,128)}, f32[2,128,256]{2,1,0:T(8,128)}, u32[]{:S(2)}, u32[]{:S(2)}) collective-permute-start(f32[2,128,256]{2,1,0:T(8,128)} %get-tuple-element.492), channel_id=1, source_target_pairs={{0,16},{16,32},{32,48},{48,64},{64,80},{80,96},{96,112},{1,17},{17... | collective-permute-start | bytes 786440 | tf_op jit(solution)/shard_map/ppermute | solution.py:18
  12.5 23.9 %collective-permute-start.5 = (f32[2,128,256]{2,1,0:T(8,128)}, f32[2,128,256]{2,1,0:T(8,128)}, u32[]{:S(2)}, u32[]{:S(2)}) collective-permute-start(f32[2,128,256]{2,1,0:T(8,128)} %get-tuple-element.491), channel_id=1, source_target_pairs={{16,0},{32,16},{48,32},{64,48},{80,64},{96,80},{112,96},{17,1},{33... | collective-permute-start | bytes 786440 | tf_op jit(solution)/shard_map/ppermute | solution.py:19
  20.1 24.8 %collective-permute-start = (f32[2,128,256]{2,1,0:T(8,128)}, f32[2,128,256]{2,1,0:T(8,128)}, u32[]{:S(2)}, u32[]{:S(2)}) collective-permute-start(f32[2,128,256]{2,1,0:T(8,128)} %get-tuple-element.490), channel_id=1, source_target_pairs={{0,16},{16,32},{32,48},{48,64},{64,80},{80,96},{96,112},{1,17},{17... | collective-permute-start | bytes 786440 | tf_op jit(solution)/shard_map/ppermute | solution.py:18
  22.0 23.9 %collective-permute-start.1 = (f32[2,128,256]{2,1,0:T(8,128)}, f32[2,128,256]{2,1,0:T(8,128)}, u32[]{:S(2)}, u32[]{:S(2)}) collective-permute-start(f32[2,128,256]{2,1,0:T(8,128)} %get-tuple-element.489), channel_id=1, source_target_pairs={{16,0},{32,16},{48,32},{64,48},{80,64},{96,80},{112,96},{17,1},{33... | collective-permute-start | bytes 786440 | tf_op jit(solution)/shard_map/ppermute | solution.py:19
  37.4 17.1 %collective-permute-start.6 = (f32[2,512,128]{2,1,0:T(8,128)S(1)}, f32[2,512,128]{2,1,0:T(8,128)S(1)}, u32[]{:S(2)}, u32[]{:S(2)}) collective-permute-start(f32[2,512,128]{2,1,0:T(8,128)S(1)} %get-tuple-element.484), channel_id=1, source_target_pairs={{0,1},{1,2},{2,3},{3,4},{4,5},{5,6},{6,7},{7,8},{8,9},{9,10},{10,1... | collective-permute-start | bytes 1572872 | tf_op jit(solution)/shard_map/ppermute | solution.py:18
  42.9 15.4 %collective-permute-start.7 = (f32[2,512,128]{2,1,0:T(8,128)S(1)}, f32[2,512,128]{2,1,0:T(8,128)S(1)}, u32[]{:S(2)}, u32[]{:S(2)}) collective-permute-start(f32[2,512,128]{2,1,0:T(8,128)S(1)} %get-tuple-element.485), channel_id=1, source_target_pairs={{1,0},{2,1},{3,2},{4,3},{5,4},{6,5},{7,6},{8,7},{9,8},{10,9},{11,1... | collective-permute-start | bytes 1572872 | tf_op jit(solution)/shard_map/ppermute | solution.py:19
  48.0 108.6 %collective-permute-start.2 = (f32[2,512,128]{2,1,0:T(8,128)}, f32[2,512,128]{2,1,0:T(8,128)}, u32[]{:S(2)}, u32[]{:S(2)}) collective-permute-start(f32[2,512,128]{2,1,0:T(8,128)} %get-tuple-element.482), channel_id=1, source_target_pairs={{0,1},{1,2},{2,3},{3,4},{4,5},{5,6},{6,7},{7,8},{8,9},{9,10},{10,1... | collective-permute-start | bytes 1572872 | tf_op jit(solution)/shard_map/ppermute | solution.py:18
  52.6 104.1 %collective-permute-start.3 = (f32[2,512,128]{2,1,0:T(8,128)}, f32[2,512,128]{2,1,0:T(8,128)}, u32[]{:S(2)}, u32[]{:S(2)}) collective-permute-start(f32[2,512,128]{2,1,0:T(8,128)} %get-tuple-element.483), channel_id=1, source_target_pairs={{1,0},{2,1},{3,2},{4,3},{5,4},{6,5},{7,6},{8,7},{9,8},{10,9},{11,1... | collective-permute-start | bytes 1572872 | tf_op jit(solution)/shard_map/ppermute | solution.py:19
  594.1 21.0 %collective-permute-start.20 = (f32[2,128,256]{2,1,0:T(8,128)}, f32[2,128,256]{2,1,0:T(8,128)}, u32[]{:S(2)}, u32[]{:S(2)}) collective-permute-start(f32[2,128,256]{2,1,0:T(8,128)} %get-tuple-element.473), channel_id=1, source_target_pairs={{16,0},{32,16},{48,32},{64,48},{80,64},{96,80},{112,96},{17,1},{33... | collective-permute-start | bytes 786440 | tf_op jit(solution)/shard_map/ppermute | solution.py:27
  597.2 20.9 %collective-permute-start.21 = (f32[2,128,256]{2,1,0:T(8,128)}, f32[2,128,256]{2,1,0:T(8,128)}, u32[]{:S(2)}, u32[]{:S(2)}) collective-permute-start(f32[2,128,256]{2,1,0:T(8,128)} %get-tuple-element.472), channel_id=1, source_target_pairs={{0,16},{16,32},{32,48},{48,64},{64,80},{80,96},{96,112},{1,17},{17... | collective-permute-start | bytes 786440 | tf_op jit(solution)/shard_map/ppermute | solution.py:27
  599.3 23.1 %collective-permute-start.22 = (f32[2,256,128]{2,1,0:T(8,128)}, f32[2,256,128]{2,1,0:T(8,128)}, u32[]{:S(2)}, u32[]{:S(2)}) collective-permute-start(f32[2,256,128]{2,1,0:T(8,128)} %get-tuple-element.471), channel_id=1, source_target_pairs={{1,0},{2,1},{3,2},{4,3},{5,4},{6,5},{7,6},{8,7},{9,8},{10,9},{11,1... | collective-permute-start | bytes 786440 | tf_op jit(solution)/shard_map/ppermute | solution.py:27
  601.3 27.8 %collective-permute-start.23 = (f32[2,256,128]{2,1,0:T(8,128)}, f32[2,256,128]{2,1,0:T(8,128)}, u32[]{:S(2)}, u32[]{:S(2)}) collective-permute-start(f32[2,256,128]{2,1,0:T(8,128)} %get-tuple-element.470), channel_id=1, source_target_pairs={{0,1},{1,2},{2,3},{3,4},{4,5},{5,6},{6,7},{7,8},{8,9},{9,10},{10,1... | collective-permute-start | bytes 786440 | tf_op jit(solution)/shard_map/ppermute | solution.py:27
  607.5 27.4 %collective-permute-start.24 = (f32[2,128,128]{2,1,0:T(8,128)}, f32[2,128,128]{2,1,0:T(8,128)}, u32[]{:S(2)}, u32[]{:S(2)}) collective-permute-start(f32[2,128,128]{2,1,0:T(8,128)} %get-tuple-element.469), channel_id=1, source_target_pairs={{16,0},{32,16},{48,32},{64,48},{80,64},{96,80},{112,96},{17,1},{33... | collective-permute-start | bytes 393224 | tf_op jit(solution)/shard_map/ppermute | solution.py:27
  615.1 30.1 %collective-permute-start.26 = (f32[2,128,128]{2,1,0:T(8,128)}, f32[2,128,128]{2,1,0:T(8,128)S(1)}, u32[]{:S(2)}, u32[]{:S(2)}) collective-permute-start(f32[2,128,128]{2,1,0:T(8,128)} %get-tuple-element.468), channel_id=1, source_target_pairs={{16,0},{32,16},{48,32},{64,48},{80,64},{96,80},{112,96},{17,1},{33... | collective-permute-start | bytes 393224 | tf_op jit(solution)/shard_map/ppermute | solution.py:27
  618.1 34.4 %collective-permute-start.28 = (f32[2,128,128]{2,1,0:T(8,128)}, f32[2,128,128]{2,1,0:T(8,128)S(1)}, u32[]{:S(2)}, u32[]{:S(2)}) collective-permute-start(f32[2,128,128]{2,1,0:T(8,128)} %get-tuple-element.467), channel_id=1, source_target_pairs={{0,16},{16,32},{32,48},{48,64},{64,80},{80,96},{96,112},{1,17},{17... | collective-permute-start | bytes 393224 | tf_op jit(solution)/shard_map/ppermute | solution.py:27
  622.5 10.5 %collective-permute-start.8 = (f32[2,128,256]{2,1,0:T(8,128)}, f32[2,128,256]{2,1,0:T(8,128)S(1)}, u32[]{:S(2)}, u32[]{:S(2)}) collective-permute-start(f32[2,128,256]{2,1,0:T(8,128)} %get-tuple-element.481), channel_id=1, source_target_pairs={{16,0},{32,16},{48,32},{64,48},{80,64},{96,80},{112,96},{17,1},{33... | collective-permute-start | bytes 786440 | tf_op jit(solution)/shard_map/ppermute | solution.py:27
  629.0 14.1 %collective-permute-start.9 = (f32[2,128,256]{2,1,0:T(8,128)}, f32[2,128,256]{2,1,0:T(8,128)S(1)}, u32[]{:S(2)}, u32[]{:S(2)}) collective-permute-start(f32[2,128,256]{2,1,0:T(8,128)} %get-tuple-element.480), channel_id=1, source_target_pairs={{0,16},{16,32},{32,48},{48,64},{64,80},{80,96},{96,112},{1,17},{17... | collective-permute-start | bytes 786440 | tf_op jit(solution)/shard_map/ppermute | solution.py:27
  633.0 38.4 %collective-permute-start.30 = (f32[2,128,128]{2,1,0:T(8,128)S(1)}, f32[2,128,128]{2,1,0:T(8,128)}, u32[]{:S(2)}, u32[]{:S(2)}) collective-permute-start(f32[2,128,128]{2,1,0:T(8,128)S(1)} %get-tuple-element.466), channel_id=1, source_target_pairs={{0,16},{16,32},{32,48},{48,64},{64,80},{80,96},{96,112},{1,17},{17... | collective-permute-start | bytes 393224 | tf_op jit(solution)/shard_map/ppermute | solution.py:27
  634.9 38.4 %collective-permute-start.10 = (f32[2,256,128]{2,1,0:T(8,128)}, f32[2,256,128]{2,1,0:T(8,128)S(1)}, u32[]{:S(2)}, u32[]{:S(2)}) collective-permute-start(f32[2,256,128]{2,1,0:T(8,128)} %get-tuple-element.479), channel_id=1, source_target_pairs={{1,0},{2,1},{3,2},{4,3},{5,4},{6,5},{7,6},{8,7},{9,8},{10,9},{11,1... | collective-permute-start | bytes 786440 | tf_op jit(solution)/shard_map/ppermute | solution.py:27
  643.2 7.4 collective-permute-start.25
  645.2 41.3 %collective-permute-start.11 = (f32[2,256,128]{2,1,0:T(8,128)}, f32[2,256,128]{2,1,0:T(8,128)S(1)}, u32[]{:S(2)}, u32[]{:S(2)}) collective-permute-start(f32[2,256,128]{2,1,0:T(8,128)} %get-tuple-element.478), channel_id=1, source_target_pairs={{0,1},{1,2},{2,3},{3,4},{4,5},{5,6},{6,7},{7,8},{8,9},{9,10},{10,1... | collective-permute-start | bytes 786440 | tf_op jit(solution)/shard_map/ppermute | solution.py:27
  652.5 22.8 %collective-permute-start.12 = (f32[2,128,128]{2,1,0:T(8,128)}, f32[2,128,128]{2,1,0:T(8,128)}, u32[]{:S(2)}, u32[]{:S(2)}) collective-permute-start(f32[2,128,128]{2,1,0:T(8,128)} %get-tuple-element.477), channel_id=1, source_target_pairs={{16,0},{32,16},{48,32},{64,48},{80,64},{96,80},{112,96},{17,1},{33... | collective-permute-start | bytes 393224 | tf_op jit(solution)/shard_map/ppermute | solution.py:27
  655.8 7.5 collective-permute-start.29
  663.3 14.2 %collective-permute-start.14 = (f32[2,128,128]{2,1,0:T(8,128)}, f32[2,128,128]{2,1,0:T(8,128)}, u32[]{:S(2)}, u32[]{:S(2)}) collective-permute-start(f32[2,128,128]{2,1,0:T(8,128)} %get-tuple-element.476), channel_id=1, source_target_pairs={{16,0},{32,16},{48,32},{64,48},{80,64},{96,80},{112,96},{17,1},{33... | collective-permute-start | bytes 393224 | tf_op jit(solution)/shard_map/ppermute | solution.py:27
  671.4 10.7 %collective-permute-start.16 = (f32[2,128,128]{2,1,0:T(8,128)}, f32[2,128,128]{2,1,0:T(8,128)S(1)}, u32[]{:S(2)}, u32[]{:S(2)}) collective-permute-start(f32[2,128,128]{2,1,0:T(8,128)} %get-tuple-element.475), channel_id=1, source_target_pairs={{0,16},{16,32},{32,48},{48,64},{64,80},{80,96},{96,112},{1,17},{17... | collective-permute-start | bytes 393224 | tf_op jit(solution)/shard_map/ppermute | solution.py:27
  673.3 10.7 %collective-permute-start.18 = (f32[2,128,128]{2,1,0:T(8,128)}, f32[2,128,128]{2,1,0:T(8,128)}, u32[]{:S(2)}, u32[]{:S(2)}) collective-permute-start(f32[2,128,128]{2,1,0:T(8,128)} %get-tuple-element.474), channel_id=1, source_target_pairs={{0,16},{16,32},{32,48},{48,64},{64,80},{80,96},{96,112},{1,17},{17... | collective-permute-start | bytes 393224 | tf_op jit(solution)/shard_map/ppermute | solution.py:27
  675.3 20.4 %collective-permute-start.31 = (f32[2,128,128]{2,1,0:T(8,128)}, f32[2,128,128]{2,1,0:T(8,128)S(1)}, u32[]{:S(2)}, u32[]{:S(2)}) collective-permute-start(f32[2,128,128]{2,1,0:T(8,128)} %collective-permute-done.30), channel_id=1, source_target_pairs={{0,1},{1,2},{2,3},{3,4},{4,5},{5,6},{6,7},{7,8},{8,9},{9,10},{10,1... | collective-permute-start | bytes 393224 | tf_op jit(solution)/shard_map/ppermute | solution.py:27
  677.5 13.1 %collective-permute-start.13 = (f32[2,128,128]{2,1,0:T(8,128)}, f32[2,128,128]{2,1,0:T(8,128)S(1)}, u32[]{:S(2)}, u32[]{:S(2)}) collective-permute-start(f32[2,128,128]{2,1,0:T(8,128)} %collective-permute-done.12), channel_id=1, source_target_pairs={{1,0},{2,1},{3,2},{4,3},{5,4},{6,5},{7,6},{8,7},{9,8},{10,9},{11,1... | collective-permute-start | bytes 393224 | tf_op jit(solution)/shard_map/ppermute | solution.py:27
  682.1 8.5 %collective-permute-start.15 = (f32[2,128,128]{2,1,0:T(8,128)}, f32[2,128,128]{2,1,0:T(8,128)S(1)}, u32[]{:S(2)}, u32[]{:S(2)}) collective-permute-start(f32[2,128,128]{2,1,0:T(8,128)} %collective-permute-done.14), channel_id=1, source_target_pairs={{0,1},{1,2},{2,3},{3,4},{4,5},{5,6},{6,7},{7,8},{8,9},{9,10},{10,1... | collective-permute-start | bytes 393224 | tf_op jit(solution)/shard_map/ppermute | solution.py:27
  684.0 7.2 collective-permute-start.17
  686.4 9.3 %collective-permute-start.19 = (f32[2,128,128]{2,1,0:T(8,128)}, f32[2,128,128]{2,1,0:T(8,128)}, u32[]{:S(2)}, u32[]{:S(2)}) collective-permute-start(f32[2,128,128]{2,1,0:T(8,128)} %collective-permute-done.18), channel_id=1, source_target_pairs={{0,1},{1,2},{2,3},{3,4},{4,5},{5,6},{6,7},{7,8},{8,9},{9,10},{10,1... | collective-permute-start | bytes 393224 | tf_op jit(solution)/shard_map/ppermute | solution.py:27
  (26 other events, 494.8 us)
Sparse Core Ops, SparseCore 0:
  615.2 149.5 all-reduce.2
where the time goes:
time: 787 us; the launch traced here: 775 us
  matrix products  246 us (31%)
  local copies, waits for them, and re-layouts  221 us (28%)
  starting transfers between devices  102 us (13%)
  waiting for transfers between devices  87.6 us (11%)
  loops' own time  62.7 us (8%)
  other arithmetic  40.8 us (5%)
  between operations  15.6 us (2%)
    dot_general x24, matrix products, right_product(): jnp.einsum('nak,kb->nab', field, table, precision=lax.Precision.HIGHEST)  127 us
    dot_general x24, matrix products, left_product(): jnp.einsum('aj,njk->nak', table, field, precision=lax.Precision.HIGHEST)  119 us
    dynamic_update_slice x16, local copies, waits for them, and re-layouts, add_piece(): return lax.dynamic_update_slice(accumulated, current + addend, place)  102 us
    ppermute x24, starting transfers between devices, passed_along(): return lax.ppermute(block, axis, route)  70.2 us
    psum x1, waiting for transfers between devices, body(): lax.psum((numerator, illumination), ('row', 'col'))  67.9 us
    another operation x2, loops' own time, spread(): return lax.fori_loop(0, term_re.shape[0], add_piece, initial)  62.5 us
    gather x48, local copies, waits for them, and re-layouts  56.9 us
    add x16, other arithmetic, add_piece(): return lax.dynamic_update_slice(accumulated, current + addend, place)  21.9 us
  transfers between devices with their start and end apart: 33, of which 8 were waited for; matrix products, arithmetic and copies ran while one was open for 16% of the time, Pallas kernels for 0%

commit v1 on v0

v1 whole, which is shorter than its diff:
```python
import jax
import jax.numpy as jnp
import ml_dtypes
import numpy as np
from jax import lax
from jax.experimental import pallas as pl
from jax.experimental.pallas import tpu as pltpu
from jax.sharding import PartitionSpec as P

phase_rate = 0.002
win = 256
half = 128
positions = 8
rows_at_once = 16
f32 = jnp.float32
bf16 = jnp.bfloat16


def real_form(table):
    return np.block([[table.real, table.imag], [-table.imag, table.real]])


def split_table(table):
    high = table.astype(np.float32).astype(ml_dtypes.bfloat16)
    low = (table - high.astype(np.float64)).astype(ml_dtypes.bfloat16)
    return high, low


def factor_tables():
    counter = np.arange(win)
    frequency = np.where(counter < half, counter, counter - win)
    kernel = np.exp(-1j * phase_rate * frequency.astype(np.float64) ** 2)
    response = np.fft.ifft(kernel)
    circulant = response[(counter[:, None] - counter[None, :]) % win]
    first, second = circulant[:half, :half], circulant[:half, half:]
    n, k = np.arange(half)[:, None], np.arange(half)[None, :]
    even = np.exp(-2j * np.pi * ((2 * n * k) % win) / win) / 16.0
    odd = np.exp(-2j * np.pi * ((n * (2 * k + 1)) % win) / win) / 16.0
    return [real_form(t) for t in (0.5 * (first + second), 0.5 * (first - second), even, odd)]


def stacked_tables():
    factors = factor_tables()
    every = factors + [t.T for t in factors]
    right, left = [], []
    for table in every:
        high, low = split_table(table)
        right.append(np.concatenate([high, high, low], axis=0))
        left.append(np.concatenate([high, high, low], axis=1))
    return np.stack(left), np.stack(right)


def column_order():
    order = np.concatenate([np.arange(0, win, 2), np.arange(1, win, 2)])
    table = np.zeros((win, win), np.float32)
    table[order, np.arange(win)] = 1.0
    return np.stack([table, table.T]).astype(ml_dtypes.bfloat16)


def split3(value):
    high = value.astype(bf16)
    rest = value - high.astype(f32)
    middle = rest.astype(bf16)
    low = (rest - middle.astype(f32)).astype(bf16)
    return high, middle, low


def prepare_body(pattern_ref, starts_ref, measured_ref, probe_ref, order_ref, sorted_ref, rolled_ref):
    position = pl.program_id(0)
    by_column = sum(jnp.dot(part, order_ref[0], preferred_element_type=f32) for part in split3(measured_ref[0]))
    sorted_ref[0] = sum(jnp.dot(order_ref[1], part, preferred_element_type=f32) for part in split3(by_column))
    down = lax.rem(starts_ref[position, 0], 8)
    across = starts_ref[position, 1]
    for plane in range(2):
        rolled_ref[0, plane] = pltpu.roll(pltpu.roll(probe_ref[plane], down, axis=0), across, axis=1)


def prepare(pattern, starts, measured, probe):
    order = jnp.asarray(column_order())
    return pl.pallas_call(
        prepare_body,
        out_shape=(
            jax.ShapeDtypeStruct((positions, win, win), f32),
            jax.ShapeDtypeStruct((positions, 2, win, win), f32),
        ),
        grid_spec=pltpu.PrefetchScalarGridSpec(
            num_scalar_prefetch=2,
            grid=(positions,),
            in_specs=[
                pl.BlockSpec((1, win, win), lambda j, pattern, starts: (pattern[j], 0, 0)),
                pl.BlockSpec((2, win, win), lambda j, pattern, starts: (0, 0, 0)),
                pl.BlockSpec((2, win, win), lambda j, pattern, starts: (0, 0, 0)),
            ],
            out_specs=[
                pl.BlockSpec((1, win, win), lambda j, pattern, starts: (j, 0, 0)),
                pl.BlockSpec((1, 2, win, win), lambda j, pattern, starts: (j, 0, 0, 0)),
            ],
        ),
        cost_estimate=pl.CostEstimate(flops=2 * 6 * positions * win**3, bytes_accessed=8 << 20, transcendentals=0),
        name="prepare",
    )(pattern, starts, measured, probe, order)


def complex_mul(left_re, left_im, right_re, right_im):
    return (left_re * right_re - left_im * right_im, left_re * right_im + left_im * right_re)


def conj_mul(left_re, left_im, right_re, right_im):
    return (left_re * right_re + left_im * right_im, left_re * right_im - left_im * right_re)


def put_left(ref, side, row, value):
    high = value.astype(bf16)
    low = (value - high.astype(f32)).astype(bf16)
    size = value.shape[0]
    ref[side, row : row + size, :] = high
    ref[side, win + row : win + row + size, :] = low
    ref[side, 2 * win + row : 2 * win + row + size, :] = high


def put_right(ref, side, row, lane, value):
    high = value.astype(bf16)
    low = (value - high.astype(f32)).astype(bf16)
    size = value.shape[0]
    ref[side, row : row + size, lane : lane + half] = high
    ref[side, row : row + size, win + lane : win + lane + half] = low
    ref[side, row : row + size, 2 * win + lane : 2 * win + lane + half] = high


def core_body(
    starts_ref,
    own_ref, left_ref, right_ref, top_ref, bottom_ref,
    rolled_ref, sorted_ref, ltab_ref, rtab_ref,
    out_top, out_mid, out_bottom, share_ref,
    wide, total, xa, xb, res, phi, shares,
):
    step = pl.program_id(0)
    R = rows_at_once

    @pl.when(step == 0)
    def _():
        wide[:, 0:half, :] = top_ref[...]
        wide[:, half + win : 2 * win, :] = bottom_ref[...]
        wide[:, half : half + win, 0:half] = left_ref[...]
        wide[:, half : half + win, half : half + win] = own_ref[...]
        wide[:, half : half + win, half + win :] = right_ref[...]
        total[...] = jnp.zeros_like(total)
        share_ref[...] = jnp.zeros_like(share_ref)

    a = starts_ref[step, 0]
    b = starts_ref[step, 1]
    offset = lax.rem(a, 8)
    base = pl.multiple_of(a - offset, 8)
    lanes = lax.broadcasted_iota(jnp.int32, (R, win), 1)
    near = lanes >= b
    below = lax.broadcasted_iota(jnp.int32, (R, win), 0) >= offset

    def row_sets(row):
        first = (pl.ds(base + row, R), None)
        return (first,) if row else (first, (pl.ds(base + win, R), below))

    def window(plane, row):
        value = None
        for rows, mask in row_sets(row):
            block = jnp.where(near, wide[plane, rows, 0:win], wide[plane, rows, win : 2 * win])
            value = block if mask is None else jnp.where(mask, value, block)
        return value

    def add_window(plane, row, value):
        zero = jnp.zeros_like(value)
        for rows, mask in row_sets(row):
            part = value
            if row == 0:
                part = jnp.where(below, value, zero) if mask is None else jnp.where(below, zero, value)
            total[plane, rows, 0:win] += jnp.where(near, part, zero)
            total[plane, rows, win : 2 * win] += jnp.where(near, zero, part)

    def left_stage(first):
        for side in range(2):
            res[side] = jnp.dot(ltab_ref[first + side], xa[side], preferred_element_type=f32)

    def right_stage(first):
        for side in range(2):
            res[side] = jnp.dot(xb[side], rtab_ref[first + side], preferred_element_type=f32)

    def row_butterfly(row, upper, lower):
        for part in range(2):
            put_left(xa, 0, part * half + row, upper[part] + lower[part])
            put_left(xa, 1, part * half + row, upper[part] - lower[part])

    def lane_butterfly(row, field):
        for part in range(2):
            near_half, far_half = field[part][:, :half], field[part][:, half:]
            put_right(xb, 0, row, part * half, near_half + far_half)
            put_right(xb, 1, row, part * half, near_half - far_half)

    def lane_join(row):
        out = []
        for part in range(2):
            plus = res[0, row : row + R, part * half : (part + 1) * half]
            minus = res[1, row : row + R, part * half : (part + 1) * half]
            out.append(jnp.concatenate([plus + minus, plus - minus], axis=1))
        return out

    def row_join(row):
        plus = [res[0, part * half + row : part * half + row + R, :] for part in range(2)]
        minus = [res[1, part * half + row : part * half + row + R, :] for part in range(2)]
        return [p + m for p, m in zip(plus, minus)], [p - m for p, m in zip(plus, minus)]

    def circulant(first_left, first_right):
        left_stage(first_left)
        for row in range(0, half, R):
            upper, lower = row_join(row)
            lane_butterfly(row, upper)
            lane_butterfly(half + row, lower)
        right_stage(first_right)

    def add_share(plane, value):
        value = pltpu.roll(value, jnp.where(offset == 0, 0, win - offset), axis=0)
        share_ref[plane] += pltpu.roll(value, jnp.where(b == 0, 0, win - b), axis=1)

    for row in range(0, half, R):
        pair = []
        for at in (row, half + row):
            o_re, o_im = window(0, at), window(1, at)
            shares[0, at : at + R, :] = o_re * o_re + o_im * o_im
            pair.append(complex_mul(rolled_ref[0, 0, at : at + R, :], rolled_ref[0, 1, at : at + R, :], o_re, o_im))
        row_butterfly(row, *pair)
    add_share(2, shares[0])
    circulant(4, 0)
    for row in range(0, half, R):
        pair = []
        for at in (row, half + row):
            p_re, p_im = lane_join(at)
            phi[0, at : at + R, :] = p_re
            phi[1, at : at + R, :] = p_im
            pair.append(complex_mul(p_re, p_im, window(2, at), window(3, at)))
        row_butterfly(row, *pair)
    left_stage(6)
    for side in range(2):
        for row in range(0, half, R):
            lane_butterfly(side * half + row, [res[side, part * half + row : part * half + row + R, :] for part in range(2)])
    right_stage(2)
    for side in range(2):
        for row in range(0, win, R):
            far_re = res[side, row : row + R, 0:half]
            far_im = res[side, row : row + R, half:win]
            amplitude = sorted_ref[0, row : row + R, side * half : (side + 1) * half]
            factor = 1.0 - amplitude * lax.rsqrt(far_re * far_re + far_im * far_im + 1.0)
            put_right(xb, side, row, 0, factor * far_re)
            put_right(xb, side, row, half, factor * far_im)
    right_stage(6)
    for side in range(2):
        for row in range(0, half, R):
            field = lane_join(side * half + row)
            for part in range(2):
                put_left(xa, side, part * half + row, field[part])
    left_stage(2)
    for row in range(0, half, R):
        pair = []
        for at, (g_re, g_im) in zip((row, half + row), row_join(row)):
            t_re, t_im = conj_mul(phi[0, at : at + R, :], phi[1, at : at + R, :], g_re, g_im)
            add_window(2, at, t_re)
            add_window(3, at, t_im)
            pair.append(conj_mul(window(2, at), window(3, at), g_re, g_im))
        row_butterfly(row, *pair)
    circulant(0, 4)
    for at in range(0, win, R):
        g_re, g_im = lane_join(at)
        t_re, t_im = conj_mul(rolled_ref[0, 0, at : at + R, :], rolled_ref[0, 1, at : at + R, :], g_re, g_im)
        add_window(0, at, t_re)
        add_window(1, at, t_im)
        s_re, s_im = conj_mul(window(0, at), window(1, at), g_re, g_im)
        shares[0, at : at + R, :] = s_re
        shares[1, at : at + R, :] = s_im
    add_share(0, shares[0])
    add_share(1, shares[1])

    @pl.when(step == positions - 1)
    def _():
        out_top[...] = total[:, 0:half, :]
        out_mid[...] = total[:, half : half + win, :]
        out_bottom[...] = total[:, half + win : 2 * win, :]


def core(starts, own, left, right, top, bottom, rolled, ordered):
    ltab, rtab = (jnp.asarray(t) for t in stacked_tables())
    whole = lambda *shape: pl.BlockSpec(shape, lambda j, starts: (0,) * len(shape))
    return pl.pallas_call(
        core_body,
        out_shape=(
            jax.ShapeDtypeStruct((4, half, 2 * win), f32),
            jax.ShapeDtypeStruct((4, win, 2 * win), f32),
            jax.ShapeDtypeStruct((4, half, 2 * win), f32),
            jax.ShapeDtypeStruct((3, win, win), f32),
        ),
        grid_spec=pltpu.PrefetchScalarGridSpec(
            num_scalar_prefetch=1,
            grid=(positions,),
            in_specs=[
                whole(4, win, win), whole(4, win, half), whole(4, win, half),
                whole(4, half, 2 * win), whole(4, half, 2 * win),
                pl.BlockSpec((1, 2, win, win), lambda j, starts: (j, 0, 0, 0)),
                pl.BlockSpec((1, win, win), lambda j, starts: (j, 0, 0)),
                whole(8, win, 3 * win), whole(8, 3 * win, win),
            ],
            out_specs=[
                whole(4, half, 2 * win), whole(4, win, 2 * win), whole(4, half, 2 * win), whole(3, win, win),
            ],
            scratch_shapes=[
                pltpu.VMEM((4, 2 * win + 8, 2 * win), f32),
                pltpu.VMEM((4, 2 * win + 8, 2 * win), f32),
                pltpu.VMEM((2, 3 * win, win), bf16),
                pltpu.VMEM((2, win, 3 * win), bf16),
                pltpu.VMEM((2, win, win), f32),
                pltpu.VMEM((2, win, win), f32),
                pltpu.VMEM((2, win, win), f32),
            ],
        ),
        compiler_params=pltpu.CompilerParams(vmem_limit_bytes=60 << 20),
        cost_estimate=pl.CostEstimate(flops=48 * 2 * positions * win**3, bytes_accessed=32 << 20, transcendentals=0),
        name="core",
    )(starts, own, left, right, top, bottom, rolled, ordered, ltab, rtab)


def shifted(block, axis, distance):
    size = lax.axis_size(axis)
    return lax.ppermute(block, axis, [(i, i + distance) for i in range(size) if 0 <= i + distance < size])


def summed_step(share):
    devices = lax.axis_size("row") * lax.axis_size("col")
    rows = win // devices
    pieces = share.reshape(3, devices, rows * win // half, half).transpose(1, 0, 2, 3)
    pieces = pieces.reshape(devices, 3 * rows * win // half, half)
    pieces = lax.all_to_all(pieces, ("row", "col"), 0, 0, tiled=True)
    piece = jnp.sum(pieces, axis=0).reshape(3, rows * win // half, half)
    step = piece[:2] * lax.rsqrt(piece[2:] + 1.0)
    flat = step.reshape(1, 2 * rows * win // half, half)
    every = lax.all_to_all(jnp.broadcast_to(flat, (devices,) + flat.shape[1:]), ("row", "col"), 0, 0, tiled=True)
    every = every.reshape(devices, 2, rows * win // half, half).transpose(1, 0, 2, 3)
    return every.reshape(2, win, win)


def body(object_one, object_two, probe, scan_pos, pattern_index, measured):
    starts = scan_pos[0, 0]
    own = jnp.concatenate([object_one, object_two], axis=0)
    left = shifted(own[:, :, half:], "col", 1)
    right = shifted(own[:, :, :half], "col", -1)
    below = jnp.concatenate([left[:, half:], own[:, half:], right[:, half:]], axis=2)
    above = jnp.concatenate([left[:, :half], own[:, :half], right[:, :half]], axis=2)
    top = shifted(below, "row", 1)
    bottom = shifted(above, "row", -1)
    ordered, rolled = prepare(pattern_index[0, 0], starts, measured[0, 0], probe)
    out_top, out_mid, out_bottom, share = core(starts, own, left, right, top, bottom, rolled, ordered)
    from_below = shifted(out_top, "row", -1)
    from_above = shifted(out_bottom, "row", 1)
    mid = jnp.concatenate([out_mid[:, :half] + from_above, out_mid[:, half:] + from_below], axis=1)
    from_after = shifted(mid[:, :, :half], "col", -1)
    from_before = shifted(mid[:, :, half + win :], "col", 1)
    grad = jnp.concatenate([mid[:, :, half:win] + from_before, mid[:, :, win : win + half] + from_after], axis=2)
    return (grad[:2], grad[2:], summed_step(share))


def solution(mesh):
    placed = (
        P(None, "row", "col"),
        P(None, "row", "col"),
        P(),
        P("row", "col", None, None),
        P("row", "col", None),
        P("row", "col", None, None, None),
    )
    return jax.shard_map(
        body,
        mesh=mesh,
        in_specs=placed,
        out_specs=(P(None, "row", "col"), P(None, "row", "col"), P()),
        check_vma=False,
    )
```

time: 787 us -> 179 us (0.23); the launches traced: 775 us -> 177 us
  matrix products: 246 us -> 0 us
  local copies, waits for them, and re-layouts: 221 us -> 7.89 us
  starting transfers between devices: 102 us -> 31.2 us
  waiting for transfers between devices: 87.6 us -> 19.8 us
  loops' own time: 62.7 us -> 0 us
  blocking collectives: 0 us -> 62.3 us
  Pallas kernels: 0 us -> 48.9 us
  other arithmetic: 40.8 us -> 5.92 us
  between operations: 15.6 us -> 0.88 us
    dot_general x48 -> x0, matrix products: 246 us -> none  [the longest x24 127 us: right_product(): jnp.einsum('nak,kb->nab', field, table, precision=lax.Precision.HIGHEST)]
    dynamic_update_slice x16 -> x0, local copies, waits for them, and re-layouts: 102 us -> none  [add_piece(): return lax.dynamic_update_slice(accumulated, current + addend, place)]
    ppermute x32 -> x8, starting transfers between devices: 102 us -> 31.2 us  [shifted(): lax.ppermute(block, axis, [(i, i + distance) for i in range(size) if 0 <=...]
    psum x1 -> x0, waiting for transfers between devices: 67.9 us -> none  [body(): lax.psum((numerator, illumination), ('row', 'col'))]
    another operation x4 -> x0, loops' own time: 62.7 us -> none  [the longest x2 62.5 us: spread(): return lax.fori_loop(0, term_re.shape[0], add_piece, initial)]
    all_to_all x0 -> x2, blocking collectives: none -> 62.3 us  [the longest x1 40.5 us: summed_step(): pieces = lax.all_to_all(pieces, ('row', 'col'), 0, 0, tiled=True)]
    gather x49 -> x0, local copies, waits for them, and re-layouts: 58.9 us -> none
    pallas_call x0 -> x2, Pallas kernels: none -> 48.9 us  [the longest x1 39.2 us: core(): pl.pallas_call(core_body, out_shape=(jax.ShapeDtypeStruct((4, half, 2 * w...]
  transfers between devices with their start and end apart: 33 -> 8, of which waited for: 8 -> 4; matrix products, arithmetic and copies ran while one was open for 16% -> 3% of each run, Pallas kernels for 0% -> 6%
where the time goes in v1:
time: 179 us; the launch traced here: 177 us
  blocking collectives  62.3 us (35%)
  Pallas kernels  48.9 us (27%)
  starting transfers between devices  31.2 us (17%)
  waiting for transfers between devices  19.8 us (11%)
  local copies, waits for them, and re-layouts  7.89 us (4%)
  other arithmetic  5.92 us (3%)
    all_to_all x1, blocking collectives, summed_step(): pieces = lax.all_to_all(pieces, ('row', 'col'), 0, 0, tiled=True)  40.5 us
    pallas_call x1, Pallas kernels, core(): pl.pallas_call(core_body, out_shape=(jax.ShapeDtypeStruct((4, half, 2 * w...  39.2 us
    ppermute x8, starting transfers between devices, shifted(): lax.ppermute(block, axis, [(i, i + distance) for i in range(size) if 0 <=...  31.2 us
    all_to_all x1, blocking collectives, summed_step(): lax.all_to_all(jnp.broadcast_to(flat, (devices,) + flat.shape[1:]), ('row...  21.8 us
    ppermute x8, waiting for transfers between devices, shifted(): lax.ppermute(block, axis, [(i, i + distance) for i in range(size) if 0 <=...  19.8 us
    pallas_call x1, Pallas kernels, prepare(): pl.pallas_call(prepare_body, out_shape=(jax.ShapeDtypeStruct((positions,...  9.78 us
  transfers between devices with their start and end apart: 8, of which 4 were waited for; matrix products, arithmetic and copies ran while one was open for 3% of the time, Pallas kernels for 6%

profile of v1, /device:TPU:7, one launch (start us, length us, event | category | flops | bytes accessed | tf_op | source)
XLA Modules:
  0.0 177.0 jit_solution(2076599482702875327)
XLA Ops:
  0.6 1.1 constant_dynamic-update-slice_fusion.1
  1.7 1.1 constant_dynamic-update-slice_fusion.own_ref
  2.9 2.6 %collective-permute-start.1 = (f32[4,256,128]{2,1,0:T(8,128)S(1)}, f32[4,256,128]{2,1,0:T(8,128)S(1)}, u32[]{:S(2)}, u32[]{:S(2)}) collective-permute-start(f32[4,256,128]{2,1,0:T(8,128)S(1)} %get-tuple-element.25), channel_id=1, source_target_pairs={{1,0},{2,1},{3,2},{4,3},{5,4},{6,5},{7,6},{8,7},{9,8},{10,9},{11,1... | collective-permute-start | bytes 1572872 | tf_op jit(solution)/shard_map/ppermute | solution.py:328
  5.5 3.9 %collective-permute-start = (f32[4,256,128]{2,1,0:T(8,128)S(1)}, f32[4,256,128]{2,1,0:T(8,128)S(1)}, u32[]{:S(2)}, u32[]{:S(2)}) collective-permute-start(f32[4,256,128]{2,1,0:T(8,128)S(1)} %get-tuple-element.26), channel_id=1, source_target_pairs={{0,1},{1,2},{2,3},{3,4},{4,5},{5,6},{6,7},{7,8},{8,9},{9,10},{10,1... | collective-permute-start | bytes 1572872 | tf_op jit(solution)/shard_map/ppermute | solution.py:328
  9.4 7.8 %collective-permute-done.1.right_ref = f32[4,256,128]{2,1,0:T(8,128)S(1)} collective-permute-done((f32[4,256,128]{2,1,0:T(8,128)S(1)}, f32[4,256,128]{2,1,0:T(8,128)S(1)}, u32[]{:S(2)}, u32[]{:S(2)}) %collective-permute-start.1) | collective-permute-done | bytes 524320 | tf_op jit(solution)/shard_map/ppermute | solution.py:328
  17.3 0.3 collective-permute-done.left_ref
  17.7 0.1 pad_maximum_fusion
  17.8 0.3 copy-done.2
  18.1 3.2 %collective-permute-start.2 = (f32[4,128,512]{2,1,0:T(8,128)S(1)}, f32[4,128,512]{2,1,0:T(8,128)}, u32[]{:S(2)}, u32[]{:S(2)}) collective-permute-start(f32[4,128,512]{2,1,0:T(8,128)S(1)} %pad_maximum_fusion), channel_id=1, source_target_pairs={{0,16},{16,32},{32,48},{48,64},{64,80},{80,96},{96,112},{1,17},{17... | collective-permute-start | bytes 3145736 | tf_op jit(solution)/shard_map/ppermute | solution.py:328
  21.4 5.7 %collective-permute-start.3 = (f32[4,128,512]{2,1,0:T(8,128)S(1)}, f32[4,128,512]{2,1,0:T(8,128)}, u32[]{:S(2)}, u32[]{:S(2)}) collective-permute-start(f32[4,128,512]{2,1,0:T(8,128)S(1)} %pad_maximum_fusion.1), channel_id=1, source_target_pairs={{16,0},{32,16},{48,32},{64,48},{80,64},{96,80},{112,96},{17,1},{33... | collective-permute-start | bytes 3145736 | tf_op jit(solution)/shard_map/ppermute | solution.py:328
  27.1 0.7 copy.22.starts_ref
  27.8 9.8 %prepare.1 = (f32[8,256,256]{2,1,0:T(8,128)}, f32[8,2,256,256]{3,2,1,0:T(8,128)}) custom-call(s32[8]{0:T(128)} %bitcast.15, s32[8,2]{1,0:T(8,128)} %copy.22.starts_ref, f32[8,256,256]{2,1,0:T(8,128)} %bitcast.14, f32[2,256,256]{2,1,0:T(8,128)} %probe_ref.1, bf16[2,256,256]{2,1,0:T(8,128)(2,1)} %constant.10.clone.order_ref), custom_call_target="tpu_custom_call" | custom-call | flops 1610612736 | bytes 8388608 | tf_op jit(solution)/shard_map/prepare/pallas_call | solution.py:80
  37.5 9.8 %collective-permute-done.2.top_ref = f32[4,128,512]{2,1,0:T(8,128)} collective-permute-done((f32[4,128,512]{2,1,0:T(8,128)S(1)}, f32[4,128,512]{2,1,0:T(8,128)}, u32[]{:S(2)}, u32[]{:S(2)}) %collective-permute-start.2) | collective-permute-done | bytes 1048608 | tf_op jit(solution)/shard_map/ppermute | solution.py:328
  47.4 1.8 collective-permute-done.3.bottom_ref
  49.1 39.2 %core.1 = (f32[4,128,512]{2,1,0:T(8,128)}, f32[4,256,512]{2,1,0:T(8,128)}, f32[4,128,512]{2,1,0:T(8,128)}, f32[3,256,256]{2,1,0:T(8,128)}) custom-call(s32[8,2]{1,0:T(8,128)} %copy.22.starts_ref, f32[4,256,256]{2,1,0:T(8,128)} %copy-done, f32[4,256,128]{2,1,0:T(8,128)} %copy-done.3, f32[4,256,128]{2,1,0:T(8,128)} %copy-done.2, ...), custom_call_target="tpu_custom_call" | custom-call | flops 12884901888 | bytes 33554432 | tf_op jit(solution)/shard_map/core/pallas_call | solution.py:289
  88.3 1.9 %collective-permute-start.4 = (f32[4,128,512]{2,1,0:T(8,128)}, f32[4,128,512]{2,1,0:T(8,128)S(1)}, u32[]{:S(2)}, u32[]{:S(2)}) collective-permute-start(f32[4,128,512]{2,1,0:T(8,128)} %get-tuple-element.12), channel_id=1, source_target_pairs={{0,16},{16,32},{32,48},{48,64},{64,80},{80,96},{96,112},{1,17},{17... | collective-permute-start | bytes 3145736 | tf_op jit(solution)/shard_map/ppermute | solution.py:328
  90.2 7.5 %collective-permute-start.5 = (f32[4,128,512]{2,1,0:T(8,128)}, f32[4,128,512]{2,1,0:T(8,128)S(1)}, u32[]{:S(2)}, u32[]{:S(2)}) collective-permute-start(f32[4,128,512]{2,1,0:T(8,128)} %get-tuple-element.13), channel_id=1, source_target_pairs={{16,0},{32,16},{48,32},{64,48},{80,64},{96,80},{112,96},{17,1},{33... | collective-permute-start | bytes 3145736 | tf_op jit(solution)/shard_map/ppermute | solution.py:328
  97.8 1.5 reshape.32
  99.3 0.5 copy.24
  99.8 40.5 %all_to_all.10 = f32[128,12,128]{2,1,0:T(8,128)S(1)} all-to-all(f32[128,12,128]{2,1,0:T(8,128)S(1)} %copy.24), channel_id=1, replica_groups=mesh['row'=8,'col'=16] {'row','col'}, dimensions={0} | all-to-all | bytes 1572864 | tf_op jit(solution)/shard_map/all_to_all | solution.py:336
  140.3 0.1 reduce_sum.9
  140.5 1.0 copy-done.1
  141.5 2.4 %slice_add_fusion = (f32[4,128,512]{2,1,0:T(8,128)S(1)}, f32[4,128,512]{2,1,0:T(8,128)S(1)}) fusion(f32[4,128,512]{2,1,0:T(8,128)} %copy-done.1, f32[4,256,512]{2,1,0:T(8,128)} %get-tuple-element.11, f32[4,128,512]{2,1,0:T(8,128)S(1)} %collective-permute-done.4), kind=kLoop, calls=%fused_computation.10 | loop fusion | flops 524288 | bytes 6291456 | tf_op jit(solution)/shard_map/add | solution.py:358
  143.9 0.9 pad_maximum_fusion.3
  144.7 2.5 %collective-permute-start.7 = (f32[4,256,128]{2,1,0:T(8,128)}, f32[4,256,128]{2,1,0:T(8,128)}, u32[]{:S(2)}, u32[]{:S(2)}) collective-permute-start(f32[4,256,128]{2,1,0:T(8,128)} %get-tuple-element.17), channel_id=1, source_target_pairs={{1,0},{2,1},{3,2},{4,3},{5,4},{6,5},{7,6},{8,7},{9,8},{10,9},{11,1... | collective-permute-start | bytes 1572872 | tf_op jit(solution)/shard_map/ppermute | solution.py:328
  147.3 3.9 %collective-permute-start.6 = (f32[4,256,128]{2,1,0:T(8,128)S(1)}, f32[4,256,128]{2,1,0:T(8,128)}, u32[]{:S(2)}, u32[]{:S(2)}) collective-permute-start(f32[4,256,128]{2,1,0:T(8,128)S(1)} %get-tuple-element.18), channel_id=1, source_target_pairs={{0,1},{1,2},{2,3},{3,4},{4,5},{5,6},{6,7},{7,8},{8,9},{9,10},{10,1... | collective-permute-start | bytes 1572872 | tf_op jit(solution)/shard_map/ppermute | solution.py:328
  151.3 21.8 %all_to_all.11 = f32[128,8,128]{2,1,0:T(8,128)S(1)} all-to-all(f32[128,8,128]{2,1,0:T(8,128)S(1)} %broadcast_in_dim.2), channel_id=1, replica_groups=mesh['row'=8,'col'=16] {'row','col'}, dimensions={0} | all-to-all | bytes 1048576 | tf_op jit(solution)/shard_map/all_to_all | solution.py:340
  173.1 0.1 copy.25
  173.2 0.3 copy.26
  173.6 1.1 reshape.35
  174.6 1.3 fusion.2
  175.9 1.0 pad_maximum_fusion.2
  (22 shorter events, 0.5 us)
Async XLA Ops:
  2.8 6.6 %copy-start = (f32[4,256,256]{2,1,0:T(8,128)}, f32[4,256,256]{2,1,0:T(8,128)S(1)}, u32[]{:S(2)}) copy-start(f32[4,256,256]{2,1,0:T(8,128)S(1)} %constant_dynamic-update-slice_fusion.own_ref) | copy-start | bytes 3145732
  2.9 14.4 %collective-permute-start.1 = (f32[4,256,128]{2,1,0:T(8,128)S(1)}, f32[4,256,128]{2,1,0:T(8,128)S(1)}, u32[]{:S(2)}, u32[]{:S(2)}) collective-permute-start(f32[4,256,128]{2,1,0:T(8,128)S(1)} %get-tuple-element.25), channel_id=1, source_target_pairs={{1,0},{2,1},{3,2},{4,3},{5,4},{6,5},{7,6},{8,7},{9,8},{10,9},{11,1... | collective-permute-start | bytes 1572872 | tf_op jit(solution)/shard_map/ppermute | solution.py:328
  5.5 12.2 %collective-permute-start = (f32[4,256,128]{2,1,0:T(8,128)S(1)}, f32[4,256,128]{2,1,0:T(8,128)S(1)}, u32[]{:S(2)}, u32[]{:S(2)}) collective-permute-start(f32[4,256,128]{2,1,0:T(8,128)S(1)} %get-tuple-element.26), channel_id=1, source_target_pairs={{0,1},{1,2},{2,3},{3,4},{4,5},{5,6},{6,7},{7,8},{8,9},{9,10},{10,1... | collective-permute-start | bytes 1572872 | tf_op jit(solution)/shard_map/ppermute | solution.py:328
  17.3 0.8 copy-start.2
  17.6 3.7 %copy-start.3 = (f32[4,256,128]{2,1,0:T(8,128)}, f32[4,256,128]{2,1,0:T(8,128)S(1)}, u32[]{:S(2)}) copy-start(f32[4,256,128]{2,1,0:T(8,128)S(1)} %collective-permute-done.left_ref) | copy-start | bytes 1572868
  17.7 9.4 %copy-start.4 = (s32[1,1,8,2]{2,3,1,0:T(2,128)S(1)}, s32[1,1,8,2]{2,3,1,0:T(2,128)}, u32[]{:S(2)}) copy-start(s32[1,1,8,2]{2,3,1,0:T(2,128)} %param.12) | copy-start | bytes 196
  18.1 29.3 %collective-permute-start.2 = (f32[4,128,512]{2,1,0:T(8,128)S(1)}, f32[4,128,512]{2,1,0:T(8,128)}, u32[]{:S(2)}, u32[]{:S(2)}) collective-permute-start(f32[4,128,512]{2,1,0:T(8,128)S(1)} %pad_maximum_fusion), channel_id=1, source_target_pairs={{0,16},{16,32},{32,48},{48,64},{64,80},{80,96},{96,112},{1,17},{17... | collective-permute-start | bytes 3145736 | tf_op jit(solution)/shard_map/ppermute | solution.py:328
  21.4 27.8 %collective-permute-start.3 = (f32[4,128,512]{2,1,0:T(8,128)S(1)}, f32[4,128,512]{2,1,0:T(8,128)}, u32[]{:S(2)}, u32[]{:S(2)}) collective-permute-start(f32[4,128,512]{2,1,0:T(8,128)S(1)} %pad_maximum_fusion.1), channel_id=1, source_target_pairs={{16,0},{32,16},{48,32},{64,48},{80,64},{96,80},{112,96},{17,1},{33... | collective-permute-start | bytes 3145736 | tf_op jit(solution)/shard_map/ppermute | solution.py:328
  88.3 52.2 %collective-permute-start.4 = (f32[4,128,512]{2,1,0:T(8,128)}, f32[4,128,512]{2,1,0:T(8,128)S(1)}, u32[]{:S(2)}, u32[]{:S(2)}) collective-permute-start(f32[4,128,512]{2,1,0:T(8,128)} %get-tuple-element.12), channel_id=1, source_target_pairs={{0,16},{16,32},{32,48},{48,64},{64,80},{80,96},{96,112},{1,17},{17... | collective-permute-start | bytes 3145736 | tf_op jit(solution)/shard_map/ppermute | solution.py:328
  90.2 50.3 %collective-permute-start.5 = (f32[4,128,512]{2,1,0:T(8,128)}, f32[4,128,512]{2,1,0:T(8,128)S(1)}, u32[]{:S(2)}, u32[]{:S(2)}) collective-permute-start(f32[4,128,512]{2,1,0:T(8,128)} %get-tuple-element.13), channel_id=1, source_target_pairs={{16,0},{32,16},{48,32},{64,48},{80,64},{96,80},{112,96},{17,1},{33... | collective-permute-start | bytes 3145736 | tf_op jit(solution)/shard_map/ppermute | solution.py:328
  140.5 1.0 copy-start.1
  144.7 29.9 %collective-permute-start.7 = (f32[4,256,128]{2,1,0:T(8,128)}, f32[4,256,128]{2,1,0:T(8,128)}, u32[]{:S(2)}, u32[]{:S(2)}) collective-permute-start(f32[4,256,128]{2,1,0:T(8,128)} %get-tuple-element.17), channel_id=1, source_target_pairs={{1,0},{2,1},{3,2},{4,3},{5,4},{6,5},{7,6},{8,7},{9,8},{10,9},{11,1... | collective-permute-start | bytes 1572872 | tf_op jit(solution)/shard_map/ppermute | solution.py:328
  147.3 27.3 %collective-permute-start.6 = (f32[4,256,128]{2,1,0:T(8,128)S(1)}, f32[4,256,128]{2,1,0:T(8,128)}, u32[]{:S(2)}, u32[]{:S(2)}) collective-permute-start(f32[4,256,128]{2,1,0:T(8,128)S(1)} %get-tuple-element.18), channel_id=1, source_target_pairs={{0,1},{1,2},{2,3},{3,4},{4,5},{5,6},{6,7},{7,8},{8,9},{9,10},{10,1... | collective-permute-start | bytes 1572872 | tf_op jit(solution)/shard_map/ppermute | solution.py:328

commit v2 on v1

v2 whole, which is shorter than its diff:
```python
import math

import jax
import jax.numpy as jnp
import ml_dtypes
import numpy as np
from jax import lax
from jax.experimental import pallas as pl
from jax.experimental.pallas import tpu as pltpu
from jax.sharding import PartitionSpec as P

phase_rate = 0.002
win = 256
half = 128
positions = 8
rows_at_once = 16
at_once = 2
f32 = jnp.float32
bf16 = jnp.bfloat16


def real_form(table):
    return np.block([[table.real, table.imag], [-table.imag, table.real]])


def split_table(table):
    high = table.astype(np.float32).astype(ml_dtypes.bfloat16)
    low = (table - high.astype(np.float64)).astype(ml_dtypes.bfloat16)
    return high, low


def factor_tables():
    counter = np.arange(win)
    frequency = np.where(counter < half, counter, counter - win)
    kernel = np.exp(-1j * phase_rate * frequency.astype(np.float64) ** 2)
    response = np.fft.ifft(kernel)
    circulant = response[(counter[:, None] - counter[None, :]) % win]
    first, second = circulant[:half, :half], circulant[:half, half:]
    n, k = np.arange(half)[:, None], np.arange(half)[None, :]
    even = np.exp(-2j * np.pi * ((2 * n * k) % win) / win) / 16.0
    odd = np.exp(-2j * np.pi * ((n * (2 * k + 1)) % win) / win) / 16.0
    return [real_form(t) for t in (0.5 * (first + second), 0.5 * (first - second), even, odd)]


def table_parts():
    return np.stack([np.stack(split_table(table)) for table in factor_tables()])


def column_order():
    order = np.concatenate([np.arange(0, win, 2), np.arange(1, win, 2)])
    table = np.zeros((win, win), np.float32)
    table[order, np.arange(win)] = 1.0
    return np.stack([table, table.T]).astype(ml_dtypes.bfloat16)


def split3(value):
    high = value.astype(bf16)
    rest = value - high.astype(f32)
    middle = rest.astype(bf16)
    low = (rest - middle.astype(f32)).astype(bf16)
    return high, middle, low


def prepare_body(
    pattern_ref, starts_ref, measured_ref, probe_ref, order_ref, parts_ref,
    sorted_ref, rolled_ref, left_ref, right_ref,
):
    position = pl.program_id(0)
    by_column = sum(jnp.dot(part, order_ref[0], preferred_element_type=f32) for part in split3(measured_ref[0]))
    sorted_ref[0] = sum(jnp.dot(order_ref[1], part, preferred_element_type=f32) for part in split3(by_column))
    down = lax.rem(starts_ref[position, 0], 8)
    across = starts_ref[position, 1]
    for plane in range(2):
        rolled_ref[0, plane] = pltpu.roll(pltpu.roll(probe_ref[plane], down, axis=0), across, axis=1)
    turned = position >= 4
    for part, spots in ((0, (0, 1)), (1, (2,))):
        table = parts_ref[0, part].astype(f32)
        table = jnp.where(turned, table.T, table).astype(bf16)
        for spot in spots:
            left_ref[0, :, spot * win : (spot + 1) * win] = table
            right_ref[0, spot * win : (spot + 1) * win, :] = table


def prepare(pattern, starts, measured, probe):
    order = jnp.asarray(column_order())
    parts = jnp.asarray(table_parts())
    return pl.pallas_call(
        prepare_body,
        out_shape=(
            jax.ShapeDtypeStruct((positions, win, win), f32),
            jax.ShapeDtypeStruct((positions, 2, win, win), f32),
            jax.ShapeDtypeStruct((8, win, 3 * win), bf16),
            jax.ShapeDtypeStruct((8, 3 * win, win), bf16),
        ),
        grid_spec=pltpu.PrefetchScalarGridSpec(
            num_scalar_prefetch=2,
            grid=(positions,),
            in_specs=[
                pl.BlockSpec((1, win, win), lambda j, pattern, starts: (pattern[j], 0, 0)),
                pl.BlockSpec((2, win, win), lambda j, pattern, starts: (0, 0, 0)),
                pl.BlockSpec((2, win, win), lambda j, pattern, starts: (0, 0, 0)),
                pl.BlockSpec((1, 2, win, win), lambda j, pattern, starts: (lax.rem(j, 4), 0, 0, 0)),
            ],
            out_specs=[
                pl.BlockSpec((1, win, win), lambda j, pattern, starts: (j, 0, 0)),
                pl.BlockSpec((1, 2, win, win), lambda j, pattern, starts: (j, 0, 0, 0)),
                pl.BlockSpec((1, win, 3 * win), lambda j, pattern, starts: (j, 0, 0)),
                pl.BlockSpec((1, 3 * win, win), lambda j, pattern, starts: (j, 0, 0)),
            ],
        ),
        cost_estimate=pl.CostEstimate(flops=2 * 6 * positions * win**3, bytes_accessed=16 << 20, transcendentals=0),
        name="prepare",
    )(pattern, starts, measured, probe, order, parts)


def complex_mul(left_re, left_im, right_re, right_im):
    return (left_re * right_re - left_im * right_im, left_re * right_im + left_im * right_re)


def conj_mul(left_re, left_im, right_re, right_im):
    return (left_re * right_re + left_im * right_im, left_re * right_im - left_im * right_re)


def put_left(ref, side, row, value):
    high = value.astype(bf16)
    low = (value - high.astype(f32)).astype(bf16)
    size = value.shape[0]
    ref[side, row : row + size, :] = high
    ref[side, win + row : win + row + size, :] = low
    ref[side, 2 * win + row : 2 * win + row + size, :] = high


def put_right(ref, side, row, lane, value):
    high = value.astype(bf16)
    low = (value - high.astype(f32)).astype(bf16)
    size = value.shape[0]
    ref[side, row : row + size, lane : lane + half] = high
    ref[side, row : row + size, win + lane : win + lane + half] = low
    ref[side, row : row + size, 2 * win + lane : 2 * win + lane + half] = high


def core_body(
    starts_ref, flags_ref,
    one_ref, two_ref, ca_ref, cb_ref, ra_ref, rb_ref,
    rolled_ref, sorted_ref, ltab_ref, rtab_ref,
    out_ra, out_rb, out_mid, out_keep, out_send,
    wide, total, share, *slots,
):
    step = pl.program_id(0)
    R = rows_at_once
    row_odd, col_odd = flags_ref[0], flags_ref[1]
    row_a = pl.multiple_of((1 - row_odd) * (win + half), half)
    row_b = pl.multiple_of(row_odd * (win + half), half)
    lane_a = pl.multiple_of((1 - col_odd) * (win + half), half)
    lane_b = pl.multiple_of(col_odd * (win + half), half)

    @pl.when(step == 0)
    def _():
        wide[:, pl.ds(row_a, half), :] = ra_ref[...]
        wide[:, pl.ds(row_b, half), :] = rb_ref[...]
        wide[:, half : half + win, pl.ds(lane_a, half)] = ca_ref[...]
        wide[:, half : half + win, pl.ds(lane_b, half)] = cb_ref[...]
        wide[0:2, half : half + win, half : half + win] = one_ref[...]
        wide[2:4, half : half + win, half : half + win] = two_ref[...]
        total[...] = jnp.zeros_like(total)
        share[...] = jnp.zeros_like(share)

    def work(slot):
        xa, xb, res, phi, shares = slots[5 * slot : 5 * slot + 5]
        position = at_once * step + slot
        a = starts_ref[position, 0]
        b = starts_ref[position, 1]
        offset = lax.rem(a, 8)
        base = pl.multiple_of(a - offset, 8)
        near = lax.broadcasted_iota(jnp.int32, (R, win), 1) >= b
        below = lax.broadcasted_iota(jnp.int32, (R, win), 0) >= offset

        def row_sets(row):
            first = (pl.ds(base + row, R), None)
            return (first,) if row else (first, (pl.ds(base + win, R), below))

        def window(plane, row):
            value = None
            for rows, mask in row_sets(row):
                block = jnp.where(near, wide[plane, rows, 0:win], wide[plane, rows, win : 2 * win])
                value = block if mask is None else jnp.where(mask, value, block)
            return value

        def add_window(plane, row, value):
            zero = jnp.zeros_like(value)
            for rows, mask in row_sets(row):
                part = value
                if row == 0:
                    part = jnp.where(below, value, zero) if mask is None else jnp.where(below, zero, value)
                total[plane, rows, 0:win] += jnp.where(near, part, zero)
                total[plane, rows, win : 2 * win] += jnp.where(near, zero, part)

        def left_stage(first):
            for side in range(2):
                res[side] = jnp.dot(ltab_ref[first + side], xa[side], preferred_element_type=f32)

        def right_stage(first):
            for side in range(2):
                res[side] = jnp.dot(xb[side], rtab_ref[first + side], preferred_element_type=f32)

        def row_butterfly(row, upper, lower):
            for part in range(2):
                put_left(xa, 0, part * half + row, upper[part] + lower[part])
                put_left(xa, 1, part * half + row, upper[part] - lower[part])

        def lane_butterfly(row, field):
            for part in range(2):
                near_half, far_half = field[part][:, :half], field[part][:, half:]
                put_right(xb, 0, row, part * half, near_half + far_half)
                put_right(xb, 1, row, part * half, near_half - far_half)

        def lane_join(row):
            out = []
            for part in range(2):
                plus = res[0, row : row + R, part * half : (part + 1) * half]
                minus = res[1, row : row + R, part * half : (part + 1) * half]
                out.append(jnp.concatenate([plus + minus, plus - minus], axis=1))
            return out

        def row_join(row):
            plus = [res[0, part * half + row : part * half + row + R, :] for part in range(2)]
            minus = [res[1, part * half + row : part * half + row + R, :] for part in range(2)]
            return [p + m for p, m in zip(plus, minus)], [p - m for p, m in zip(plus, minus)]

        def rows_to_lanes():
            for row in range(0, half, R):
                upper, lower = row_join(row)
                lane_butterfly(row, upper)
                lane_butterfly(half + row, lower)

        def add_share(plane, value):
            value = pltpu.roll(value, jnp.where(offset == 0, 0, win - offset), axis=0)
            share[plane] += pltpu.roll(value, jnp.where(b == 0, 0, win - b), axis=1)

        def probe(part, row):
            return rolled_ref[slot, part, row : row + R, :]

        for row in range(0, half, R):
            pair = []
            for at in (row, half + row):
                o_re, o_im = window(0, at), window(1, at)
                shares[0, at : at + R, :] = o_re * o_re + o_im * o_im
                pair.append(complex_mul(probe(0, at), probe(1, at), o_re, o_im))
            row_butterfly(row, *pair)
        yield
        left_stage(4)
        add_share(2, shares[0])
        yield
        rows_to_lanes()
        yield
        right_stage(0)
        yield
        for row in range(0, half, R):
            pair = []
            for at in (row, half + row):
                p_re, p_im = lane_join(at)
                phi[0, at : at + R, :] = p_re
                phi[1, at : at + R, :] = p_im
                pair.append(complex_mul(p_re, p_im, window(2, at), window(3, at)))
            row_butterfly(row, *pair)
        yield
        left_stage(6)
        yield
        for side in range(2):
            for row in range(0, half, R):
                lane_butterfly(
                    side * half + row, [res[side, part * half + row : part * half + row + R, :] for part in range(2)]
                )
        yield
        right_stage(2)
        yield
        for side in range(2):
            for row in range(0, win, R):
                far_re = res[side, row : row + R, 0:half]
                far_im = res[side, row : row + R, half:win]
                amplitude = sorted_ref[slot, row : row + R, side * half : (side + 1) * half]
                factor = 1.0 - amplitude * lax.rsqrt(far_re * far_re + far_im * far_im + 1.0)
                put_right(xb, side, row, 0, factor * far_re)
                put_right(xb, side, row, half, factor * far_im)
        yield
        right_stage(6)
        yield
        for side in range(2):
            for row in range(0, half, R):
                field = lane_join(side * half + row)
                for part in range(2):
                    put_left(xa, side, part * half + row, field[part])
        yield
        left_stage(2)
        yield
        for row in range(0, half, R):
            pair = []
            for at, (g_re, g_im) in zip((row, half + row), row_join(row)):
                t_re, t_im = conj_mul(phi[0, at : at + R, :], phi[1, at : at + R, :], g_re, g_im)
                add_window(2, at, t_re)
                add_window(3, at, t_im)
                pair.append(conj_mul(window(2, at), window(3, at), g_re, g_im))
            row_butterfly(row, *pair)
        yield
        left_stage(0)
        yield
        rows_to_lanes()
        yield
        right_stage(4)
        yield
        for at in range(0, win, R):
            g_re, g_im = lane_join(at)
            t_re, t_im = conj_mul(probe(0, at), probe(1, at), g_re, g_im)
            add_window(0, at, t_re)
            add_window(1, at, t_im)
            s_re, s_im = conj_mul(window(0, at), window(1, at), g_re, g_im)
            shares[0, at : at + R, :] = s_re
            shares[1, at : at + R, :] = s_im
        add_share(0, shares[0])
        add_share(1, shares[1])
        yield

    running = [work(slot) for slot in range(at_once)]
    live = []
    while running or live:
        if running:
            live.append(running.pop(0))
        live = [w for w in live if next(w, "end") is None]

    @pl.when(step == positions // at_once - 1)
    def _():
        out_ra[...] = total[:, pl.ds(row_a, half), :]
        out_rb[...] = total[:, pl.ds(row_b, half), :]
        out_mid[...] = total[:, half : half + win, :]
        out_keep[...] = share[:, pl.ds(pl.multiple_of(col_odd * half, half), half), :]
        out_send[...] = share[:, pl.ds(pl.multiple_of((1 - col_odd) * half, half), half), :]


def whole(*shape):
    return pl.BlockSpec(shape, lambda *ids: (0,) * len(shape))


def core(starts, flags, one, two, ca, cb, ra, rb, rolled, ordered, ltab, rtab):
    shapes = ((4, half, 2 * win), (4, half, 2 * win), (4, win, 2 * win), (3, half, win), (3, half, win))
    slot = [
        pltpu.VMEM((2, 3 * win, win), bf16),
        pltpu.VMEM((2, win, 3 * win), bf16),
        pltpu.VMEM((2, win, win), f32),
        pltpu.VMEM((2, win, win), f32),
        pltpu.VMEM((2, win, win), f32),
    ]
    return pl.pallas_call(
        core_body,
        out_shape=[jax.ShapeDtypeStruct(shape, f32) for shape in shapes],
        grid_spec=pltpu.PrefetchScalarGridSpec(
            num_scalar_prefetch=2,
            grid=(positions // at_once,),
            in_specs=[
                whole(2, win, win), whole(2, win, win), whole(4, win, half), whole(4, win, half),
                whole(4, half, 2 * win), whole(4, half, 2 * win),
                pl.BlockSpec((at_once, 2, win, win), lambda j, *prefetched: (j, 0, 0, 0)),
                pl.BlockSpec((at_once, win, win), lambda j, *prefetched: (j, 0, 0)),
                whole(8, win, 3 * win), whole(8, 3 * win, win),
            ],
            out_specs=[whole(*shape) for shape in shapes],
            scratch_shapes=[
                pltpu.VMEM((4, 2 * win + 8, 2 * win), f32),
                pltpu.VMEM((4, 2 * win + 8, 2 * win), f32),
                pltpu.VMEM((3, win, win), f32),
            ] + slot * at_once,
        ),
        compiler_params=pltpu.CompilerParams(vmem_limit_bytes=60 << 20),
        cost_estimate=pl.CostEstimate(flops=48 * 2 * positions * win**3, bytes_accessed=32 << 20, transcendentals=0),
        name="core",
    )(starts, flags, one, two, ca, cb, ra, rb, rolled, ordered, ltab, rtab)


def small_kernel(kernel, name, flags, inputs, shapes):
    size = sum(x.size for x in inputs) + sum(math.prod(shape) for shape in shapes)
    return pl.pallas_call(
        kernel,
        out_shape=[jax.ShapeDtypeStruct(shape, f32) for shape in shapes],
        grid_spec=pltpu.PrefetchScalarGridSpec(
            num_scalar_prefetch=1,
            grid=(1,),
            in_specs=[whole(*x.shape) for x in inputs],
            out_specs=[whole(*shape) for shape in shapes],
        ),
        compiler_params=pltpu.CompilerParams(vmem_limit_bytes=48 << 20),
        cost_estimate=pl.CostEstimate(flops=size, bytes_accessed=4 * size, transcendentals=0),
        name=name,
    )(flags, *inputs)


def half_at(choice):
    return pl.ds(pl.multiple_of(choice * half, half), half)


def pack_columns(flags_ref, one_ref, two_ref, a_ref, b_ref):
    odd = flags_ref[1]
    for out, lanes in ((a_ref, half_at(1 - odd)), (b_ref, half_at(odd))):
        out[0:2] = one_ref[:, :, lanes]
        out[2:4] = two_ref[:, :, lanes]


def pack_rows(flags_ref, one_ref, two_ref, ca_ref, cb_ref, a_ref, b_ref):
    row_odd, col_odd = flags_ref[0], flags_ref[1]
    for out, rows in ((a_ref, half_at(1 - row_odd)), (b_ref, half_at(row_odd))):
        out[0:2, :, half : half + win] = one_ref[:, rows, :]
        out[2:4, :, half : half + win] = two_ref[:, rows, :]
        out[:, :, half_at(3 * (1 - col_odd))] = ca_ref[:, rows, :]
        out[:, :, half_at(3 * col_odd)] = cb_ref[:, rows, :]


def fold_rows(flags_ref, mid_ref, qa_ref, qb_ref, a_ref, b_ref, center_ref):
    row_odd, col_odd = flags_ref[0], flags_ref[1]
    for got, rows in ((qa_ref, half_at(1 - row_odd)), (qb_ref, half_at(row_odd))):
        center_ref[:, rows, :] = mid_ref[:, rows, half : half + win] + got[:, :, half : half + win]
        for out, lanes in ((a_ref, half_at(3 * (1 - col_odd))), (b_ref, half_at(3 * col_odd))):
            out[:, rows, :] = mid_ref[:, rows, lanes] + got[:, :, lanes]


def fold_columns(flags_ref, center_ref, a_ref, b_ref, one_ref, two_ref):
    odd = flags_ref[1]
    for got, lanes in ((a_ref, half_at(1 - odd)), (b_ref, half_at(odd))):
        one_ref[:, :, lanes] = center_ref[0:2, :, lanes] + got[0:2]
        two_ref[:, :, lanes] = center_ref[2:4, :, lanes] + got[2:4]


def pack_share(flags_ref, keep_ref, got_ref, out_ref):
    for tile in range(64):
        for plane, spot in ((tile // 32, 0), (2, 8)):
            rows = slice(tile % 32 // 2 * 8, tile % 32 // 2 * 8 + 8)
            lanes = slice(tile % 2 * half, tile % 2 * half + half)
            out_ref[tile, spot : spot + 8, :] = keep_ref[plane, rows, lanes] + got_ref[plane, rows, lanes]


def take_step(flags_ref, parts_ref, out_ref):
    total = parts_ref[0]
    for tile in range(1, 64):
        total = total + parts_ref[tile]
    step = total[0:8] * lax.rsqrt(total[8:16] + 1.0)
    for tile in range(64):
        out_ref[tile] = step


def join_step(flags_ref, own_ref, other_ref, out_ref):
    odd = flags_ref[1]
    for tile in range(64):
        row = tile % 32 // 2 * 8
        lanes = slice(tile % 2 * half, tile % 2 * half + half)
        out_ref[tile // 32, pl.ds(pl.multiple_of(odd * half + row, 8), 8), lanes] = own_ref[tile]
        out_ref[tile // 32, pl.ds(pl.multiple_of((1 - odd) * half + row, 8), 8), lanes] = other_ref[tile]


def swapped(block, axis, first):
    pairs = [(i, i + 1) for i in range(first, lax.axis_size(axis) - 1, 2)]
    return lax.ppermute(block, axis, pairs + [(j, i) for i, j in pairs])


def exchanged(parts):
    rows, cols = lax.axis_size("row"), lax.axis_size("col")
    groups = [[r * cols + c for r in range(rows) for c in range(odd, cols, 2)] for odd in range(2)]
    return lax.all_to_all(parts, ("row", "col"), 0, 0, axis_index_groups=groups, tiled=True)


def body(object_one, object_two, probe, scan_pos, pattern_index, measured):
    starts = scan_pos[0, 0]
    flags = jnp.stack([lax.axis_index("row") % 2, lax.axis_index("col") % 2]).astype(jnp.int32)
    side, slab = (4, win, half), (4, half, 2 * win)
    ca, cb = small_kernel(pack_columns, "pack_columns", flags, (object_one, object_two), (side, side))
    ca, cb = swapped(ca, "col", 0), swapped(cb, "col", 1)
    ra, rb = small_kernel(pack_rows, "pack_rows", flags, (object_one, object_two, ca, cb), (slab, slab))
    ra, rb = swapped(ra, "row", 0), swapped(rb, "row", 1)
    ordered, rolled, ltab, rtab = prepare(pattern_index[0, 0], starts, measured[0, 0], probe)
    out_ra, out_rb, mid, keep, send = core(
        starts, flags, object_one, object_two, ca, cb, ra, rb, rolled, ordered, ltab, rtab
    )
    share = small_kernel(pack_share, "pack_share", flags, (keep, swapped(send, "col", 0)), ((64, 16, half),))[0]
    qa, qb = swapped(out_ra, "row", 0), swapped(out_rb, "row", 1)
    fa, fb, center = small_kernel(fold_rows, "fold_rows", flags, (mid, qa, qb), (side, side, (4, win, win)))
    ga, gb = swapped(fa, "col", 0), swapped(fb, "col", 1)
    step = small_kernel(take_step, "take_step", flags, (exchanged(share),), ((64, 8, half),))[0]
    step = exchanged(step)
    tile_shape = (2, win, win)
    grad_one, grad_two = small_kernel(fold_columns, "fold_columns", flags, (center, ga, gb), (tile_shape, tile_shape))
    probe_step = small_kernel(join_step, "join_step", flags, (step, swapped(step, "col", 0)), (tile_shape,))[0]
    return (grad_one, grad_two, probe_step)


def solution(mesh):
    placed = (
        P(None, "row", "col"),
        P(None, "row", "col"),
        P(),
        P("row", "col", None, None),
        P("row", "col", None),
        P("row", "col", None, None, None),
    )
    return jax.shard_map(
        body,
        mesh=mesh,
        in_specs=placed,
        out_specs=(P(None, "row", "col"), P(None, "row", "col"), P()),
        check_vma=False,
    )
```

time: 179 us -> 156 us (0.87)
  blocking collectives: 62.3 us -> 18.8 us
  waiting for transfers between devices: 19.8 us -> 43.1 us
  other arithmetic: 5.92 us -> 0.08 us
  Pallas kernels: 48.9 us -> 52.8 us
  starting transfers between devices: 31.2 us -> 33.3 us
  local copies, waits for them, and re-layouts: 7.89 us -> 6 us
    all_to_all x2 -> x1, blocking collectives: 62.3 us -> 18.8 us  [exchanged(): lax.all_to_all(parts, ('row', 'col'), 0, 0, axis_index_groups=groups, til...]
    ppermute x8 -> x10, waiting for transfers between devices: 19.8 us -> 43.1 us  [swapped(): return lax.ppermute(block, axis, pairs + [(j, i) for i, j in pairs])]
    all_to_all x0 -> x1, starting transfers between devices: none -> 10.6 us  [exchanged(): lax.all_to_all(parts, ('row', 'col'), 0, 0, axis_index_groups=groups, til...]
    ppermute x8 -> x10, starting transfers between devices: 31.2 us -> 22.7 us  [swapped(): return lax.ppermute(block, axis, pairs + [(j, i) for i, j in pairs])]
    add x2 -> x0, other arithmetic: 3.66 us -> none  [the longest x1 2.36 us: body(): out_mid[:, half:] + from_below]
    reshape x4 -> x0, local copies, waits for them, and re-layouts: 3.1 us -> none  [the longest x2 1.56 us: summed_step(): share.reshape(3, devices, rows * win // half, half).transpose(1, 0, 2, 3)]
    unnamed x11 -> x20, local copies, waits for them, and re-layouts: 2.34 us -> 5.34 us
    pallas_call x1 -> x8, Pallas kernels: 39.2 us -> 41.8 us  [the longest x1 31 us: core(): pl.pallas_call(core_body, out_shape=[jax.ShapeDtypeStruct(shape, f32) for...]
  transfers between devices with their start and end apart: 8 -> 11, of which waited for: 4 -> 7; matrix products, arithmetic and copies ran while one was open for 3% -> 0% of each run, Pallas kernels for 6% -> 11%
where the time goes in v2:
time: 156 us; the launch traced here: 155 us
  Pallas kernels  52.8 us (34%)
  waiting for transfers between devices  43.1 us (28%)
  starting transfers between devices  33.3 us (21%)
  blocking collectives  18.8 us (12%)
  local copies, waits for them, and re-layouts  6 us (4%)
    ppermute x10, waiting for transfers between devices, swapped(): return lax.ppermute(block, axis, pairs + [(j, i) for i, j in pairs])  43.1 us
    pallas_call x1, Pallas kernels, core(): pl.pallas_call(core_body, out_shape=[jax.ShapeDtypeStruct(shape, f32) for...  31 us
    ppermute x10, starting transfers between devices, swapped(): return lax.ppermute(block, axis, pairs + [(j, i) for i, j in pairs])  22.7 us
    all_to_all x1, blocking collectives, exchanged(): lax.all_to_all(parts, ('row', 'col'), 0, 0, axis_index_groups=groups, til...  18.8 us
    pallas_call x1, Pallas kernels, prepare(): pl.pallas_call(prepare_body, out_shape=(jax.ShapeDtypeStruct((positions,...  11 us
    pallas_call x7, Pallas kernels, small_kernel(): pl.pallas_call(kernel, out_shape=[jax.ShapeDtypeStruct(shape, f32) for sh...  10.8 us
    all_to_all x1, starting transfers between devices, exchanged(): lax.all_to_all(parts, ('row', 'col'), 0, 0, axis_index_groups=groups, til...  10.6 us
    unnamed x20, local copies, waits for them, and re-layouts  5.34 us
  transfers between devices with their start and end apart: 11, of which 7 were waited for; matrix products, arithmetic and copies ran while one was open for 0% of the time, Pallas kernels for 11%

profile of v2, /device:TPU:7, one launch (start us, length us, event | category | flops | bytes accessed | tf_op | source)
XLA Modules:
  0.0 154.9 jit_solution(13453396372556559773)
XLA Ops:
  0.7 1.0 copy-done
  1.8 1.0 copy-done.1
  2.8 0.6 pack_columns.1
  3.4 0.8 collective-permute-start
  4.2 3.7 %collective-permute-start.1 = (f32[4,256,128]{2,1,0:T(8,128)S(1)}, f32[4,256,128]{2,1,0:T(8,128)S(1)}, u32[]{:S(2)}, u32[]{:S(2)}) collective-permute-start(f32[4,256,128]{2,1,0:T(8,128)S(1)} %get-tuple-element.22), channel_id=1, source_target_pairs={{1,2},{3,4},{5,6},{7,8},{9,10},{11,12},{13,14},{2,1},{4,3},{6,5},{... | collective-permute-start | bytes 1572872 | tf_op jit(solution)/shard_map/ppermute | solution.py:458
  7.9 13.1 %collective-permute-done.1.cb_ref = f32[4,256,128]{2,1,0:T(8,128)S(1)} collective-permute-done((f32[4,256,128]{2,1,0:T(8,128)S(1)}, f32[4,256,128]{2,1,0:T(8,128)S(1)}, u32[]{:S(2)}, u32[]{:S(2)}) %collective-permute-start.1) | collective-permute-done | bytes 524320 | tf_op jit(solution)/shard_map/ppermute | solution.py:458
  21.0 1.8 %pack_rows.1 = (f32[4,128,512]{2,1,0:T(8,128)}, f32[4,128,512]{2,1,0:T(8,128)S(1)}) custom-call(s32[2]{0:T(128)S(1)} %pad_add_fusion.flags_ref, f32[2,256,256]{2,1,0:T(8,128)S(1)} %copy-done, f32[2,256,256]{2,1,0:T(8,128)S(1)} %copy-done.1, f32[4,256,128]{2,1,0:T(8,128)S(1)} %collective-permute-done.ca_ref, f32[4,256,128]{2,1,0:T(8,128)S(1)} %collective-permute-done.1.cb_ref), custom_call_target="tpu_custom_call" | custom-call | flops 1048576 | bytes 4194304 | tf_op jit(solution)/shard_map/pack_rows/pallas_call | solution.py:380
  22.8 1.3 collective-permute-start.2
  24.1 4.6 %collective-permute-start.3 = (f32[4,128,512]{2,1,0:T(8,128)S(1)}, f32[4,128,512]{2,1,0:T(8,128)}, u32[]{:S(2)}, u32[]{:S(2)}) collective-permute-start(f32[4,128,512]{2,1,0:T(8,128)S(1)} %get-tuple-element.24), channel_id=1, source_target_pairs={{16,32},{48,64},{80,96},{32,16},{64,48},{96,80},{17,33},{49,65},{8... | collective-permute-start | bytes 3145736 | tf_op jit(solution)/shard_map/ppermute | solution.py:458
  28.7 0.7 copy.12.starts_ref
  29.4 11.0 %prepare.1 = (f32[8,256,256]{2,1,0:T(8,128)}, f32[8,2,256,256]{3,2,1,0:T(8,128)}, bf16[8,256,768]{2,1,0:T(8,128)(2,1)}, bf16[8,768,256]{2,1,0:T(8,128)(2,1)}) custom-call(s32[8]{0:T(128)} %bitcast.7, s32[8,2]{1,0:T(8,128)} %copy.12.starts_ref, f32[8,256,256]{2,1,0:T(8,128)} %bitcast.6, f32[2,256,256]{2,1,0:T(8,128)} %probe_ref.1, ...), custom_call_target="tpu_custom_call" | custom-call | flops 1610612736 | bytes 16777216 | tf_op jit(solution)/shard_map/prepare/pallas_call | solution.py:87
  40.5 5.9 %collective-permute-done.2.ra_ref = f32[4,128,512]{2,1,0:T(8,128)} collective-permute-done((f32[4,128,512]{2,1,0:T(8,128)}, f32[4,128,512]{2,1,0:T(8,128)}, u32[]{:S(2)}, u32[]{:S(2)}) %collective-permute-start.2) | collective-permute-done | bytes 1048608 | tf_op jit(solution)/shard_map/ppermute | solution.py:458
  46.4 6.6 %collective-permute-done.3.rb_ref = f32[4,128,512]{2,1,0:T(8,128)} collective-permute-done((f32[4,128,512]{2,1,0:T(8,128)S(1)}, f32[4,128,512]{2,1,0:T(8,128)}, u32[]{:S(2)}, u32[]{:S(2)}) %collective-permute-start.3) | collective-permute-done | bytes 1048608 | tf_op jit(solution)/shard_map/ppermute | solution.py:458
  53.0 31.0 %core.1 = (f32[4,128,512]{2,1,0:T(8,128)}, f32[4,128,512]{2,1,0:T(8,128)}, f32[4,256,512]{2,1,0:T(8,128)}, f32[3,128,256]{2,1,0:T(8,128)}, f32[3,128,256]{2,1,0:T(8,128)}) custom-call(s32[8,2]{1,0:T(8,128)} %copy.12.starts_ref, s32[2]{0:T(128)} %copy-done.7, f32[2,256,256]{2,1,0:T(8,128)} %one_ref.5, f32[2,256,256]{2,1,0:T(8,128)} %two_ref.5, ...), custom_call_target="tpu_custom_call" | custom-call | flops 12884901888 | bytes 33554432 | tf_op jit(solution)/shard_map/core/pallas_call | solution.py:352
  84.0 4.4 %collective-permute-start.5 = (f32[4,128,512]{2,1,0:T(8,128)}, f32[4,128,512]{2,1,0:T(8,128)S(1)}, u32[]{:S(2)}, u32[]{:S(2)}) collective-permute-start(f32[4,128,512]{2,1,0:T(8,128)} %get-tuple-element.31), channel_id=1, source_target_pairs={{16,32},{48,64},{80,96},{32,16},{64,48},{96,80},{17,33},{49,65},{8... | collective-permute-start | bytes 3145736 | tf_op jit(solution)/shard_map/ppermute | solution.py:458
  88.5 1.9 %collective-permute-done.8.got_ref = f32[3,128,256]{2,1,0:T(8,128)S(1)} collective-permute-done((f32[3,128,256]{2,1,0:T(8,128)}, f32[3,128,256]{2,1,0:T(8,128)S(1)}, u32[]{:S(2)}, u32[]{:S(2)}) %collective-permute-start.8) | collective-permute-done | bytes 393248 | tf_op jit(solution)/shard_map/ppermute | solution.py:458
  90.4 1.0 copy-done.6
  91.4 1.4 pack_share.1
  92.8 10.6 %all-to-all-start = ((f32[64,16,128]{2,1,0:T(8,128)}), f32[64,16,128]{2,1,0:T(8,128)S(1)}, u32[]{:S(2)}, u32[]{:S(2)}) async-start(f32[64,16,128]{2,1,0:T(8,128)} %pack_share.1), calls=%async_computation | async-start | bytes 1048576 | tf_op jit(solution)/shard_map/all_to_all | solution.py:464
  103.4 10.2 %collective-permute-done.4.qa_ref = f32[4,128,512]{2,1,0:T(8,128)S(1)} collective-permute-done((f32[4,128,512]{2,1,0:T(8,128)}, f32[4,128,512]{2,1,0:T(8,128)S(1)}, u32[]{:S(2)}, u32[]{:S(2)}) %collective-permute-start.4) | collective-permute-done | bytes 1048608 | tf_op jit(solution)/shard_map/ppermute | solution.py:458
  113.6 4.3 %collective-permute-done.5.qb_ref = f32[4,128,512]{2,1,0:T(8,128)S(1)} collective-permute-done((f32[4,128,512]{2,1,0:T(8,128)}, f32[4,128,512]{2,1,0:T(8,128)S(1)}, u32[]{:S(2)}, u32[]{:S(2)}) %collective-permute-start.5) | collective-permute-done | bytes 1048608 | tf_op jit(solution)/shard_map/ppermute | solution.py:458
  117.9 3.3 %fold_rows.1 = (f32[4,256,128]{2,1,0:T(8,128)}, f32[4,256,128]{2,1,0:T(8,128)S(1)}, f32[4,256,256]{2,1,0:T(8,128)S(1)}) custom-call(s32[2]{0:T(128)S(1)} %copy-done.8, f32[4,256,512]{2,1,0:T(8,128)} %get-tuple-element.29.mid_ref, f32[4,128,512]{2,1,0:T(8,128)S(1)} %collective-permute-done.4.qa_ref, f32[4,128,512]{2,1,0:T(8,128)S(1)} %collective-permute-done.5.qb_ref), custom_call_target="tpu_custom_call" | custom-call | flops 1572864 | bytes 6291456 | tf_op jit(solution)/shard_map/fold_rows/pallas_call | solution.py:380
  121.1 1.0 copy-done.2
  122.2 0.1 collective-permute-start.6
  122.3 6.7 %collective-permute-start.7 = (f32[4,256,128]{2,1,0:T(8,128)S(1)}, f32[4,256,128]{2,1,0:T(8,128)S(1)}, u32[]{:S(2)}, u32[]{:S(2)}) collective-permute-start(f32[4,256,128]{2,1,0:T(8,128)S(1)} %get-tuple-element.34), channel_id=1, source_target_pairs={{1,2},{3,4},{5,6},{7,8},{9,10},{11,12},{13,14},{2,1},{4,3},{6,5},{... | collective-permute-start | bytes 1572872 | tf_op jit(solution)/shard_map/ppermute | solution.py:458
  129.0 0.6 take_step.1
  129.6 18.8 %all_to_all.10.own_ref = f32[64,8,128]{2,1,0:T(8,128)S(1)} all-to-all(f32[64,8,128]{2,1,0:T(8,128)S(1)} %take_step.1), channel_id=1, replica_groups={{0,2,4,6,8,10,12,14,16,18,20,22,24,26,28,30,32,34,36,38,40,42,44,46,48,..., dimensions={0} | all-to-all | bytes 524288 | tf_op jit(solution)/shard_map/all_to_all | solution.py:464
  148.4 1.1 collective-permute-start.9
  149.4 1.2 collective-permute-done.9.other_ref
  150.6 1.4 join_step.1
  152.0 1.2 copy-done.3
  153.3 1.7 %fold_columns.1 = (f32[2,256,256]{2,1,0:T(8,128)}, f32[2,256,256]{2,1,0:T(8,128)}) custom-call(s32[2]{0:T(128)S(1)} %copy-done.8, f32[4,256,256]{2,1,0:T(8,128)S(1)} %copy-done.3, f32[4,256,128]{2,1,0:T(8,128)S(1)} %collective-permute-done.6.a_ref, f32[4,256,128]{2,1,0:T(8,128)S(1)} %collective-permute-done.7.b_ref), custom_call_target="tpu_custom_call" | custom-call | flops 786432 | bytes 3145728 | tf_op jit(solution)/shard_map/fold_columns/pallas_call | solution.py:380
  (22 shorter events, 0.2 us)
Async XLA Ops:
  0.6 28.1 %copy-start.9 = (s32[1,1,8,2]{2,3,1,0:T(2,128)S(1)}, s32[1,1,8,2]{2,3,1,0:T(2,128)}, u32[]{:S(2)}) copy-start(s32[1,1,8,2]{2,3,1,0:T(2,128)} %param.11) | copy-start | bytes 196
  0.7 1.0 copy-start
  1.8 1.0 copy-start.1
  2.8 37.6 %copy-start.7 = (s32[2]{0:T(128)}, s32[2]{0:T(128)S(1)}, u32[]{:S(2)}) copy-start(s32[2]{0:T(128)S(1)} %pad_add_fusion.flags_ref) | copy-start | bytes 28
  3.4 4.5 %collective-permute-start = (f32[4,256,128]{2,1,0:T(8,128)S(1)}, f32[4,256,128]{2,1,0:T(8,128)S(1)}, u32[]{:S(2)}, u32[]{:S(2)}) collective-permute-start(f32[4,256,128]{2,1,0:T(8,128)S(1)} %get-tuple-element.21), channel_id=1, source_target_pairs={{0,1},{2,3},{4,5},{6,7},{8,9},{10,11},{12,13},{14,15},{1,0},{3,2},... | collective-permute-start | bytes 1572872 | tf_op jit(solution)/shard_map/ppermute | solution.py:458
  4.2 16.8 %collective-permute-start.1 = (f32[4,256,128]{2,1,0:T(8,128)S(1)}, f32[4,256,128]{2,1,0:T(8,128)S(1)}, u32[]{:S(2)}, u32[]{:S(2)}) collective-permute-start(f32[4,256,128]{2,1,0:T(8,128)S(1)} %get-tuple-element.22), channel_id=1, source_target_pairs={{1,2},{3,4},{5,6},{7,8},{9,10},{11,12},{13,14},{2,1},{4,3},{6,5},{... | collective-permute-start | bytes 1572872 | tf_op jit(solution)/shard_map/ppermute | solution.py:458
  7.9 32.5 %copy-start.4 = (f32[4,256,128]{2,1,0:T(8,128)}, f32[4,256,128]{2,1,0:T(8,128)S(1)}, u32[]{:S(2)}) copy-start(f32[4,256,128]{2,1,0:T(8,128)S(1)} %collective-permute-done.ca_ref) | copy-start | bytes 1572868
  21.0 19.5 %copy-start.5 = (f32[4,256,128]{2,1,0:T(8,128)}, f32[4,256,128]{2,1,0:T(8,128)S(1)}, u32[]{:S(2)}) copy-start(f32[4,256,128]{2,1,0:T(8,128)S(1)} %collective-permute-done.1.cb_ref) | copy-start | bytes 1572868
  22.8 23.6 %collective-permute-start.2 = (f32[4,128,512]{2,1,0:T(8,128)}, f32[4,128,512]{2,1,0:T(8,128)}, u32[]{:S(2)}, u32[]{:S(2)}) collective-permute-start(f32[4,128,512]{2,1,0:T(8,128)} %get-tuple-element.23), channel_id=1, source_target_pairs={{0,16},{32,48},{64,80},{96,112},{16,0},{48,32},{80,64},{112,96},{1... | collective-permute-start | bytes 3145736 | tf_op jit(solution)/shard_map/ppermute | solution.py:458
  24.1 28.9 %collective-permute-start.3 = (f32[4,128,512]{2,1,0:T(8,128)S(1)}, f32[4,128,512]{2,1,0:T(8,128)}, u32[]{:S(2)}, u32[]{:S(2)}) collective-permute-start(f32[4,128,512]{2,1,0:T(8,128)S(1)} %get-tuple-element.24), channel_id=1, source_target_pairs={{16,32},{48,64},{80,96},{32,16},{64,48},{96,80},{17,33},{49,65},{8... | collective-permute-start | bytes 3145736 | tf_op jit(solution)/shard_map/ppermute | solution.py:458
  53.0 37.4 %copy-start.8 = (s32[2]{0:T(128)S(1)}, s32[2]{0:T(128)}, u32[]{:S(2)}) copy-start(s32[2]{0:T(128)} %copy-done.7) | copy-start | bytes 28
  84.0 29.6 %collective-permute-start.4 = (f32[4,128,512]{2,1,0:T(8,128)}, f32[4,128,512]{2,1,0:T(8,128)S(1)}, u32[]{:S(2)}, u32[]{:S(2)}) collective-permute-start(f32[4,128,512]{2,1,0:T(8,128)} %get-tuple-element.30), channel_id=1, source_target_pairs={{0,16},{32,48},{64,80},{96,112},{16,0},{48,32},{80,64},{112,96},{1... | collective-permute-start | bytes 3145736 | tf_op jit(solution)/shard_map/ppermute | solution.py:458
  84.0 33.9 %collective-permute-start.5 = (f32[4,128,512]{2,1,0:T(8,128)}, f32[4,128,512]{2,1,0:T(8,128)S(1)}, u32[]{:S(2)}, u32[]{:S(2)}) collective-permute-start(f32[4,128,512]{2,1,0:T(8,128)} %get-tuple-element.31), channel_id=1, source_target_pairs={{16,32},{48,64},{80,96},{32,16},{64,48},{96,80},{17,33},{49,65},{8... | collective-permute-start | bytes 3145736 | tf_op jit(solution)/shard_map/ppermute | solution.py:458
  88.4 2.0 %collective-permute-start.8 = (f32[3,128,256]{2,1,0:T(8,128)}, f32[3,128,256]{2,1,0:T(8,128)S(1)}, u32[]{:S(2)}, u32[]{:S(2)}) collective-permute-start(f32[3,128,256]{2,1,0:T(8,128)} %get-tuple-element.38), channel_id=1, source_target_pairs={{0,1},{2,3},{4,5},{6,7},{8,9},{10,11},{12,13},{14,15},{1,0},{3,2},... | collective-permute-start | bytes 1179656 | tf_op jit(solution)/shard_map/ppermute | solution.py:458
  90.4 1.0 copy-start.6
  92.8 36.2 %all-to-all-start = ((f32[64,16,128]{2,1,0:T(8,128)}), f32[64,16,128]{2,1,0:T(8,128)S(1)}, u32[]{:S(2)}, u32[]{:S(2)}) async-start(f32[64,16,128]{2,1,0:T(8,128)} %pack_share.1), calls=%async_computation | async-start | bytes 1048576 | tf_op jit(solution)/shard_map/all_to_all | solution.py:464
  121.1 1.0 copy-start.2
  122.2 29.9 %collective-permute-start.6 = (f32[4,256,128]{2,1,0:T(8,128)}, f32[4,256,128]{2,1,0:T(8,128)S(1)}, u32[]{:S(2)}, u32[]{:S(2)}) collective-permute-start(f32[4,256,128]{2,1,0:T(8,128)} %get-tuple-element.33), channel_id=1, source_target_pairs={{0,1},{2,3},{4,5},{6,7},{8,9},{10,11},{12,13},{14,15},{1,0},{3,2},... | collective-permute-start | bytes 1572872 | tf_op jit(solution)/shard_map/ppermute | solution.py:458
  122.3 29.7 %collective-permute-start.7 = (f32[4,256,128]{2,1,0:T(8,128)S(1)}, f32[4,256,128]{2,1,0:T(8,128)S(1)}, u32[]{:S(2)}, u32[]{:S(2)}) collective-permute-start(f32[4,256,128]{2,1,0:T(8,128)S(1)} %get-tuple-element.34), channel_id=1, source_target_pairs={{1,2},{3,4},{5,6},{7,8},{9,10},{11,12},{13,14},{2,1},{4,3},{6,5},{... | collective-permute-start | bytes 1572872 | tf_op jit(solution)/shard_map/ppermute | solution.py:458
  148.4 2.2 %collective-permute-start.9 = (f32[64,8,128]{2,1,0:T(8,128)S(1)}, f32[64,8,128]{2,1,0:T(8,128)S(1)}, u32[]{:S(2)}, u32[]{:S(2)}) collective-permute-start(f32[64,8,128]{2,1,0:T(8,128)S(1)} %all_to_all.10.own_ref), channel_id=1, source_target_pairs={{0,1},{2,3},{4,5},{6,7},{8,9},{10,11},{12,13},{14,15},{1,0},{3,2},... | collective-permute-start | bytes 786440 | tf_op jit(solution)/shard_map/ppermute | solution.py:458
  152.0 1.2 copy-start.3

commit v3 on v2

--- a/solution.py
+++ b/solution.py
@@ -141,9 +141,9 @@
 
 def core_body(
     starts_ref, flags_ref,
-    one_ref, two_ref, ca_ref, cb_ref, ra_ref, rb_ref,
+    one_ref, ca1_ref, cb1_ref, ra1_ref, rb1_ref, two_ref, ra2_ref, rb2_ref, ca2_ref, cb2_ref,
     rolled_ref, sorted_ref, ltab_ref, rtab_ref,
-    out_ra, out_rb, out_mid, out_keep, out_send,
+    wall_a, wall_b, mid_one, slab_a, slab_b, mid_two, out_keep, out_send,
     wide, total, share, *slots,
 ):
     step = pl.program_id(0)
@@ -156,11 +156,15 @@
 
     @pl.when(step == 0)
     def _():
-        wide[:, pl.ds(row_a, half), :] = ra_ref[...]
-        wide[:, pl.ds(row_b, half), :] = rb_ref[...]
-        wide[:, half : half + win, pl.ds(lane_a, half)] = ca_ref[...]
-        wide[:, half : half + win, pl.ds(lane_b, half)] = cb_ref[...]
+        wide[0:2, pl.ds(row_a, half), :] = ra1_ref[...]
+        wide[0:2, pl.ds(row_b, half), :] = rb1_ref[...]
+        wide[0:2, half : half + win, pl.ds(lane_a, half)] = ca1_ref[...]
+        wide[0:2, half : half + win, pl.ds(lane_b, half)] = cb1_ref[...]
         wide[0:2, half : half + win, half : half + win] = one_ref[...]
+        wide[2:4, 0 : 2 * win, pl.ds(lane_a, half)] = ca2_ref[...]
+        wide[2:4, 0 : 2 * win, pl.ds(lane_b, half)] = cb2_ref[...]
+        wide[2:4, pl.ds(row_a, half), half : half + win] = ra2_ref[...]
+        wide[2:4, pl.ds(row_b, half), half : half + win] = rb2_ref[...]
         wide[2:4, half : half + win, half : half + win] = two_ref[...]
         total[...] = jnp.zeros_like(total)
         share[...] = jnp.zeros_like(share)
@@ -329,9 +333,12 @@
 
     @pl.when(step == positions // at_once - 1)
     def _():
-        out_ra[...] = total[:, pl.ds(row_a, half), :]
-        out_rb[...] = total[:, pl.ds(row_b, half), :]
-        out_mid[...] = total[:, half : half + win, :]
+        wall_a[...] = total[0:2, 0 : 2 * win, pl.ds(lane_a, half)]
+        wall_b[...] = total[0:2, 0 : 2 * win, pl.ds(lane_b, half)]
+        mid_one[...] = total[0:2, 0 : 2 * win, half : half + win]
+        slab_a[...] = total[2:4, pl.ds(row_a, half), :]
+        slab_b[...] = total[2:4, pl.ds(row_b, half), :]
+        mid_two[...] = total[2:4, half : half + win, :]
         out_keep[...] = share[:, pl.ds(pl.multiple_of(col_odd * half, half), half), :]
         out_send[...] = share[:, pl.ds(pl.multiple_of((1 - col_odd) * half, half), half), :]
 
@@ -340,8 +347,9 @@
     return pl.BlockSpec(shape, lambda *ids: (0,) * len(shape))
 
 
-def core(starts, flags, one, two, ca, cb, ra, rb, rolled, ordered, ltab, rtab):
-    shapes = ((4, half, 2 * win), (4, half, 2 * win), (4, win, 2 * win), (3, half, win), (3, half, win))
+def core(starts, flags, pieces, rolled, ordered, ltab, rtab):
+    wall, slab, share = (2, 2 * win, half), (2, half, 2 * win), (3, half, win)
+    shapes = (wall, wall, (2, 2 * win, win), slab, slab, (2, win, 2 * win), share, share)
     slot = [
         pltpu.VMEM((2, 3 * win, win), bf16),
         pltpu.VMEM((2, win, 3 * win), bf16),
@@ -356,8 +364,7 @@
             num_scalar_prefetch=2,
             grid=(positions // at_once,),
             in_specs=[
-                whole(2, win, win), whole(2, win, win), whole(4, win, half), whole(4, win, half),
-                whole(4, half, 2 * win), whole(4, half, 2 * win),
+                *(whole(*piece.shape) for piece in pieces),
                 pl.BlockSpec((at_once, 2, win, win), lambda j, *prefetched: (j, 0, 0, 0)),
                 pl.BlockSpec((at_once, win, win), lambda j, *prefetched: (j, 0, 0)),
                 whole(8, win, 3 * win), whole(8, 3 * win, win),
@@ -372,7 +379,7 @@
         compiler_params=pltpu.CompilerParams(vmem_limit_bytes=60 << 20),
         cost_estimate=pl.CostEstimate(flops=48 * 2 * positions * win**3, bytes_accessed=32 << 20, transcendentals=0),
         name="core",
-    )(starts, flags, one, two, ca, cb, ra, rb, rolled, ordered, ltab, rtab)
+    )(starts, flags, *pieces, rolled, ordered, ltab, rtab)
 
 
 def small_kernel(kernel, name, flags, inputs, shapes):
@@ -396,23 +403,31 @@
     return pl.ds(pl.multiple_of(choice * half, half), half)
 
 
-def pack_columns(flags_ref, one_ref, two_ref, a_ref, b_ref):
-    odd = flags_ref[1]
-    for out, lanes in ((a_ref, half_at(1 - odd)), (b_ref, half_at(odd))):
-        out[0:2] = one_ref[:, :, lanes]
-        out[2:4] = two_ref[:, :, lanes]
-
-
-def pack_rows(flags_ref, one_ref, two_ref, ca_ref, cb_ref, a_ref, b_ref):
+def pack_first(flags_ref, one_ref, two_ref, ca_ref, cb_ref, ra_ref, rb_ref):
+    row_odd, col_odd = flags_ref[0], flags_ref[1]
+    for out, lanes in ((ca_ref, half_at(1 - col_odd)), (cb_ref, half_at(col_odd))):
+        out[...] = one_ref[:, :, lanes]
+    for out, rows in ((ra_ref, half_at(1 - row_odd)), (rb_ref, half_at(row_odd))):
+        out[...] = two_ref[:, rows, :]
+
+
+def pack_slabs(flags_ref, one_ref, ca_ref, cb_ref, a_ref, b_ref):
     row_odd, col_odd = flags_ref[0], flags_ref[1]
     for out, rows in ((a_ref, half_at(1 - row_odd)), (b_ref, half_at(row_odd))):
-        out[0:2, :, half : half + win] = one_ref[:, rows, :]
-        out[2:4, :, half : half + win] = two_ref[:, rows, :]
+        out[:, :, half : half + win] = one_ref[:, rows, :]
         out[:, :, half_at(3 * (1 - col_odd))] = ca_ref[:, rows, :]
         out[:, :, half_at(3 * col_odd)] = cb_ref[:, rows, :]
 
 
-def fold_rows(flags_ref, mid_ref, qa_ref, qb_ref, a_ref, b_ref, center_ref):
+def pack_walls(flags_ref, two_ref, ra_ref, rb_ref, a_ref, b_ref):
+    row_odd, col_odd = flags_ref[0], flags_ref[1]
+    for out, lanes in ((a_ref, half_at(1 - col_odd)), (b_ref, half_at(col_odd))):
+        out[:, half : half + win, :] = two_ref[:, :, lanes]
+        out[:, half_at(3 * (1 - row_odd)), :] = ra_ref[:, :, lanes]
+        out[:, half_at(3 * row_odd), :] = rb_ref[:, :, lanes]
+
+
+def fold_slabs(flags_ref, mid_ref, qa_ref, qb_ref, a_ref, b_ref, center_ref):
     row_odd, col_odd = flags_ref[0], flags_ref[1]
     for got, rows in ((qa_ref, half_at(1 - row_odd)), (qb_ref, half_at(row_odd))):
         center_ref[:, rows, :] = mid_ref[:, rows, half : half + win] + got[:, :, half : half + win]
@@ -420,11 +435,24 @@
             out[:, rows, :] = mid_ref[:, rows, lanes] + got[:, :, lanes]
 
 
-def fold_columns(flags_ref, center_ref, a_ref, b_ref, one_ref, two_ref):
+def fold_walls(flags_ref, mid_ref, qa_ref, qb_ref, a_ref, b_ref, center_ref):
+    row_odd, col_odd = flags_ref[0], flags_ref[1]
+    for got, lanes in ((qa_ref, half_at(1 - col_odd)), (qb_ref, half_at(col_odd))):
+        center_ref[:, :, lanes] = mid_ref[:, half : half + win, lanes] + got[:, half : half + win, :]
+        for out, rows in ((a_ref, half_at(3 * (1 - row_odd))), (b_ref, half_at(3 * row_odd))):
+            out[:, :, lanes] = mid_ref[:, rows, lanes] + got[:, rows, :]
+
+
+def fold_columns(flags_ref, center_ref, a_ref, b_ref, out_ref):
     odd = flags_ref[1]
     for got, lanes in ((a_ref, half_at(1 - odd)), (b_ref, half_at(odd))):
-        one_ref[:, :, lanes] = center_ref[0:2, :, lanes] + got[0:2]
-        two_ref[:, :, lanes] = center_ref[2:4, :, lanes] + got[2:4]
+        out_ref[:, :, lanes] = center_ref[:, :, lanes] + got[...]
+
+
+def fold_rows(flags_ref, center_ref, a_ref, b_ref, out_ref):
+    odd = flags_ref[0]
+    for got, rows in ((a_ref, half_at(1 - odd)), (b_ref, half_at(odd))):
+        out_ref[:, rows, :] = center_ref[:, rows, :] + got[...]
 
 
 def pack_share(flags_ref, keep_ref, got_ref, out_ref):
@@ -467,24 +495,29 @@
 def body(object_one, object_two, probe, scan_pos, pattern_index, measured):
     starts = scan_pos[0, 0]
     flags = jnp.stack([lax.axis_index("row") % 2, lax.axis_index("col") % 2]).astype(jnp.int32)
-    side, slab = (4, win, half), (4, half, 2 * win)
-    ca, cb = small_kernel(pack_columns, "pack_columns", flags, (object_one, object_two), (side, side))
-    ca, cb = swapped(ca, "col", 0), swapped(cb, "col", 1)
-    ra, rb = small_kernel(pack_rows, "pack_rows", flags, (object_one, object_two, ca, cb), (slab, slab))
-    ra, rb = swapped(ra, "row", 0), swapped(rb, "row", 1)
+    side, edge, wall, slab, tile = (2, win, half), (2, half, win), (2, 2 * win, half), (2, half, 2 * win), (2, win, win)
+    first = small_kernel(pack_first, "pack_first", flags, (object_one, object_two), (side, side, edge, edge))
+    ca1, cb1 = swapped(first[0], "col", 0), swapped(first[1], "col", 1)
+    ra2, rb2 = swapped(first[2], "row", 0), swapped(first[3], "row", 1)
+    ra1, rb1 = small_kernel(pack_slabs, "pack_slabs", flags, (object_one, ca1, cb1), (slab, slab))
+    ra1, rb1 = swapped(ra1, "row", 0), swapped(rb1, "row", 1)
+    ca2, cb2 = small_kernel(pack_walls, "pack_walls", flags, (object_two, ra2, rb2), (wall, wall))
+    ca2, cb2 = swapped(ca2, "col", 0), swapped(cb2, "col", 1)
     ordered, rolled, ltab, rtab = prepare(pattern_index[0, 0], starts, measured[0, 0], probe)
-    out_ra, out_rb, mid, keep, send = core(
-        starts, flags, object_one, object_two, ca, cb, ra, rb, rolled, ordered, ltab, rtab
-    )
+    pieces = (object_one, ca1, cb1, ra1, rb1, object_two, ra2, rb2, ca2, cb2)
+    wa, wb, mid_one, sa, sb, mid_two, keep, send = core(starts, flags, pieces, rolled, ordered, ltab, rtab)
     share = small_kernel(pack_share, "pack_share", flags, (keep, swapped(send, "col", 0)), ((64, 16, half),))[0]
-    qa, qb = swapped(out_ra, "row", 0), swapped(out_rb, "row", 1)
-    fa, fb, center = small_kernel(fold_rows, "fold_rows", flags, (mid, qa, qb), (side, side, (4, win, win)))
-    ga, gb = swapped(fa, "col", 0), swapped(fb, "col", 1)
+    sa, sb = swapped(sa, "row", 0), swapped(sb, "row", 1)
+    wa, wb = swapped(wa, "col", 0), swapped(wb, "col", 1)
+    ga, gb, center_one = small_kernel(fold_walls, "fold_walls", flags, (mid_one, wa, wb), (edge, edge, tile))
+    ga, gb = swapped(ga, "row", 0), swapped(gb, "row", 1)
+    ha, hb, center_two = small_kernel(fold_slabs, "fold_slabs", flags, (mid_two, sa, sb), (side, side, tile))
+    ha, hb = swapped(ha, "col", 0), swapped(hb, "col", 1)
     step = small_kernel(take_step, "take_step", flags, (exchanged(share),), ((64, 8, half),))[0]
     step = exchanged(step)
-    tile_shape = (2, win, win)
-    grad_one, grad_two = small_kernel(fold_columns, "fold_columns", flags, (center, ga, gb), (tile_shape, tile_shape))
-    probe_step = small_kernel(join_step, "join_step", flags, (step, swapped(step, "col", 0)), (tile_shape,))[0]
+    grad_one = small_kernel(fold_rows, "fold_rows", flags, (center_one, ga, gb), (tile,))[0]
+    grad_two = small_kernel(fold_columns, "fold_columns", flags, (center_two, ha, hb), (tile,))[0]
+    probe_step = small_kernel(join_step, "join_step", flags, (step, swapped(step, "col", 0)), (tile,))[0]
     return (grad_one, grad_two, probe_step)
 
 

time: 156 us -> 148 us (0.949)
  starting transfers between devices: 33.3 us -> 55.5 us
  blocking collectives: 18.8 us -> 0 us
  waiting for transfers between devices: 43.1 us -> 27 us
  Pallas kernels: 52.8 us -> 56 us
    all_to_all x1 -> x0, blocking collectives: 18.8 us -> none  [exchanged(): lax.all_to_all(parts, ('row', 'col'), 0, 0, axis_index_groups=groups, til...]
    ppermute x10 -> x18, starting transfers between devices: 22.7 us -> 40.9 us  [swapped(): return lax.ppermute(block, axis, pairs + [(j, i) for i, j in pairs])]
    ppermute x10 -> x18, waiting for transfers between devices: 43.1 us -> 25.5 us  [swapped(): return lax.ppermute(block, axis, pairs + [(j, i) for i, j in pairs])]
    all_to_all x1 -> x2, starting transfers between devices: 10.6 us -> 14.6 us  [exchanged(): lax.all_to_all(parts, ('row', 'col'), 0, 0, axis_index_groups=groups, til...]
    pallas_call x7 -> x10, Pallas kernels: 10.8 us -> 13.8 us  [small_kernel(): pl.pallas_call(kernel, out_shape=[jax.ShapeDtypeStruct(shape, f32) for sh...]
    unnamed x20 -> x32, local copies, waits for them, and re-layouts: 5.34 us -> 6.33 us
  transfers between devices with their start and end apart: 11 -> 20, of which waited for: 7 -> 8; matrix products, arithmetic and copies ran while one was open for 0% -> 0% of each run, Pallas kernels for 11% -> 15%
where the time goes in v3:
time: 148 us; the launch traced here: 147 us
  Pallas kernels  56 us (38%)
  starting transfers between devices  55.5 us (38%)
  waiting for transfers between devices  27 us (18%)
  local copies, waits for them, and re-layouts  7 us (5%)
    ppermute x18, starting transfers between devices, swapped(): return lax.ppermute(block, axis, pairs + [(j, i) for i, j in pairs])  40.9 us
    pallas_call x1, Pallas kernels, core(): pl.pallas_call(core_body, out_shape=[jax.ShapeDtypeStruct(shape, f32) for...  31.2 us
    ppermute x18, waiting for transfers between devices, swapped(): return lax.ppermute(block, axis, pairs + [(j, i) for i, j in pairs])  25.5 us
    all_to_all x2, starting transfers between devices, exchanged(): lax.all_to_all(parts, ('row', 'col'), 0, 0, axis_index_groups=groups, til...  14.6 us
    pallas_call x10, Pallas kernels, small_kernel(): pl.pallas_call(kernel, out_shape=[jax.ShapeDtypeStruct(shape, f32) for sh...  13.8 us
    pallas_call x1, Pallas kernels, prepare(): pl.pallas_call(prepare_body, out_shape=(jax.ShapeDtypeStruct((positions,...  11 us
    unnamed x32, local copies, waits for them, and re-layouts  6.33 us
  transfers between devices with their start and end apart: 20, of which 8 were waited for; matrix products, arithmetic and copies ran while one was open for 0% of the time, Pallas kernels for 15%

profile of v3, /device:TPU:7, one launch (start us, length us, event | category | flops | bytes accessed | tf_op | source)
XLA Modules:
  0.0 146.6 jit_solution(4136922646967095223)
XLA Ops:
  3.4 1.4 collective-permute-start.4
  4.8 4.6 %collective-permute-start.5 = (f32[2,128,256]{2,1,0:T(8,128)S(1)}, f32[2,128,256]{2,1,0:T(8,128)S(1)}, u32[]{:S(2)}, u32[]{:S(2)}) collective-permute-start(f32[2,128,256]{2,1,0:T(8,128)S(1)} %get-tuple-element.34), channel_id=1, source_target_pairs={{16,32},{48,64},{80,96},{32,16},{64,48},{96,80},{17,33},{49,65},{8... | collective-permute-start | bytes 786440 | tf_op jit(solution)/shard_map/ppermute | solution.py:486
  9.5 1.3 collective-permute-start
  10.8 2.8 %collective-permute-start.1 = (f32[2,256,128]{2,1,0:T(8,128)S(1)}, f32[2,256,128]{2,1,0:T(8,128)S(1)}, u32[]{:S(2)}, u32[]{:S(2)}) collective-permute-start(f32[2,256,128]{2,1,0:T(8,128)S(1)} %get-tuple-element.30), channel_id=1, source_target_pairs={{1,2},{3,4},{5,6},{7,8},{9,10},{11,12},{13,14},{2,1},{4,3},{6,5},{... | collective-permute-start | bytes 786440 | tf_op jit(solution)/shard_map/ppermute | solution.py:486
  13.6 3.6 %collective-permute-done.5.rb_ref.rb2_ref = f32[2,128,256]{2,1,0:T(8,128)S(1)} collective-permute-done((f32[2,128,256]{2,1,0:T(8,128)S(1)}, f32[2,128,256]{2,1,0:T(8,128)S(1)}, u32[]{:S(2)}, u32[]{:S(2)}) %collective-permute-start.5) | collective-permute-done | bytes 262176 | tf_op jit(solution)/shard_map/ppermute | solution.py:486
  18.9 1.9 %collective-permute-start.6 = (f32[2,512,128]{2,1,0:T(8,128)S(1)}, f32[2,512,128]{2,1,0:T(8,128)}, u32[]{:S(2)}, u32[]{:S(2)}) collective-permute-start(f32[2,512,128]{2,1,0:T(8,128)S(1)} %get-tuple-element.35), channel_id=1, source_target_pairs={{0,1},{2,3},{4,5},{6,7},{8,9},{10,11},{12,13},{14,15},{1,0},{3,2},... | collective-permute-start | bytes 1572872 | tf_op jit(solution)/shard_map/ppermute | solution.py:486
  20.8 5.1 %collective-permute-start.7 = (f32[2,512,128]{2,1,0:T(8,128)S(1)}, f32[2,512,128]{2,1,0:T(8,128)}, u32[]{:S(2)}, u32[]{:S(2)}) collective-permute-start(f32[2,512,128]{2,1,0:T(8,128)S(1)} %get-tuple-element.36), channel_id=1, source_target_pairs={{1,2},{3,4},{5,6},{7,8},{9,10},{11,12},{13,14},{2,1},{4,3},{6,5},{... | collective-permute-start | bytes 1572872 | tf_op jit(solution)/shard_map/ppermute | solution.py:486
  25.9 1.1 copy-done.1
  27.8 3.6 %collective-permute-start.3 = (f32[2,128,512]{2,1,0:T(8,128)S(1)}, f32[2,128,512]{2,1,0:T(8,128)}, u32[]{:S(2)}, u32[]{:S(2)}) collective-permute-start(f32[2,128,512]{2,1,0:T(8,128)S(1)} %get-tuple-element.32), channel_id=1, source_target_pairs={{16,32},{48,64},{80,96},{32,16},{64,48},{96,80},{17,33},{49,65},{8... | collective-permute-start | bytes 1572872 | tf_op jit(solution)/shard_map/ppermute | solution.py:486
  32.1 11.0 %prepare.1 = (f32[8,256,256]{2,1,0:T(8,128)}, f32[8,2,256,256]{3,2,1,0:T(8,128)}, bf16[8,256,768]{2,1,0:T(8,128)(2,1)}, bf16[8,768,256]{2,1,0:T(8,128)(2,1)}) custom-call(s32[8]{0:T(128)} %bitcast.7, s32[8,2]{1,0:T(8,128)} %copy.12.starts_ref, f32[8,256,256]{2,1,0:T(8,128)} %bitcast.6, f32[2,256,256]{2,1,0:T(8,128)} %probe_ref.1, ...), custom_call_target="tpu_custom_call" | custom-call | flops 1610612736 | bytes 16777216 | tf_op jit(solution)/shard_map/prepare/pallas_call | solution.py:87
  43.3 7.3 %collective-permute-done.3.rb1_ref = f32[2,128,512]{2,1,0:T(8,128)} collective-permute-done((f32[2,128,512]{2,1,0:T(8,128)S(1)}, f32[2,128,512]{2,1,0:T(8,128)}, u32[]{:S(2)}, u32[]{:S(2)}) %collective-permute-start.3) | collective-permute-done | bytes 524320 | tf_op jit(solution)/shard_map/ppermute | solution.py:486
  50.6 31.2 %core.1 = (f32[2,512,128]{2,1,0:T(8,128)}, f32[2,512,128]{2,1,0:T(8,128)}, f32[2,512,256]{2,1,0:T(8,128)}, f32[2,128,512]{2,1,0:T(8,128)}, f32[2,128,512]{2,1,0:...) custom-call(s32[8,2]{1,0:T(8,128)} %copy.12.starts_ref, s32[2]{0:T(128)} %copy-done.13, ...), custom_call_target="tpu_custom_call" | custom-call | flops 12884901888 | bytes 33554432 | tf_op jit(solution)/shard_map/core/pallas_call | solution.py:360
  82.0 1.8 %collective-permute-done.16.got_ref = f32[3,128,256]{2,1,0:T(8,128)S(1)} collective-permute-done((f32[3,128,256]{2,1,0:T(8,128)}, f32[3,128,256]{2,1,0:T(8,128)S(1)}, u32[]{:S(2)}, u32[]{:S(2)}) %collective-permute-start.16) | collective-permute-done | bytes 393248 | tf_op jit(solution)/shard_map/ppermute | solution.py:486
  84.8 1.4 pack_share.1
  86.2 8.8 %all-to-all-start = ((f32[64,16,128]{2,1,0:T(8,128)}), f32[64,16,128]{2,1,0:T(8,128)S(1)}, u32[]{:S(2)}, u32[]{:S(2)}) async-start(f32[64,16,128]{2,1,0:T(8,128)} %pack_share.1), calls=%async_computation | async-start | bytes 1048576 | tf_op jit(solution)/shard_map/all_to_all | solution.py:492
  95.9 3.3 %collective-permute-start.9 = (f32[2,512,128]{2,1,0:T(8,128)}, f32[2,512,128]{2,1,0:T(8,128)}, u32[]{:S(2)}, u32[]{:S(2)}) collective-permute-start(f32[2,512,128]{2,1,0:T(8,128)} %get-tuple-element.43), channel_id=1, source_target_pairs={{1,2},{3,4},{5,6},{7,8},{9,10},{11,12},{13,14},{2,1},{4,3},{6,5},{... | collective-permute-start | bytes 1572872 | tf_op jit(solution)/shard_map/ppermute | solution.py:486
  99.2 1.3 collective-permute-start.12
  100.5 4.1 %collective-permute-start.13 = (f32[2,128,512]{2,1,0:T(8,128)}, f32[2,128,512]{2,1,0:T(8,128)}, u32[]{:S(2)}, u32[]{:S(2)}) collective-permute-start(f32[2,128,512]{2,1,0:T(8,128)} %get-tuple-element.49), channel_id=1, source_target_pairs={{16,32},{48,64},{80,96},{32,16},{64,48},{96,80},{17,33},{49,65},{8... | collective-permute-start | bytes 1572872 | tf_op jit(solution)/shard_map/ppermute | solution.py:486
  104.6 1.4 all-to-all-done.parts_ref
  106.1 1.3 take_step.1
  107.4 5.9 %all-to-all-start.1 = ((f32[64,8,128]{2,1,0:T(8,128)}), f32[64,8,128]{2,1,0:T(8,128)S(1)}, u32[]{:S(2)}, u32[]{:S(2)}) async-start(f32[64,8,128]{2,1,0:T(8,128)} %take_step.1), calls=%async_computation.1 | async-start | bytes 524288 | tf_op jit(solution)/shard_map/all_to_all | solution.py:492
  113.3 1.9 %collective-permute-done.9.qb_ref = f32[2,512,128]{2,1,0:T(8,128)} collective-permute-done((f32[2,512,128]{2,1,0:T(8,128)}, f32[2,512,128]{2,1,0:T(8,128)}, u32[]{:S(2)}, u32[]{:S(2)}) %collective-permute-start.9) | collective-permute-done | bytes 524320 | tf_op jit(solution)/shard_map/ppermute | solution.py:486
  115.2 2.6 %fold_walls.1 = (f32[2,128,256]{2,1,0:T(8,128)}, f32[2,128,256]{2,1,0:T(8,128)S(1)}, f32[2,256,256]{2,1,0:T(8,128)S(1)}) custom-call(s32[2]{0:T(128)S(1)} %copy-done.14, f32[2,512,256]{2,1,0:T(8,128)S(1)} %copy-done.5, f32[2,512,128]{2,1,0:T(8,128)} %collective-permute-done.8.qa_ref, f32[2,512,128]{2,1,0:T(8,128)} %collective-permute-done.9.qb_ref), custom_call_target="tpu_custom_call" | custom-call | flops 786432 | bytes 3145728 | tf_op jit(solution)/shard_map/fold_walls/pallas_call | solution.py:387
  118.0 4.6 %collective-permute-start.11 = (f32[2,128,256]{2,1,0:T(8,128)S(1)}, f32[2,128,256]{2,1,0:T(8,128)S(1)}, u32[]{:S(2)}, u32[]{:S(2)}) collective-permute-start(f32[2,128,256]{2,1,0:T(8,128)S(1)} %get-tuple-element.46), channel_id=1, source_target_pairs={{16,32},{48,64},{80,96},{32,16},{64,48},{96,80},{17,33},{49,65},{8... | collective-permute-start | bytes 786440 | tf_op jit(solution)/shard_map/ppermute | solution.py:486
  122.7 5.4 %collective-permute-done.13.qb_ref = f32[2,128,512]{2,1,0:T(8,128)} collective-permute-done((f32[2,128,512]{2,1,0:T(8,128)}, f32[2,128,512]{2,1,0:T(8,128)}, u32[]{:S(2)}, u32[]{:S(2)}) %collective-permute-start.13) | collective-permute-done | bytes 524320 | tf_op jit(solution)/shard_map/ppermute | solution.py:486
  128.1 2.4 %fold_slabs.1 = (f32[2,256,128]{2,1,0:T(8,128)}, f32[2,256,128]{2,1,0:T(8,128)S(1)}, f32[2,256,256]{2,1,0:T(8,128)S(1)}) custom-call(s32[2]{0:T(128)S(1)} %copy-done.14, f32[2,256,512]{2,1,0:T(8,128)S(1)} %copy-done.4, f32[2,128,512]{2,1,0:T(8,128)S(1)} %collective-permute-done.12.qa_ref, f32[2,128,512]{2,1,0:T(8,128)} %collective-permute-done.13.qb_ref), custom_call_target="tpu_custom_call" | custom-call | flops 786432 | bytes 3145728 | tf_op jit(solution)/shard_map/fold_slabs/pallas_call | solution.py:387
  130.5 2.5 %collective-permute-start.14 = (f32[2,256,128]{2,1,0:T(8,128)}, f32[2,256,128]{2,1,0:T(8,128)S(1)}, u32[]{:S(2)}, u32[]{:S(2)}) collective-permute-start(f32[2,256,128]{2,1,0:T(8,128)} %get-tuple-element.51), channel_id=1, source_target_pairs={{0,1},{2,3},{4,5},{6,7},{8,9},{10,11},{12,13},{14,15},{1,0},{3,2},... | collective-permute-start | bytes 786440 | tf_op jit(solution)/shard_map/ppermute | solution.py:486
  133.0 2.8 %collective-permute-start.15 = (f32[2,256,128]{2,1,0:T(8,128)S(1)}, f32[2,256,128]{2,1,0:T(8,128)S(1)}, u32[]{:S(2)}, u32[]{:S(2)}) collective-permute-start(f32[2,256,128]{2,1,0:T(8,128)S(1)} %get-tuple-element.52), channel_id=1, source_target_pairs={{1,2},{3,4},{5,6},{7,8},{9,10},{11,12},{13,14},{2,1},{4,3},{6,5},{... | collective-permute-start | bytes 786440 | tf_op jit(solution)/shard_map/ppermute | solution.py:486
  137.5 1.4 fold_rows.1
  138.9 4.9 %collective-permute-done.15.b_ref = f32[2,256,128]{2,1,0:T(8,128)S(1)} collective-permute-done((f32[2,256,128]{2,1,0:T(8,128)S(1)}, f32[2,256,128]{2,1,0:T(8,128)S(1)}, u32[]{:S(2)}, u32[]{:S(2)}) %collective-permute-start.15) | collective-permute-done | bytes 262176 | tf_op jit(solution)/shard_map/ppermute | solution.py:486
  143.8 1.4 fold_columns.1
  145.2 1.4 join_step.1
  (54 shorter events, 9.9 us)
Async XLA Ops:
  0.6 30.8 %copy-start.15 = (s32[1,1,8,2]{2,3,1,0:T(2,128)S(1)}, s32[1,1,8,2]{2,3,1,0:T(2,128)}, u32[]{:S(2)}) copy-start(s32[1,1,8,2]{2,3,1,0:T(2,128)} %param.11) | copy-start | bytes 196
  0.7 1.0 copy-start
  2.8 40.4 %copy-start.13 = (s32[2]{0:T(128)}, s32[2]{0:T(128)S(1)}, u32[]{:S(2)}) copy-start(s32[2]{0:T(128)S(1)} %pad_add_fusion.flags_ref) | copy-start | bytes 28
  3.4 10.2 %collective-permute-start.4 = (f32[2,128,256]{2,1,0:T(8,128)S(1)}, f32[2,128,256]{2,1,0:T(8,128)S(1)}, u32[]{:S(2)}, u32[]{:S(2)}) collective-permute-start(f32[2,128,256]{2,1,0:T(8,128)S(1)} %get-tuple-element.33), channel_id=1, source_target_pairs={{0,16},{32,48},{64,80},{96,112},{16,0},{48,32},{80,64},{112,96},{1... | collective-permute-start | bytes 786440 | tf_op jit(solution)/shard_map/ppermute | solution.py:486
  4.8 12.4 %collective-permute-start.5 = (f32[2,128,256]{2,1,0:T(8,128)S(1)}, f32[2,128,256]{2,1,0:T(8,128)S(1)}, u32[]{:S(2)}, u32[]{:S(2)}) collective-permute-start(f32[2,128,256]{2,1,0:T(8,128)S(1)} %get-tuple-element.34), channel_id=1, source_target_pairs={{16,32},{48,64},{80,96},{32,16},{64,48},{96,80},{17,33},{49,65},{8... | collective-permute-start | bytes 786440 | tf_op jit(solution)/shard_map/ppermute | solution.py:486
  9.5 16.4 %collective-permute-start = (f32[2,256,128]{2,1,0:T(8,128)S(1)}, f32[2,256,128]{2,1,0:T(8,128)S(1)}, u32[]{:S(2)}, u32[]{:S(2)}) collective-permute-start(f32[2,256,128]{2,1,0:T(8,128)S(1)} %get-tuple-element.29), channel_id=1, source_target_pairs={{0,1},{2,3},{4,5},{6,7},{8,9},{10,11},{12,13},{14,15},{1,0},{3,2},... | collective-permute-start | bytes 786440 | tf_op jit(solution)/shard_map/ppermute | solution.py:486
  10.8 15.2 %collective-permute-start.1 = (f32[2,256,128]{2,1,0:T(8,128)S(1)}, f32[2,256,128]{2,1,0:T(8,128)S(1)}, u32[]{:S(2)}, u32[]{:S(2)}) collective-permute-start(f32[2,256,128]{2,1,0:T(8,128)S(1)} %get-tuple-element.30), channel_id=1, source_target_pairs={{1,2},{3,4},{5,6},{7,8},{9,10},{11,12},{13,14},{2,1},{4,3},{6,5},{... | collective-permute-start | bytes 786440 | tf_op jit(solution)/shard_map/ppermute | solution.py:486
  13.6 29.6 %copy-start.9 = (f32[2,128,256]{2,1,0:T(8,128)}, f32[2,128,256]{2,1,0:T(8,128)S(1)}, u32[]{:S(2)}) copy-start(f32[2,128,256]{2,1,0:T(8,128)S(1)} %collective-permute-done.4.ra_ref.ra2_ref) | copy-start | bytes 786436
  18.3 24.9 %copy-start.10 = (f32[2,128,256]{2,1,0:T(8,128)}, f32[2,128,256]{2,1,0:T(8,128)S(1)}, u32[]{:S(2)}) copy-start(f32[2,128,256]{2,1,0:T(8,128)S(1)} %collective-permute-done.5.rb_ref.rb2_ref) | copy-start | bytes 786436
  18.9 24.3 %collective-permute-start.6 = (f32[2,512,128]{2,1,0:T(8,128)S(1)}, f32[2,512,128]{2,1,0:T(8,128)}, u32[]{:S(2)}, u32[]{:S(2)}) collective-permute-start(f32[2,512,128]{2,1,0:T(8,128)S(1)} %get-tuple-element.35), channel_id=1, source_target_pairs={{0,1},{2,3},{4,5},{6,7},{8,9},{10,11},{12,13},{14,15},{1,0},{3,2},... | collective-permute-start | bytes 1572872 | tf_op jit(solution)/shard_map/ppermute | solution.py:486
  20.8 22.5 %collective-permute-start.7 = (f32[2,512,128]{2,1,0:T(8,128)S(1)}, f32[2,512,128]{2,1,0:T(8,128)}, u32[]{:S(2)}, u32[]{:S(2)}) collective-permute-start(f32[2,512,128]{2,1,0:T(8,128)S(1)} %get-tuple-element.36), channel_id=1, source_target_pairs={{1,2},{3,4},{5,6},{7,8},{9,10},{11,12},{13,14},{2,1},{4,3},{6,5},{... | collective-permute-start | bytes 1572872 | tf_op jit(solution)/shard_map/ppermute | solution.py:486
  25.9 17.3 %copy-start.11 = (f32[2,256,128]{2,1,0:T(8,128)}, f32[2,256,128]{2,1,0:T(8,128)S(1)}, u32[]{:S(2)}) copy-start(f32[2,256,128]{2,1,0:T(8,128)S(1)} %collective-permute-done.ca_ref.ca1_ref) | copy-start | bytes 786436
  25.9 1.1 copy-start.1
  27.1 16.1 %copy-start.12 = (f32[2,256,128]{2,1,0:T(8,128)}, f32[2,256,128]{2,1,0:T(8,128)S(1)}, u32[]{:S(2)}) copy-start(f32[2,256,128]{2,1,0:T(8,128)S(1)} %collective-permute-done.1.cb_ref.cb1_ref) | copy-start | bytes 786436
  27.7 15.5 %collective-permute-start.2 = (f32[2,128,512]{2,1,0:T(8,128)S(1)}, f32[2,128,512]{2,1,0:T(8,128)}, u32[]{:S(2)}, u32[]{:S(2)}) collective-permute-start(f32[2,128,512]{2,1,0:T(8,128)S(1)} %get-tuple-element.31), channel_id=1, source_target_pairs={{0,16},{32,48},{64,80},{96,112},{16,0},{48,32},{80,64},{112,96},{1... | collective-permute-start | bytes 1572872 | tf_op jit(solution)/shard_map/ppermute | solution.py:486
  27.8 22.7 %collective-permute-start.3 = (f32[2,128,512]{2,1,0:T(8,128)S(1)}, f32[2,128,512]{2,1,0:T(8,128)}, u32[]{:S(2)}, u32[]{:S(2)}) collective-permute-start(f32[2,128,512]{2,1,0:T(8,128)S(1)} %get-tuple-element.32), channel_id=1, source_target_pairs={{16,32},{48,64},{80,96},{32,16},{64,48},{96,80},{17,33},{49,65},{8... | collective-permute-start | bytes 1572872 | tf_op jit(solution)/shard_map/ppermute | solution.py:486
  50.6 33.2 %copy-start.14 = (s32[2]{0:T(128)S(1)}, s32[2]{0:T(128)}, u32[]{:S(2)}) copy-start(s32[2]{0:T(128)} %copy-done.13) | copy-start | bytes 28
  81.8 33.5 %copy-start.5 = (f32[2,512,256]{2,1,0:T(8,128)S(1)}, f32[2,512,256]{2,1,0:T(8,128)}, u32[]{:S(2)}) copy-start(f32[2,512,256]{2,1,0:T(8,128)} %get-tuple-element.41.mid_ref) | copy-start | bytes 3145732
  81.8 46.4 %copy-start.4 = (f32[2,256,512]{2,1,0:T(8,128)S(1)}, f32[2,256,512]{2,1,0:T(8,128)}, u32[]{:S(2)}) copy-start(f32[2,256,512]{2,1,0:T(8,128)} %get-tuple-element.47.mid_ref) | copy-start | bytes 3145732
  81.8 2.0 %collective-permute-start.16 = (f32[3,128,256]{2,1,0:T(8,128)}, f32[3,128,256]{2,1,0:T(8,128)S(1)}, u32[]{:S(2)}, u32[]{:S(2)}) collective-permute-start(f32[3,128,256]{2,1,0:T(8,128)} %get-tuple-element.54), channel_id=1, source_target_pairs={{0,1},{2,3},{4,5},{6,7},{8,9},{10,11},{12,13},{14,15},{1,0},{3,2},... | collective-permute-start | bytes 1179656 | tf_op jit(solution)/shard_map/ppermute | solution.py:486
  86.2 19.9 %all-to-all-start = ((f32[64,16,128]{2,1,0:T(8,128)}), f32[64,16,128]{2,1,0:T(8,128)S(1)}, u32[]{:S(2)}, u32[]{:S(2)}) async-start(f32[64,16,128]{2,1,0:T(8,128)} %pack_share.1), calls=%async_computation | async-start | bytes 1048576 | tf_op jit(solution)/shard_map/all_to_all | solution.py:492
  95.0 18.3 %collective-permute-start.8 = (f32[2,512,128]{2,1,0:T(8,128)}, f32[2,512,128]{2,1,0:T(8,128)}, u32[]{:S(2)}, u32[]{:S(2)}) collective-permute-start(f32[2,512,128]{2,1,0:T(8,128)} %get-tuple-element.42), channel_id=1, source_target_pairs={{0,1},{2,3},{4,5},{6,7},{8,9},{10,11},{12,13},{14,15},{1,0},{3,2},... | collective-permute-start | bytes 1572872 | tf_op jit(solution)/shard_map/ppermute | solution.py:486
  95.9 19.3 %collective-permute-start.9 = (f32[2,512,128]{2,1,0:T(8,128)}, f32[2,512,128]{2,1,0:T(8,128)}, u32[]{:S(2)}, u32[]{:S(2)}) collective-permute-start(f32[2,512,128]{2,1,0:T(8,128)} %get-tuple-element.43), channel_id=1, source_target_pairs={{1,2},{3,4},{5,6},{7,8},{9,10},{11,12},{13,14},{2,1},{4,3},{6,5},{... | collective-permute-start | bytes 1572872 | tf_op jit(solution)/shard_map/ppermute | solution.py:486
  99.2 23.5 %collective-permute-start.12 = (f32[2,128,512]{2,1,0:T(8,128)}, f32[2,128,512]{2,1,0:T(8,128)S(1)}, u32[]{:S(2)}, u32[]{:S(2)}) collective-permute-start(f32[2,128,512]{2,1,0:T(8,128)} %get-tuple-element.48), channel_id=1, source_target_pairs={{0,16},{32,48},{64,80},{96,112},{16,0},{48,32},{80,64},{112,96},{1... | collective-permute-start | bytes 1572872 | tf_op jit(solution)/shard_map/ppermute | solution.py:486
  100.5 27.6 %collective-permute-start.13 = (f32[2,128,512]{2,1,0:T(8,128)}, f32[2,128,512]{2,1,0:T(8,128)}, u32[]{:S(2)}, u32[]{:S(2)}) collective-permute-start(f32[2,128,512]{2,1,0:T(8,128)} %get-tuple-element.49), channel_id=1, source_target_pairs={{16,32},{48,64},{80,96},{32,16},{64,48},{96,80},{17,33},{49,65},{8... | collective-permute-start | bytes 1572872 | tf_op jit(solution)/shard_map/ppermute | solution.py:486
  107.4 28.4 %all-to-all-start.1 = ((f32[64,8,128]{2,1,0:T(8,128)}), f32[64,8,128]{2,1,0:T(8,128)S(1)}, u32[]{:S(2)}, u32[]{:S(2)}) async-start(f32[64,8,128]{2,1,0:T(8,128)} %take_step.1), calls=%async_computation.1 | async-start | bytes 524288 | tf_op jit(solution)/shard_map/all_to_all | solution.py:492
  117.8 15.2 %copy-start.6 = (f32[2,256,256]{2,1,0:T(8,128)}, f32[2,256,256]{2,1,0:T(8,128)S(1)}, u32[]{:S(2)}) copy-start(f32[2,256,256]{2,1,0:T(8,128)S(1)} %get-tuple-element.44.center_ref) | copy-start | bytes 1572868
  117.8 18.1 %collective-permute-start.10 = (f32[2,128,256]{2,1,0:T(8,128)}, f32[2,128,256]{2,1,0:T(8,128)S(1)}, u32[]{:S(2)}, u32[]{:S(2)}) collective-permute-start(f32[2,128,256]{2,1,0:T(8,128)} %get-tuple-element.45), channel_id=1, source_target_pairs={{0,16},{32,48},{64,80},{96,112},{16,0},{48,32},{80,64},{112,96},{1... | collective-permute-start | bytes 786440 | tf_op jit(solution)/shard_map/ppermute | solution.py:486
  118.0 18.4 %collective-permute-start.11 = (f32[2,128,256]{2,1,0:T(8,128)S(1)}, f32[2,128,256]{2,1,0:T(8,128)S(1)}, u32[]{:S(2)}, u32[]{:S(2)}) collective-permute-start(f32[2,128,256]{2,1,0:T(8,128)S(1)} %get-tuple-element.46), channel_id=1, source_target_pairs={{16,32},{48,64},{80,96},{32,16},{64,48},{96,80},{17,33},{49,65},{8... | collective-permute-start | bytes 786440 | tf_op jit(solution)/shard_map/ppermute | solution.py:486
  130.5 8.3 %collective-permute-start.14 = (f32[2,256,128]{2,1,0:T(8,128)}, f32[2,256,128]{2,1,0:T(8,128)S(1)}, u32[]{:S(2)}, u32[]{:S(2)}) collective-permute-start(f32[2,256,128]{2,1,0:T(8,128)} %get-tuple-element.51), channel_id=1, source_target_pairs={{0,1},{2,3},{4,5},{6,7},{8,9},{10,11},{12,13},{14,15},{1,0},{3,2},... | collective-permute-start | bytes 786440 | tf_op jit(solution)/shard_map/ppermute | solution.py:486
  133.0 10.8 %collective-permute-start.15 = (f32[2,256,128]{2,1,0:T(8,128)S(1)}, f32[2,256,128]{2,1,0:T(8,128)S(1)}, u32[]{:S(2)}, u32[]{:S(2)}) collective-permute-start(f32[2,256,128]{2,1,0:T(8,128)S(1)} %get-tuple-element.52), channel_id=1, source_target_pairs={{1,2},{3,4},{5,6},{7,8},{9,10},{11,12},{13,14},{2,1},{4,3},{6,5},{... | collective-permute-start | bytes 786440 | tf_op jit(solution)/shard_map/ppermute | solution.py:486
  135.8 9.4 %collective-permute-start.17 = (f32[64,8,128]{2,1,0:T(8,128)S(1)}, f32[64,8,128]{2,1,0:T(8,128)S(1)}, u32[]{:S(2)}, u32[]{:S(2)}) collective-permute-start(f32[64,8,128]{2,1,0:T(8,128)S(1)} %all-to-all-done.1.own_ref), channel_id=1, source_target_pairs={{0,1},{2,3},{4,5},{6,7},{8,9},{10,11},{12,13},{14,15},{1,0},{3,2},... | collective-permute-start | bytes 786440 | tf_op jit(solution)/shard_map/ppermute | solution.py:486
  (4 other events, 4.1 us)

commit v4 on v3

v4 whole, which is shorter than its diff:
```python
import math

import jax
import jax.numpy as jnp
import ml_dtypes
import numpy as np
from jax import lax
from jax.experimental import pallas as pl
from jax.experimental.pallas import tpu as pltpu
from jax.sharding import PartitionSpec as P

phase_rate = 0.002
win = 256
half = 128
positions = 8
R = 16
at_once = 2
f32 = jnp.float32
bf16 = jnp.bfloat16


def real_form(table):
    return np.block([[table.real, table.imag], [-table.imag, table.real]])


def split_table(table):
    high = table.astype(np.float32).astype(ml_dtypes.bfloat16)
    low = (table - high.astype(np.float64)).astype(ml_dtypes.bfloat16)
    return high, low


def factor_tables():
    counter = np.arange(win)
    frequency = np.where(counter < half, counter, counter - win)
    kernel = np.exp(-1j * phase_rate * frequency.astype(np.float64) ** 2)
    response = np.fft.ifft(kernel)
    circulant = response[(counter[:, None] - counter[None, :]) % win]
    first, second = circulant[:half, :half], circulant[:half, half:]
    n, k = np.arange(half)[:, None], np.arange(half)[None, :]
    even = np.exp(-2j * np.pi * ((2 * n * k) % win) / win) / 16.0
    odd = np.exp(-2j * np.pi * ((n * (2 * k + 1)) % win) / win) / 16.0
    return [real_form(t) for t in (0.5 * (first + second), 0.5 * (first - second), even, odd)]


def table_parts():
    factors = factor_tables()
    return np.stack([np.stack(split_table(table)) for table in factors + [t.T for t in factors]])


def column_order():
    order = np.concatenate([np.arange(0, win, 2), np.arange(1, win, 2)])
    table = np.zeros((win, win), np.float32)
    table[order, np.arange(win)] = 1.0
    return table.astype(ml_dtypes.bfloat16)


def split3(value):
    high = value.astype(bf16)
    rest = value - high.astype(f32)
    middle = rest.astype(bf16)
    low = (rest - middle.astype(f32)).astype(bf16)
    return high, middle, low


steps_before = 2


def sort_body(pattern_ref, near_ref, far_ref, order_ref, sorted_ref):
    order = order_ref[...]
    many = positions // steps_before

    def one_position(spot, carry):
        pattern = pattern_ref[pl.program_id(0) * many + spot]
        for parity in range(2):
            rows = [ref[pattern, pl.ds(parity, half, stride=2), :] for ref in (near_ref, far_ref)]
            parts = split3(jnp.concatenate(rows, axis=1))
            sorted_ref[spot, parity * half : (parity + 1) * half, :] = sum(
                jnp.dot(part, order, preferred_element_type=f32) for part in parts
            )
        return carry

    lax.fori_loop(0, many, one_position, 0)


def sort_patterns(pattern, measured):
    return pl.pallas_call(
        sort_body,
        out_shape=jax.ShapeDtypeStruct((positions, win, win), f32),
        grid_spec=pltpu.PrefetchScalarGridSpec(
            num_scalar_prefetch=1,
            grid=(steps_before,),
            in_specs=[
                pl.BlockSpec((positions, win, half), lambda j, pattern: (0, 0, 0)),
                pl.BlockSpec((positions, win, half), lambda j, pattern: (0, 0, 1)),
                whole(win, win),
            ],
            out_specs=pl.BlockSpec((positions // steps_before, win, win), lambda j, pattern: (j, 0, 0)),
        ),
        cost_estimate=pl.CostEstimate(flops=2 * 3 * positions * win**3, bytes_accessed=4 << 20, transcendentals=0),
        name="sort_patterns",
    )(pattern, measured, measured, jnp.asarray(column_order()))


def prepare_body(starts_ref, probe_ref, parts_ref, rolled_ref, left_ref, right_ref):
    many = positions // steps_before

    def one_position(spot, carry):
        position = pl.program_id(0) * many + spot
        down = lax.rem(starts_ref[position, 0], 8)
        across = starts_ref[position, 1]
        kept = lax.broadcasted_iota(jnp.int32, (8, win), 0) >= down
        for plane in range(2):
            above = pltpu.roll(probe_ref[plane, win - 8 : win, :], down, axis=0)
            for row in range(0, win, 8):
                block = pltpu.roll(probe_ref[plane, row : row + 8, :], down, axis=0)
                rolled_ref[spot, plane, row : row + 8, :] = pltpu.roll(jnp.where(kept, block, above), across, axis=1)
                above = block
        for part, places in ((0, (0, 1)), (1, (2,))):
            table = parts_ref[spot, part]
            for place in places:
                left_ref[spot, :, place * win : (place + 1) * win] = table
                right_ref[spot, place * win : (place + 1) * win, :] = table
        return carry

    lax.fori_loop(0, many, one_position, 0)


def prepare(starts, probe):
    many = positions // steps_before
    return pl.pallas_call(
        prepare_body,
        out_shape=(
            jax.ShapeDtypeStruct((positions, 2, win, win), f32),
            jax.ShapeDtypeStruct((8, win, 3 * win), bf16),
            jax.ShapeDtypeStruct((8, 3 * win, win), bf16),
        ),
        grid_spec=pltpu.PrefetchScalarGridSpec(
            num_scalar_prefetch=1,
            grid=(steps_before,),
            in_specs=[
                whole(2, win, win),
                pl.BlockSpec((many, 2, win, win), lambda j, starts: (j, 0, 0, 0)),
            ],
            out_specs=[
                pl.BlockSpec((many, 2, win, win), lambda j, starts: (j, 0, 0, 0)),
                pl.BlockSpec((many, win, 3 * win), lambda j, starts: (j, 0, 0)),
                pl.BlockSpec((many, 3 * win, win), lambda j, starts: (j, 0, 0)),
            ],
        ),
        compiler_params=pltpu.CompilerParams(vmem_limit_bytes=44 << 20),
        cost_estimate=pl.CostEstimate(flops=positions * win**3, bytes_accessed=12 << 20, transcendentals=0),
        name="prepare",
    )(starts, probe, jnp.asarray(table_parts()))


def complex_mul(left_re, left_im, right_re, right_im):
    return (left_re * right_re - left_im * right_im, left_re * right_im + left_im * right_re)


def conj_mul(left_re, left_im, right_re, right_im):
    return (left_re * right_re + left_im * right_im, left_re * right_im - left_im * right_re)


def put_left(ref, side, row, value):
    high = value.astype(bf16)
    low = (value - high.astype(f32)).astype(bf16)
    size = value.shape[0]
    ref[side, row : row + size, :] = high
    ref[side, win + row : win + row + size, :] = low
    ref[side, 2 * win + row : 2 * win + row + size, :] = high


def put_right(ref, side, row, lane, value):
    high = value.astype(bf16)
    low = (value - high.astype(f32)).astype(bf16)
    size = value.shape[0]
    ref[side, row : row + size, lane : lane + half] = high
    ref[side, row : row + size, win + lane : win + lane + half] = low
    ref[side, row : row + size, 2 * win + lane : 2 * win + lane + half] = high


class Work:
    def __init__(self, starts_ref, position, wide, total, xa, xb, res):
        self.wide, self.total, self.xa, self.xb, self.res = wide, total, xa, xb, res
        a = starts_ref[position, 0]
        self.b = starts_ref[position, 1]
        self.offset = lax.rem(a, 8)
        self.base = pl.multiple_of(a - self.offset, 8)
        self.near = lax.broadcasted_iota(jnp.int32, (R, win), 1) >= self.b
        self.below = lax.broadcasted_iota(jnp.int32, (R, win), 0) >= self.offset

    def row_sets(self, row):
        first = (pl.ds(self.base + row, R), None)
        return (first,) if row else (first, (pl.ds(self.base + win, R), self.below))

    def window(self, plane, row):
        value = None
        for rows, mask in self.row_sets(row):
            block = jnp.where(self.near, self.wide[plane, rows, 0:win], self.wide[plane, rows, win : 2 * win])
            value = block if mask is None else jnp.where(mask, value, block)
        return value

    def add_window(self, plane, row, value):
        zero = jnp.zeros_like(value)
        for rows, mask in self.row_sets(row):
            part = value
            if row == 0:
                part = jnp.where(self.below, value, zero) if mask is None else jnp.where(self.below, zero, value)
            self.total[plane, rows, 0:win] += jnp.where(self.near, part, zero)
            self.total[plane, rows, win : 2 * win] += jnp.where(self.near, zero, part)

    def left_stage(self, table):
        for side in range(2):
            self.res[side] = jnp.dot(table[side], self.xa[side], preferred_element_type=f32)

    def right_stage(self, table):
        for side in range(2):
            self.res[side] = jnp.dot(self.xb[side], table[side], preferred_element_type=f32)

    def row_butterfly(self, row, upper, lower):
        for part in range(2):
            put_left(self.xa, 0, part * half + row, upper[part] + lower[part])
            put_left(self.xa, 1, part * half + row, upper[part] - lower[part])

    def lane_butterfly(self, row, field):
        for part in range(2):
            near_half, far_half = field[part][:, :half], field[part][:, half:]
            put_right(self.xb, 0, row, part * half, near_half + far_half)
            put_right(self.xb, 1, row, part * half, near_half - far_half)

    def lane_join(self, row):
        out = []
        for part in range(2):
            plus = self.res[0, row : row + R, part * half : (part + 1) * half]
            minus = self.res[1, row : row + R, part * half : (part + 1) * half]
            out.append(jnp.concatenate([plus + minus, plus - minus], axis=1))
        return out

    def row_join(self, row):
        plus = [self.res[0, part * half + row : part * half + row + R, :] for part in range(2)]
        minus = [self.res[1, part * half + row : part * half + row + R, :] for part in range(2)]
        return [p + m for p, m in zip(plus, minus)], [p - m for p, m in zip(plus, minus)]

    def rows_to_lanes(self):
        for row in range(0, half, R):
            upper, lower = self.row_join(row)
            self.lane_butterfly(row, upper)
            self.lane_butterfly(half + row, lower)

    def add_unrolled(self, target, source):
        up = jnp.where(self.offset == 0, 0, 8 - self.offset)
        across = jnp.where(self.b == 0, 0, win - self.b)
        kept = lax.broadcasted_iota(jnp.int32, (8, win), 0) < 8 - self.offset
        first = block = pltpu.roll(source[0:8, :], up, axis=0)
        for row in range(0, win, 8):
            below = pltpu.roll(source[row + 8 : row + 16, :], up, axis=0) if row + 8 < win else first
            target[row : row + 8, :] += pltpu.roll(jnp.where(kept, block, below), across, axis=1)
            block = below


def run_together(works):
    running, live = list(works), []
    while running or live:
        if running:
            live.append(running.pop(0))
        live = [w for w in live if next(w, "end") is None]


def assemble(flags_ref, wide, own_ref, ra_ref, rb_ref, ca_ref, cb_ref):
    row_odd, col_odd = flags_ref[0], flags_ref[1]
    wide[:, half_at(3 * (1 - row_odd)), half : half + win] = ra_ref[...]
    wide[:, half_at(3 * row_odd), half : half + win] = rb_ref[...]
    wide[:, 0 : 2 * win, half_at(3 * (1 - col_odd))] = ca_ref[...]
    wide[:, 0 : 2 * win, half_at(3 * col_odd)] = cb_ref[...]
    wide[:, half : half + win, half : half + win] = own_ref[...]


def give_out(flags_ref, total, wall_a, wall_b, mid):
    col_odd = flags_ref[1]
    wall_a[...] = total[:, 0 : 2 * win, half_at(3 * (1 - col_odd))]
    wall_b[...] = total[:, 0 : 2 * win, half_at(3 * col_odd)]
    mid[...] = total[:, 0 : 2 * win, half : half + win]


def propagate_body(
    starts_ref, flags_ref, own_ref, ra_ref, rb_ref, ca_ref, cb_ref, rolled_ref, left_ref, right_ref,
    phi_ref, wide, light, *slots,
):
    step = pl.program_id(0)

    @pl.when(step == 0)
    def _():
        assemble(flags_ref, wide, own_ref, ra_ref, rb_ref, ca_ref, cb_ref)
        light[...] = jnp.zeros_like(light)

    def work(slot):
        xa, xb, res, shares = slots[4 * slot : 4 * slot + 4]
        w = Work(starts_ref, at_once * step + slot, wide, None, xa, xb, res)
        for row in range(0, half, R):
            pair = []
            for at in (row, half + row):
                o_re, o_im = w.window(0, at), w.window(1, at)
                shares[0, at : at + R, :] = o_re * o_re + o_im * o_im
                probe = [rolled_ref[slot, part, at : at + R, :] for part in range(2)]
                pair.append(complex_mul(*probe, o_re, o_im))
            w.row_butterfly(row, *pair)
        yield
        w.left_stage(left_ref)
        w.add_unrolled(light, shares.at[0])
        yield
        w.rows_to_lanes()
        yield
        w.right_stage(right_ref)
        yield
        for row in range(0, win, R):
            phi_ref[slot, 0, row : row + R, :], phi_ref[slot, 1, row : row + R, :] = w.lane_join(row)
        yield

    run_together(work(slot) for slot in range(at_once))


def detect_body(
    starts_ref, flags_ref, own_ref, ra_ref, rb_ref, ca_ref, cb_ref, phi_ref, sorted_ref,
    left_ref, right_ref, left_back, right_back,
    inner_ref, wall_a, wall_b, mid, wide, total, *slots,
):
    step = pl.program_id(0)

    @pl.when(step == 0)
    def _():
        assemble(flags_ref, wide, own_ref, ra_ref, rb_ref, ca_ref, cb_ref)
        total[...] = jnp.zeros_like(total)

    def work(slot):
        xa, xb, res = slots[4 * slot : 4 * slot + 3]
        w = Work(starts_ref, at_once * step + slot, wide, total, xa, xb, res)

        def phi(row):
            return [phi_ref[slot, part, row : row + R, :] for part in range(2)]

        for row in range(0, half, R):
            pair = [complex_mul(*phi(at), w.window(0, at), w.window(1, at)) for at in (row, half + row)]
            w.row_butterfly(row, *pair)
        yield
        w.left_stage(left_ref)
        yield
        for side in range(2):
            for row in range(0, half, R):
                w.lane_butterfly(
                    side * half + row, [res[side, part * half + row : part * half + row + R, :] for part in range(2)]
                )
        yield
        w.right_stage(right_ref)
        yield
        for side in range(2):
            for row in range(0, win, R):
                far_re = res[side, row : row + R, 0:half]
                far_im = res[side, row : row + R, half:win]
                amplitude = sorted_ref[slot, row : row + R, side * half : (side + 1) * half]
                factor = 1.0 - amplitude * lax.rsqrt(far_re * far_re + far_im * far_im + 1.0)
                put_right(xb, side, row, 0, factor * far_re)
                put_right(xb, side, row, half, factor * far_im)
        yield
        w.right_stage(right_back)
        yield
        for side in range(2):
            for row in range(0, half, R):
                field = w.lane_join(side * half + row)
                for part in range(2):
                    put_left(xa, side, part * half + row, field[part])
        yield
        w.left_stage(left_back)
        yield
        for row in range(0, half, R):
            for at, back in zip((row, half + row), w.row_join(row)):
                for part, term in enumerate(conj_mul(*phi(at), *back)):
                    w.add_window(part, at, term)
                inner = conj_mul(w.window(0, at), w.window(1, at), *back)
                inner_ref[slot, 0, at : at + R, :], inner_ref[slot, 1, at : at + R, :] = inner
        yield

    run_together(work(slot) for slot in range(at_once))

    @pl.when(step == positions // at_once - 1)
    def _():
        give_out(flags_ref, total, wall_a, wall_b, mid)


def return_body(
    starts_ref, flags_ref, wide, inner_ref, rolled_ref, light, left_ref, right_ref,
    wall_a, wall_b, mid, keep, send, total, share, *slots,
):
    step = pl.program_id(0)

    @pl.when(step == 0)
    def _():
        total[...] = jnp.zeros_like(total)
        share[0:2] = jnp.zeros((2, win, win), f32)
        share[2] = light[...]

    def work(slot):
        xa, xb, res, shares = slots[4 * slot : 4 * slot + 4]
        w = Work(starts_ref, at_once * step + slot, wide, total, xa, xb, res)
        for row in range(0, half, R):
            pair = [[inner_ref[slot, part, at : at + R, :] for part in range(2)] for at in (row, half + row)]
            w.row_butterfly(row, *pair)
        yield
        w.left_stage(left_ref)
        yield
        w.rows_to_lanes()
        yield
        w.right_stage(right_ref)
        yield
        for at in range(0, win, R):
            entry = w.lane_join(at)
            probe = [rolled_ref[slot, part, at : at + R, :] for part in range(2)]
            for part, term in enumerate(conj_mul(*probe, *entry)):
                w.add_window(part, at, term)
            terms = conj_mul(w.window(0, at), w.window(1, at), *entry)
            shares[0, at : at + R, :], shares[1, at : at + R, :] = terms
        for part in range(2):
            w.add_unrolled(share.at[part], shares.at[part])
        yield

    run_together(work(slot) for slot in range(at_once))

    @pl.when(step == positions // at_once - 1)
    def _():
        give_out(flags_ref, total, wall_a, wall_b, mid)
        keep[...] = share[:, half_at(flags_ref[1]), :]
        send[...] = share[:, half_at(1 - flags_ref[1]), :]


def position_kernel(body, products, starts, flags, inputs, outputs, scratch):
    def spec(shape, kind):
        if kind == "each":
            return pl.BlockSpec((at_once,) + shape[1:], lambda j, *_: (j,) + (0,) * (len(shape) - 1))
        if kind == "whole":
            return whole(*shape)
        return pl.BlockSpec((2,) + shape[1:], lambda j, *_: (kind,) + (0,) * (len(shape) - 1))

    slot = [
        pltpu.VMEM((2, 3 * win, win), bf16),
        pltpu.VMEM((2, win, 3 * win), bf16),
        pltpu.VMEM((2, win, win), f32),
        pltpu.VMEM((2, win, win), f32),
    ]
    return pl.pallas_call(
        body,
        out_shape=[jax.ShapeDtypeStruct(shape, f32) for shape, _ in outputs],
        grid_spec=pltpu.PrefetchScalarGridSpec(
            num_scalar_prefetch=2,
            grid=(positions // at_once,),
            in_specs=[spec(x.shape, kind) for x, kind in inputs],
            out_specs=[spec(shape, kind) for shape, kind in outputs],
            scratch_shapes=scratch + slot * at_once,
        ),
        compiler_params=pltpu.CompilerParams(vmem_limit_bytes=44 << 20),
        cost_estimate=pl.CostEstimate(
            flops=products * 24 * positions * win**3, bytes_accessed=products * (8 << 20), transcendentals=0
        ),
    )(starts, flags, *(x for x, _ in inputs))


def whole(*shape):
    return pl.BlockSpec(shape, lambda *ids: (0,) * len(shape))


def small_kernel(kernel, flags, inputs, shapes):
    size = sum(x.size for x in inputs) + sum(math.prod(shape) for shape in shapes)
    return pl.pallas_call(
        kernel,
        out_shape=[jax.ShapeDtypeStruct(shape, f32) for shape in shapes],
        grid_spec=pltpu.PrefetchScalarGridSpec(
            num_scalar_prefetch=1,
            grid=(1,),
            in_specs=[whole(*x.shape) for x in inputs],
            out_specs=[whole(*shape) for shape in shapes],
        ),
        compiler_params=pltpu.CompilerParams(vmem_limit_bytes=48 << 20),
        cost_estimate=pl.CostEstimate(flops=size, bytes_accessed=4 * size, transcendentals=0),
    )(flags, *inputs)


def half_at(choice):
    return pl.ds(pl.multiple_of(choice * half, half), half)


def pack_edges(flags_ref, own_ref, a_ref, b_ref):
    row_odd = flags_ref[0]
    for out, rows in ((a_ref, half_at(1 - row_odd)), (b_ref, half_at(row_odd))):
        out[...] = own_ref[:, rows, :]


def pack_walls(flags_ref, two_ref, ra_ref, rb_ref, a_ref, b_ref):
    row_odd, col_odd = flags_ref[0], flags_ref[1]
    for out, lanes in ((a_ref, half_at(1 - col_odd)), (b_ref, half_at(col_odd))):
        out[:, half : half + win, :] = two_ref[:, :, lanes]
        out[:, half_at(3 * (1 - row_odd)), :] = ra_ref[:, :, lanes]
        out[:, half_at(3 * row_odd), :] = rb_ref[:, :, lanes]


def fold_walls(flags_ref, mid_ref, qa_ref, qb_ref, a_ref, b_ref, center_ref):
    row_odd, col_odd = flags_ref[0], flags_ref[1]
    for got, lanes in ((qa_ref, half_at(1 - col_odd)), (qb_ref, half_at(col_odd))):
        center_ref[:, :, lanes] = mid_ref[:, half : half + win, lanes] + got[:, half : half + win, :]
        for out, rows in ((a_ref, half_at(3 * (1 - row_odd))), (b_ref, half_at(3 * row_odd))):
            out[:, :, lanes] = mid_ref[:, rows, lanes] + got[:, rows, :]


def fold_rows(flags_ref, center_ref, a_ref, b_ref, out_ref):
    odd = flags_ref[0]
    for got, rows in ((a_ref, half_at(1 - odd)), (b_ref, half_at(odd))):
        out_ref[:, rows, :] = center_ref[:, rows, :] + got[...]


def pack_share(flags_ref, keep_ref, got_ref, out_ref):
    for tile in range(64):
        for plane, spot in ((tile // 32, 0), (2, 8)):
            rows = slice(tile % 32 // 2 * 8, tile % 32 // 2 * 8 + 8)
            lanes = slice(tile % 2 * half, tile % 2 * half + half)
            out_ref[tile, spot : spot + 8, :] = keep_ref[plane, rows, lanes] + got_ref[plane, rows, lanes]


def take_step(flags_ref, parts_ref, out_ref):
    total = parts_ref[0]
    for tile in range(1, 64):
        total = total + parts_ref[tile]
    step = total[0:8] * lax.rsqrt(total[8:16] + 1.0)
    for tile in range(64):
        out_ref[tile] = step


def join_step(flags_ref, own_ref, other_ref, out_ref):
    odd = flags_ref[1]
    for tile in range(64):
        row = tile % 32 // 2 * 8
        lanes = slice(tile % 2 * half, tile % 2 * half + half)
        out_ref[tile // 32, pl.ds(pl.multiple_of(odd * half + row, 8), 8), lanes] = own_ref[tile]
        out_ref[tile // 32, pl.ds(pl.multiple_of((1 - odd) * half + row, 8), 8), lanes] = other_ref[tile]


def swapped(block, axis, first):
    pairs = [(i, i + 1) for i in range(first, lax.axis_size(axis) - 1, 2)]
    return lax.ppermute(block, axis, pairs + [(j, i) for i, j in pairs])


def exchanged(parts):
    rows, cols = lax.axis_size("row"), lax.axis_size("col")
    groups = [[r * cols + c for r in range(rows) for c in range(odd, cols, 2)] for odd in range(2)]
    return lax.all_to_all(parts, ("row", "col"), 0, 0, axis_index_groups=groups, tiled=True)


def gradients(object_one, object_two, probe, scan_pos, pattern_index, measured):
    starts = scan_pos[0, 0]
    flags = jnp.stack([lax.axis_index("row") % 2, lax.axis_index("col") % 2]).astype(jnp.int32)
    edge, wall, tile = (2, half, win), (2, 2 * win, half), (2, win, win)

    def edges_of(own):
        ra, rb = small_kernel(pack_edges, flags, (own,), (edge, edge))
        return swapped(ra, "row", 0), swapped(rb, "row", 1)

    def walls_of(own, edges):
        ca, cb = small_kernel(pack_walls, flags, (own,) + edges, (wall, wall))
        return swapped(ca, "col", 0), swapped(cb, "col", 1)

    def folded(wa, wb, mid):
        wa = swapped(wa, "col", 0)
        wb = swapped(wb, "col", 1)
        ga, gb, center = small_kernel(fold_walls, flags, (mid, wa, wb), (edge, edge, tile))
        ga = swapped(ga, "row", 0)
        gb = swapped(gb, "row", 1)
        return small_kernel(fold_rows, flags, (center, ga, gb), (tile,))[0]

    edges_one, edges_two = edges_of(object_one), edges_of(object_two)
    walls_one = walls_of(object_one, edges_one)
    walls_two = walls_of(object_two, edges_two)
    ordered = sort_patterns(pattern_index[0, 0], measured[0, 0])
    rolled, ltab, rtab = prepare(starts, probe)
    stack, wide_shape = (positions, 2, win, win), (2, 2 * win + 8, 2 * win)
    parts = (wall, "whole"), (wall, "whole"), ((2, 2 * win, win), "whole")
    pieces = [(x, "whole") for x in (object_one,) + edges_one + walls_one]
    phi, wide, light = position_kernel(
        propagate_body, 1, starts, flags,
        pieces + [(rolled, "each"), (ltab, 2), (rtab, 0)],
        [(stack, "each"), (wide_shape, "whole"), ((win, win), "whole")], [],
    )
    pieces = [(x, "whole") for x in (object_two,) + edges_two + walls_two]
    inner, *two = position_kernel(
        detect_body, 2, starts, flags,
        pieces + [(phi, "each"), (ordered, "each"), (ltab, 3), (rtab, 1), (ltab, 1), (rtab, 3)],
        [(stack, "each"), *parts], [pltpu.VMEM(wide_shape, f32), pltpu.VMEM(wide_shape, f32)],
    )
    *one, keep, send = position_kernel(
        return_body, 1, starts, flags,
        [(wide, "whole"), (inner, "each"), (rolled, "each"), (light, "whole"), (ltab, 0), (rtab, 2)],
        [*parts, ((3, half, win), "whole"), ((3, half, win), "whole")],
        [pltpu.VMEM(wide_shape, f32), pltpu.VMEM((3, win, win), f32)],
    )
    share = small_kernel(pack_share, flags, (keep, swapped(send, "col", 0)), ((64, 16, half),))[0]
    grad_two = folded(*two)
    grad_one = folded(*one)
    step = small_kernel(take_step, flags, (exchanged(share),), ((64, 8, half),))[0]
    step = exchanged(step)
    probe_step = small_kernel(join_step, flags, (step, swapped(step, "col", 0)), (tile,))[0]
    return (grad_one, grad_two, probe_step)


def solution(mesh):
    placed = (
        P(None, "row", "col"),
        P(None, "row", "col"),
        P(),
        P("row", "col", None, None),
        P("row", "col", None),
        P("row", "col", None, None, None),
    )
    return jax.shard_map(
        gradients,
        mesh=mesh,
        in_specs=placed,
        out_specs=(P(None, "row", "col"), P(None, "row", "col"), P()),
        check_vma=False,
    )
```

time: 148 us -> 164 us (1.11)
  waiting for transfers between devices: 27 us -> 38.6 us
  local copies, waits for them, and re-layouts: 7 us -> 12.1 us
  starting transfers between devices: 55.5 us -> 52.9 us
  Pallas kernels: 56 us -> 58.4 us
    ppermute x18, waiting for transfers between devices: 25.5 us -> 34.8 us  [swapped(): return lax.ppermute(block, axis, pairs + [(j, i) for i, j in pairs])]
    pallas_call x1 -> x4, Pallas kernels: 31.2 us -> 38.9 us  [the longest x3 33.5 us: position_kernel(): pl.pallas_call(body, out_shape=[jax.ShapeDtypeStruct(shape, f32) for shap...]
    pallas_call x1, Pallas kernels: 11 us -> 3.86 us  [prepare(): pl.pallas_call(prepare_body, out_shape=(jax.ShapeDtypeStruct((positions,...]
    unnamed x32 -> x50, local copies, waits for them, and re-layouts: 6.33 us -> 12 us
    ppermute x18, starting transfers between devices: 40.9 us -> 38.1 us  [swapped(): return lax.ppermute(block, axis, pairs + [(j, i) for i, j in pairs])]
    all_to_all x2, waiting for transfers between devices: 1.45 us -> 3.8 us  [exchanged(): lax.all_to_all(parts, ('row', 'col'), 0, 0, axis_index_groups=groups, til...]
    pallas_call x10 -> x11, Pallas kernels: 13.8 us -> 15.7 us  [small_kernel(): pl.pallas_call(kernel, out_shape=[jax.ShapeDtypeStruct(shape, f32) for sh...]
  transfers between devices with their start and end apart: 20 -> 20, of which waited for: 8 -> 10; matrix products, arithmetic and copies ran while one was open for 0% -> 0% of each run, Pallas kernels for 15% -> 18%
where the time goes in v4:
time: 164 us; the launch traced here: 163 us
  Pallas kernels  58.4 us (36%)
  starting transfers between devices  52.9 us (32%)
  waiting for transfers between devices  38.6 us (24%)
  local copies, waits for them, and re-layouts  12.1 us (7%)
    ppermute x18, starting transfers between devices, swapped(): return lax.ppermute(block, axis, pairs + [(j, i) for i, j in pairs])  38.1 us
    ppermute x18, waiting for transfers between devices, swapped(): return lax.ppermute(block, axis, pairs + [(j, i) for i, j in pairs])  34.8 us
    pallas_call x3, Pallas kernels, position_kernel(): pl.pallas_call(body, out_shape=[jax.ShapeDtypeStruct(shape, f32) for shap...  33.5 us
    pallas_call x11, Pallas kernels, small_kernel(): pl.pallas_call(kernel, out_shape=[jax.ShapeDtypeStruct(shape, f32) for sh...  15.7 us
    all_to_all x2, starting transfers between devices, exchanged(): lax.all_to_all(parts, ('row', 'col'), 0, 0, axis_index_groups=groups, til...  14.7 us
    unnamed x50, local copies, waits for them, and re-layouts  12 us
    pallas_call x1, Pallas kernels, sort_patterns(): pl.pallas_call(sort_body, out_shape=jax.ShapeDtypeStruct((positions, win,...  5.46 us
    pallas_call x1, Pallas kernels, prepare(): pl.pallas_call(prepare_body, out_shape=(jax.ShapeDtypeStruct((positions,...  3.86 us
  transfers between devices with their start and end apart: 20, of which 10 were waited for; matrix products, arithmetic and copies ran while one was open for 0% of the time, Pallas kernels for 18%

profile of v4, /device:TPU:7, one launch (start us, length us, event | category | flops | bytes accessed | tf_op | source)
XLA Modules:
  0.0 163.0 jit_solution(2274309583278459117)
XLA Ops:
  3.7 4.6 %collective-permute-start.1 = (f32[2,128,256]{2,1,0:T(8,128)S(1)}, f32[2,128,256]{2,1,0:T(8,128)S(1)}, u32[]{:S(2)}, u32[]{:S(2)}) collective-permute-start(f32[2,128,256]{2,1,0:T(8,128)S(1)} %get-tuple-element.33), channel_id=1, source_target_pairs={{16,32},{48,64},{80,96},{32,16},{64,48},{96,80},{17,33},{49,65},{8... | collective-permute-start | bytes 786440 | tf_op jit(solution)/shard_map/ppermute | solution.py:545
  9.6 6.5 %collective-permute-done.1.rb_ref = f32[2,128,256]{2,1,0:T(8,128)S(1)} collective-permute-done((f32[2,128,256]{2,1,0:T(8,128)S(1)}, f32[2,128,256]{2,1,0:T(8,128)S(1)}, u32[]{:S(2)}, u32[]{:S(2)}) %collective-permute-start.1) | collective-permute-done | bytes 262176 | tf_op jit(solution)/shard_map/ppermute | solution.py:545
  16.1 1.6 shard_map.104
  17.8 1.8 %collective-permute-start.2 = (f32[2,512,128]{2,1,0:T(8,128)}, f32[2,512,128]{2,1,0:T(8,128)}, u32[]{:S(2)}, u32[]{:S(2)}) collective-permute-start(f32[2,512,128]{2,1,0:T(8,128)} %get-tuple-element.34), channel_id=1, source_target_pairs={{0,1},{2,3},{4,5},{6,7},{8,9},{10,11},{12,13},{14,15},{1,0},{3,2},... | collective-permute-start | bytes 1572872 | tf_op jit(solution)/shard_map/ppermute | solution.py:545
  19.6 3.7 %collective-permute-start.3 = (f32[2,512,128]{2,1,0:T(8,128)}, f32[2,512,128]{2,1,0:T(8,128)}, u32[]{:S(2)}, u32[]{:S(2)}) collective-permute-start(f32[2,512,128]{2,1,0:T(8,128)} %get-tuple-element.35), channel_id=1, source_target_pairs={{1,2},{3,4},{5,6},{7,8},{9,10},{11,12},{13,14},{2,1},{4,3},{6,5},{... | collective-permute-start | bytes 1572872 | tf_op jit(solution)/shard_map/ppermute | solution.py:545
  25.0 4.4 %collective-permute-start.5 = (f32[2,128,256]{2,1,0:T(8,128)S(1)}, f32[2,128,256]{2,1,0:T(8,128)S(1)}, u32[]{:S(2)}, u32[]{:S(2)}) collective-permute-start(f32[2,128,256]{2,1,0:T(8,128)S(1)} %get-tuple-element.41), channel_id=1, source_target_pairs={{16,32},{48,64},{80,96},{32,16},{64,48},{96,80},{17,33},{49,65},{8... | collective-permute-start | bytes 786440 | tf_op jit(solution)/shard_map/ppermute | solution.py:545
  29.4 3.3 %collective-permute-done.4.ra_ref = f32[2,128,256]{2,1,0:T(8,128)S(1)} collective-permute-done((f32[2,128,256]{2,1,0:T(8,128)S(1)}, f32[2,128,256]{2,1,0:T(8,128)S(1)}, u32[]{:S(2)}, u32[]{:S(2)}) %collective-permute-start.4) | collective-permute-done | bytes 262176 | tf_op jit(solution)/shard_map/ppermute | solution.py:545
  32.6 10.4 %collective-permute-done.5.rb_ref = f32[2,128,256]{2,1,0:T(8,128)S(1)} collective-permute-done((f32[2,128,256]{2,1,0:T(8,128)S(1)}, f32[2,128,256]{2,1,0:T(8,128)S(1)}, u32[]{:S(2)}, u32[]{:S(2)}) %collective-permute-start.5) | collective-permute-done | bytes 262176 | tf_op jit(solution)/shard_map/ppermute | solution.py:545
  43.1 1.6 shard_map.107
  44.7 3.7 %collective-permute-start.7 = (f32[2,512,128]{2,1,0:T(8,128)}, f32[2,512,128]{2,1,0:T(8,128)}, u32[]{:S(2)}, u32[]{:S(2)}) collective-permute-start(f32[2,512,128]{2,1,0:T(8,128)} %get-tuple-element.43), channel_id=1, source_target_pairs={{1,2},{3,4},{5,6},{7,8},{9,10},{11,12},{13,14},{2,1},{4,3},{6,5},{... | collective-permute-start | bytes 1572872 | tf_op jit(solution)/shard_map/ppermute | solution.py:545
  48.5 1.6 copy-done.4
  51.2 3.9 %prepare.1 = (f32[8,2,256,256]{3,2,1,0:T(8,128)}, bf16[8,256,768]{2,1,0:T(8,128)(2,1)S(1)}, bf16[8,768,256]{2,1,0:T(8,128)(2,1)S(1)}) custom-call(s32[8,2]{1,0:T(8,128)S(1)} %copy.14.starts_ref, f32[2,256,256]{2,1,0:T(8,128)S(1)} %copy-done.13, bf16[8,2,256,256]{3,2,1,0:T(8,128)(2,1)S(1)} %copy-done.4), custom_call_target="tpu_custom_call" | custom-call | flops 134217728 | bytes 12582912 | tf_op jit(solution)/shard_map/prepare/pallas_call | solution.py:130
  55.0 1.6 copy-done
  56.6 5.5 %sort_patterns.1.sorted_ref = f32[8,256,256]{2,1,0:T(8,128)} custom-call(s32[8]{0:T(128)} %bitcast.8, f32[8,256,256]{2,1,0:T(8,128)} %bitcast.5, f32[8,256,256]{2,1,0:T(8,128)} %bitcast.6, bf16[256,256]{1,0:T(8,128)(2,1)} %constant.30.clone.order_ref), custom_call_target="tpu_custom_call" | custom-call | flops 805306368 | bytes 4194304 | tf_op jit(solution)/shard_map/sort_patterns/pallas_call | solution.py:86
  64.1 9.5 %shard_map.105 = (f32[8,2,256,256]{3,2,1,0:T(8,128)}, f32[2,520,512]{2,1,0:T(8,128)S(1)}, f32[256,256]{1,0:T(8,128)S(1)}) custom-call(s32[8,2]{1,0:T(8,128)S(1)} %copy.14.starts_ref, s32[2]{0:T(128)S(1)} %pad_add_fusion.flags_ref, f32[2,256,256]{2,1,0:T(8,128)S(1)} %copy-done.2, f32[2,128,256]{2,1,0:T(8,128)S(1)} %collective-permute-done.ra_ref, ...), custom_call_target="tpu_custom_call" | custom-call | flops 3221225472 | bytes 8388608 | tf_op jit(solution)/shard_map/pallas_call | solution.py:448
  73.6 14.7 %shard_map.108 = (f32[8,2,256,256]{3,2,1,0:T(8,128)}, f32[2,512,128]{2,1,0:T(8,128)S(1)}, f32[2,512,128]{2,1,0:T(8,128)S(1)}, f32[2,512,256]{2,1,0:T(8,128)S(1)}) custom-call(s32[8,2]{1,0:T(8,128)S(1)} %copy.14.starts_ref, s32[2]{0:T(128)S(1)} %pad_add_fusion.flags_ref, f32[2,256,256]{2,1,0:T(8,128)S(1)} %copy-done.6, f32[2,128,256]{2,1,0:T(8,128)S(1)} %copy-done.17, ...), custom_call_target="tpu_custom_call" | custom-call | flops 6442450944 | bytes 16777216 | tf_op jit(solution)/shard_map/pallas_call | solution.py:448
  88.3 9.3 %shard_map.109 = (f32[2,512,128]{2,1,0:T(8,128)S(1)}, f32[2,512,128]{2,1,0:T(8,128)S(1)}, f32[2,512,256]{2,1,0:T(8,128)S(1)}, f32[3,128,256]{2,1,0:T(8,128)S(1)}, f32[3,128,256]{2,1,0:T(8,128)S(1)}) custom-call(s32[8,2]{1,0:T(8,128)S(1)} %copy.14.starts_ref, s32[2]{0:T(128)S(1)} %pad_add_fusion.flags_ref, f32[2,520,512]{2,1,0:T(8,128)S(1)} %get-tuple-element.39.wide, ...), custom_call_target="tpu_custom_call" | custom-call | flops 3221225472 | bytes 8388608 | tf_op jit(solution)/shard_map/pallas_call | solution.py:448
  100.3 1.7 %collective-permute-done.16.got_ref = f32[3,128,256]{2,1,0:T(8,128)S(1)} collective-permute-done((f32[3,128,256]{2,1,0:T(8,128)S(1)}, f32[3,128,256]{2,1,0:T(8,128)S(1)}, u32[]{:S(2)}, u32[]{:S(2)}) %collective-permute-start.16) | collective-permute-done | bytes 393248 | tf_op jit(solution)/shard_map/ppermute | solution.py:545
  103.4 8.8 %all-to-all-start = ((f32[64,16,128]{2,1,0:T(8,128)}), f32[64,16,128]{2,1,0:T(8,128)S(1)}, u32[]{:S(2)}, u32[]{:S(2)}) async-start(f32[64,16,128]{2,1,0:T(8,128)} %shard_map.114), calls=%async_computation | async-start | bytes 1048576 | tf_op jit(solution)/shard_map/all_to_all | solution.py:551
  112.9 3.3 %collective-permute-start.9 = (f32[2,512,128]{2,1,0:T(8,128)}, f32[2,512,128]{2,1,0:T(8,128)}, u32[]{:S(2)}, u32[]{:S(2)}) collective-permute-start(f32[2,512,128]{2,1,0:T(8,128)} %copy-done.22), channel_id=1, source_target_pairs={{1,2},{3,4},{5,6},{7,8},{9,10},{11,12},{13,14},{2,1},{4,3},{6,5},{... | collective-permute-start | bytes 1572872 | tf_op jit(solution)/shard_map/ppermute | solution.py:545
  116.3 3.2 %collective-permute-start.13 = (f32[2,512,128]{2,1,0:T(8,128)}, f32[2,512,128]{2,1,0:T(8,128)}, u32[]{:S(2)}, u32[]{:S(2)}) collective-permute-start(f32[2,512,128]{2,1,0:T(8,128)} %copy-done.20), channel_id=1, source_target_pairs={{1,2},{3,4},{5,6},{7,8},{9,10},{11,12},{13,14},{2,1},{4,3},{6,5},{... | collective-permute-start | bytes 1572872 | tf_op jit(solution)/shard_map/ppermute | solution.py:545
  119.5 3.8 %all-to-all-done.parts_ref = f32[64,16,128]{2,1,0:T(8,128)S(1)} async-done(((f32[64,16,128]{2,1,0:T(8,128)}), f32[64,16,128]{2,1,0:T(8,128)S(1)}, u32[]{:S(2)}, u32[]{:S(2)}) %all-to-all-start) | async-done | bytes 524320 | tf_op jit(solution)/shard_map/all_to_all | solution.py:551
  124.7 5.9 %all-to-all-start.1 = ((f32[64,8,128]{2,1,0:T(8,128)}), f32[64,8,128]{2,1,0:T(8,128)S(1)}, u32[]{:S(2)}, u32[]{:S(2)}) async-start(f32[64,8,128]{2,1,0:T(8,128)} %shard_map.115), calls=%async_computation.1 | async-start | bytes 524288 | tf_op jit(solution)/shard_map/all_to_all | solution.py:551
  130.6 1.6 %collective-permute-done.9.qb_ref = f32[2,512,128]{2,1,0:T(8,128)} collective-permute-done((f32[2,512,128]{2,1,0:T(8,128)}, f32[2,512,128]{2,1,0:T(8,128)}, u32[]{:S(2)}, u32[]{:S(2)}) %collective-permute-start.9) | collective-permute-done | bytes 524320 | tf_op jit(solution)/shard_map/ppermute | solution.py:545
  132.3 1.9 %shard_map.110 = (f32[2,128,256]{2,1,0:T(8,128)S(1)}, f32[2,128,256]{2,1,0:T(8,128)S(1)}, f32[2,256,256]{2,1,0:T(8,128)S(1)}) custom-call(s32[2]{0:T(128)S(1)} %pad_add_fusion.flags_ref, f32[2,512,256]{2,1,0:T(8,128)S(1)} %copy-done.10, f32[2,512,128]{2,1,0:T(8,128)} %collective-permute-done.8.qa_ref, f32[2,512,128]{2,1,0:T(8,128)} %collective-permute-done.9.qb_ref), custom_call_target="tpu_custom_call" | custom-call | flops 786432 | bytes 3145728 | tf_op jit(solution)/shard_map/pallas_call | solution.py:471
  135.5 4.1 %collective-permute-start.11 = (f32[2,128,256]{2,1,0:T(8,128)S(1)}, f32[2,128,256]{2,1,0:T(8,128)S(1)}, u32[]{:S(2)}, u32[]{:S(2)}) collective-permute-start(f32[2,128,256]{2,1,0:T(8,128)S(1)} %get-tuple-element.52), channel_id=1, source_target_pairs={{16,32},{48,64},{80,96},{32,16},{64,48},{96,80},{17,33},{49,65},{8... | collective-permute-start | bytes 786440 | tf_op jit(solution)/shard_map/ppermute | solution.py:545
  139.6 3.9 %collective-permute-done.13.qb_ref = f32[2,512,128]{2,1,0:T(8,128)} collective-permute-done((f32[2,512,128]{2,1,0:T(8,128)}, f32[2,512,128]{2,1,0:T(8,128)}, u32[]{:S(2)}, u32[]{:S(2)}) %collective-permute-start.13) | collective-permute-done | bytes 524320 | tf_op jit(solution)/shard_map/ppermute | solution.py:545
  143.5 2.5 %shard_map.112 = (f32[2,128,256]{2,1,0:T(8,128)}, f32[2,128,256]{2,1,0:T(8,128)}, f32[2,256,256]{2,1,0:T(8,128)S(1)}) custom-call(s32[2]{0:T(128)S(1)} %pad_add_fusion.flags_ref, f32[2,512,256]{2,1,0:T(8,128)S(1)} %copy-done.8, f32[2,512,128]{2,1,0:T(8,128)S(1)} %collective-permute-done.12.qa_ref, f32[2,512,128]{2,1,0:T(8,128)} %collective-permute-done.13.qb_ref), custom_call_target="tpu_custom_call" | custom-call | flops 786432 | bytes 3145728 | tf_op jit(solution)/shard_map/pallas_call | solution.py:471
  146.0 1.4 collective-permute-start.14
  147.4 4.1 %collective-permute-start.15 = (f32[2,128,256]{2,1,0:T(8,128)}, f32[2,128,256]{2,1,0:T(8,128)S(1)}, u32[]{:S(2)}, u32[]{:S(2)}) collective-permute-start(f32[2,128,256]{2,1,0:T(8,128)} %get-tuple-element.58), channel_id=1, source_target_pairs={{16,32},{48,64},{80,96},{32,16},{64,48},{96,80},{17,33},{49,65},{8... | collective-permute-start | bytes 786440 | tf_op jit(solution)/shard_map/ppermute | solution.py:545
  154.6 5.7 %collective-permute-done.15.b_ref = f32[2,128,256]{2,1,0:T(8,128)S(1)} collective-permute-done((f32[2,128,256]{2,1,0:T(8,128)}, f32[2,128,256]{2,1,0:T(8,128)S(1)}, u32[]{:S(2)}, u32[]{:S(2)}) %collective-permute-start.15) | collective-permute-done | bytes 262176 | tf_op jit(solution)/shard_map/ppermute | solution.py:545
  161.6 1.4 shard_map.116
  (76 shorter events, 21.1 us)
Async XLA Ops:
  0.6 47.8 %copy-start.24 = (s32[1,1,8,2]{2,3,1,0:T(2,128)S(1)}, s32[1,1,8,2]{2,3,1,0:T(2,128)}, u32[]{:S(2)}) copy-start(s32[1,1,8,2]{2,3,1,0:T(2,128)} %param.11) | copy-start | bytes 196
  2.4 7.3 %collective-permute-start = (f32[2,128,256]{2,1,0:T(8,128)S(1)}, f32[2,128,256]{2,1,0:T(8,128)S(1)}, u32[]{:S(2)}, u32[]{:S(2)}) collective-permute-start(f32[2,128,256]{2,1,0:T(8,128)S(1)} %get-tuple-element.32), channel_id=1, source_target_pairs={{0,16},{32,48},{64,80},{96,112},{16,0},{48,32},{80,64},{112,96},{1... | collective-permute-start | bytes 786440 | tf_op jit(solution)/shard_map/ppermute | solution.py:545
  3.7 12.4 %collective-permute-start.1 = (f32[2,128,256]{2,1,0:T(8,128)S(1)}, f32[2,128,256]{2,1,0:T(8,128)S(1)}, u32[]{:S(2)}, u32[]{:S(2)}) collective-permute-start(f32[2,128,256]{2,1,0:T(8,128)S(1)} %get-tuple-element.33), channel_id=1, source_target_pairs={{16,32},{48,64},{80,96},{32,16},{64,48},{96,80},{17,33},{49,65},{8... | collective-permute-start | bytes 786440 | tf_op jit(solution)/shard_map/ppermute | solution.py:545
  17.8 44.3 %collective-permute-start.2 = (f32[2,512,128]{2,1,0:T(8,128)}, f32[2,512,128]{2,1,0:T(8,128)}, u32[]{:S(2)}, u32[]{:S(2)}) collective-permute-start(f32[2,512,128]{2,1,0:T(8,128)} %get-tuple-element.34), channel_id=1, source_target_pairs={{0,1},{2,3},{4,5},{6,7},{8,9},{10,11},{12,13},{14,15},{1,0},{3,2},... | collective-permute-start | bytes 1572872 | tf_op jit(solution)/shard_map/ppermute | solution.py:545
  19.6 42.5 %collective-permute-start.3 = (f32[2,512,128]{2,1,0:T(8,128)}, f32[2,512,128]{2,1,0:T(8,128)}, u32[]{:S(2)}, u32[]{:S(2)}) collective-permute-start(f32[2,512,128]{2,1,0:T(8,128)} %get-tuple-element.35), channel_id=1, source_target_pairs={{1,2},{3,4},{5,6},{7,8},{9,10},{11,12},{13,14},{2,1},{4,3},{6,5},{... | collective-permute-start | bytes 1572872 | tf_op jit(solution)/shard_map/ppermute | solution.py:545
  24.9 7.7 %collective-permute-start.4 = (f32[2,128,256]{2,1,0:T(8,128)S(1)}, f32[2,128,256]{2,1,0:T(8,128)S(1)}, u32[]{:S(2)}, u32[]{:S(2)}) collective-permute-start(f32[2,128,256]{2,1,0:T(8,128)S(1)} %get-tuple-element.40), channel_id=1, source_target_pairs={{0,16},{32,48},{64,80},{96,112},{16,0},{48,32},{80,64},{112,96},{1... | collective-permute-start | bytes 786440 | tf_op jit(solution)/shard_map/ppermute | solution.py:545
  25.0 18.0 %collective-permute-start.5 = (f32[2,128,256]{2,1,0:T(8,128)S(1)}, f32[2,128,256]{2,1,0:T(8,128)S(1)}, u32[]{:S(2)}, u32[]{:S(2)}) collective-permute-start(f32[2,128,256]{2,1,0:T(8,128)S(1)} %get-tuple-element.41), channel_id=1, source_target_pairs={{16,32},{48,64},{80,96},{32,16},{64,48},{96,80},{17,33},{49,65},{8... | collective-permute-start | bytes 786440 | tf_op jit(solution)/shard_map/ppermute | solution.py:545
  32.6 12.0 %copy-start.16 = (f32[2,128,256]{2,1,0:T(8,128)}, f32[2,128,256]{2,1,0:T(8,128)S(1)}, u32[]{:S(2)}) copy-start(f32[2,128,256]{2,1,0:T(8,128)S(1)} %collective-permute-done.4.ra_ref) | copy-start | bytes 786436
  44.7 28.9 %collective-permute-start.6 = (f32[2,512,128]{2,1,0:T(8,128)}, f32[2,512,128]{2,1,0:T(8,128)}, u32[]{:S(2)}, u32[]{:S(2)}) collective-permute-start(f32[2,512,128]{2,1,0:T(8,128)} %get-tuple-element.42), channel_id=1, source_target_pairs={{0,1},{2,3},{4,5},{6,7},{8,9},{10,11},{12,13},{14,15},{1,0},{3,2},... | collective-permute-start | bytes 1572872 | tf_op jit(solution)/shard_map/ppermute | solution.py:545
  44.7 28.9 %collective-permute-start.7 = (f32[2,512,128]{2,1,0:T(8,128)}, f32[2,512,128]{2,1,0:T(8,128)}, u32[]{:S(2)}, u32[]{:S(2)}) collective-permute-start(f32[2,512,128]{2,1,0:T(8,128)} %get-tuple-element.43), channel_id=1, source_target_pairs={{1,2},{3,4},{5,6},{7,8},{9,10},{11,12},{13,14},{2,1},{4,3},{6,5},{... | collective-permute-start | bytes 1572872 | tf_op jit(solution)/shard_map/ppermute | solution.py:545
  64.1 9.5 %copy-start.3 = (f32[8,256,256]{2,1,0:T(8,128)S(1)}, f32[8,256,256]{2,1,0:T(8,128)}, u32[]{:S(2)}) copy-start(f32[8,256,256]{2,1,0:T(8,128)} %sort_patterns.1.sorted_ref) | copy-start | bytes 6291460
  64.1 9.5 %copy-start.6 = (f32[2,256,256]{2,1,0:T(8,128)S(1)}, f32[2,256,256]{2,1,0:T(8,128)}, u32[]{:S(2)}) copy-start(f32[2,256,256]{2,1,0:T(8,128)} %own_ref.7) | copy-start | bytes 1572868
  64.1 9.5 %copy-start.17 = (f32[2,128,256]{2,1,0:T(8,128)S(1)}, f32[2,128,256]{2,1,0:T(8,128)}, u32[]{:S(2)}) copy-start(f32[2,128,256]{2,1,0:T(8,128)} %copy-done.16) | copy-start | bytes 786436
  64.1 9.5 %copy-start.19 = (f32[2,128,256]{2,1,0:T(8,128)S(1)}, f32[2,128,256]{2,1,0:T(8,128)}, u32[]{:S(2)}) copy-start(f32[2,128,256]{2,1,0:T(8,128)} %copy-done.18) | copy-start | bytes 786436
  88.3 9.3 %copy-start.7 = (f32[2,512,256]{2,1,0:T(8,128)}, f32[2,512,256]{2,1,0:T(8,128)S(1)}, u32[]{:S(2)}) copy-start(f32[2,512,256]{2,1,0:T(8,128)S(1)} %get-tuple-element.53.mid_ref) | copy-start | bytes 3145732
  88.3 9.3 %copy-start.20 = (f32[2,512,128]{2,1,0:T(8,128)}, f32[2,512,128]{2,1,0:T(8,128)S(1)}, u32[]{:S(2)}) copy-start(f32[2,512,128]{2,1,0:T(8,128)S(1)} %get-tuple-element.55) | copy-start | bytes 1572868
  88.3 9.3 %copy-start.21 = (f32[2,512,128]{2,1,0:T(8,128)}, f32[2,512,128]{2,1,0:T(8,128)S(1)}, u32[]{:S(2)}) copy-start(f32[2,512,128]{2,1,0:T(8,128)S(1)} %get-tuple-element.54) | copy-start | bytes 1572868
  100.3 32.0 %copy-start.10 = (f32[2,512,256]{2,1,0:T(8,128)S(1)}, f32[2,512,256]{2,1,0:T(8,128)}, u32[]{:S(2)}) copy-start(f32[2,512,256]{2,1,0:T(8,128)} %copy-done.9) | copy-start | bytes 3145732
  100.3 43.2 %copy-start.8 = (f32[2,512,256]{2,1,0:T(8,128)S(1)}, f32[2,512,256]{2,1,0:T(8,128)}, u32[]{:S(2)}) copy-start(f32[2,512,256]{2,1,0:T(8,128)} %copy-done.7) | copy-start | bytes 3145732
  100.3 1.7 %collective-permute-start.16 = (f32[3,128,256]{2,1,0:T(8,128)S(1)}, f32[3,128,256]{2,1,0:T(8,128)S(1)}, u32[]{:S(2)}, u32[]{:S(2)}) collective-permute-start(f32[3,128,256]{2,1,0:T(8,128)S(1)} %get-tuple-element.60), channel_id=1, source_target_pairs={{0,1},{2,3},{4,5},{6,7},{8,9},{10,11},{12,13},{14,15},{1,0},{3,2},... | collective-permute-start | bytes 1179656 | tf_op jit(solution)/shard_map/ppermute | solution.py:545
  103.4 19.9 %all-to-all-start = ((f32[64,16,128]{2,1,0:T(8,128)}), f32[64,16,128]{2,1,0:T(8,128)S(1)}, u32[]{:S(2)}, u32[]{:S(2)}) async-start(f32[64,16,128]{2,1,0:T(8,128)} %shard_map.114), calls=%async_computation | async-start | bytes 1048576 | tf_op jit(solution)/shard_map/all_to_all | solution.py:551
  112.2 18.4 %collective-permute-start.8 = (f32[2,512,128]{2,1,0:T(8,128)}, f32[2,512,128]{2,1,0:T(8,128)}, u32[]{:S(2)}, u32[]{:S(2)}) collective-permute-start(f32[2,512,128]{2,1,0:T(8,128)} %copy-done.23), channel_id=1, source_target_pairs={{0,1},{2,3},{4,5},{6,7},{8,9},{10,11},{12,13},{14,15},{1,0},{3,2},... | collective-permute-start | bytes 1572872 | tf_op jit(solution)/shard_map/ppermute | solution.py:545
  112.9 19.3 %collective-permute-start.9 = (f32[2,512,128]{2,1,0:T(8,128)}, f32[2,512,128]{2,1,0:T(8,128)}, u32[]{:S(2)}, u32[]{:S(2)}) collective-permute-start(f32[2,512,128]{2,1,0:T(8,128)} %copy-done.22), channel_id=1, source_target_pairs={{1,2},{3,4},{5,6},{7,8},{9,10},{11,12},{13,14},{2,1},{4,3},{6,5},{... | collective-permute-start | bytes 1572872 | tf_op jit(solution)/shard_map/ppermute | solution.py:545
  116.2 23.4 %collective-permute-start.12 = (f32[2,512,128]{2,1,0:T(8,128)}, f32[2,512,128]{2,1,0:T(8,128)S(1)}, u32[]{:S(2)}, u32[]{:S(2)}) collective-permute-start(f32[2,512,128]{2,1,0:T(8,128)} %copy-done.21), channel_id=1, source_target_pairs={{0,1},{2,3},{4,5},{6,7},{8,9},{10,11},{12,13},{14,15},{1,0},{3,2},... | collective-permute-start | bytes 1572872 | tf_op jit(solution)/shard_map/ppermute | solution.py:545
  116.3 27.2 %collective-permute-start.13 = (f32[2,512,128]{2,1,0:T(8,128)}, f32[2,512,128]{2,1,0:T(8,128)}, u32[]{:S(2)}, u32[]{:S(2)}) collective-permute-start(f32[2,512,128]{2,1,0:T(8,128)} %copy-done.20), channel_id=1, source_target_pairs={{1,2},{3,4},{5,6},{7,8},{9,10},{11,12},{13,14},{2,1},{4,3},{6,5},{... | collective-permute-start | bytes 1572872 | tf_op jit(solution)/shard_map/ppermute | solution.py:545
  124.7 26.9 %all-to-all-start.1 = ((f32[64,8,128]{2,1,0:T(8,128)}), f32[64,8,128]{2,1,0:T(8,128)S(1)}, u32[]{:S(2)}, u32[]{:S(2)}) async-start(f32[64,8,128]{2,1,0:T(8,128)} %shard_map.115), calls=%async_computation.1 | async-start | bytes 524288 | tf_op jit(solution)/shard_map/all_to_all | solution.py:551
  134.1 13.3 %copy-start.14 = (f32[2,256,256]{2,1,0:T(8,128)}, f32[2,256,256]{2,1,0:T(8,128)S(1)}, u32[]{:S(2)}) copy-start(f32[2,256,256]{2,1,0:T(8,128)S(1)} %get-tuple-element.50.center_ref) | copy-start | bytes 1572868
  134.2 17.5 %collective-permute-start.10 = (f32[2,128,256]{2,1,0:T(8,128)S(1)}, f32[2,128,256]{2,1,0:T(8,128)S(1)}, u32[]{:S(2)}, u32[]{:S(2)}) collective-permute-start(f32[2,128,256]{2,1,0:T(8,128)S(1)} %get-tuple-element.51), channel_id=1, source_target_pairs={{0,16},{32,48},{64,80},{96,112},{16,0},{48,32},{80,64},{112,96},{1... | collective-permute-start | bytes 786440 | tf_op jit(solution)/shard_map/ppermute | solution.py:545
  135.5 16.7 %collective-permute-start.11 = (f32[2,128,256]{2,1,0:T(8,128)S(1)}, f32[2,128,256]{2,1,0:T(8,128)S(1)}, u32[]{:S(2)}, u32[]{:S(2)}) collective-permute-start(f32[2,128,256]{2,1,0:T(8,128)S(1)} %get-tuple-element.52), channel_id=1, source_target_pairs={{16,32},{48,64},{80,96},{32,16},{64,48},{96,80},{17,33},{49,65},{8... | collective-permute-start | bytes 786440 | tf_op jit(solution)/shard_map/ppermute | solution.py:545
  146.0 8.6 %collective-permute-start.14 = (f32[2,128,256]{2,1,0:T(8,128)}, f32[2,128,256]{2,1,0:T(8,128)S(1)}, u32[]{:S(2)}, u32[]{:S(2)}) collective-permute-start(f32[2,128,256]{2,1,0:T(8,128)} %get-tuple-element.57), channel_id=1, source_target_pairs={{0,16},{32,48},{64,80},{96,112},{16,0},{48,32},{80,64},{112,96},{1... | collective-permute-start | bytes 786440 | tf_op jit(solution)/shard_map/ppermute | solution.py:545
  147.4 12.8 %collective-permute-start.15 = (f32[2,128,256]{2,1,0:T(8,128)}, f32[2,128,256]{2,1,0:T(8,128)S(1)}, u32[]{:S(2)}, u32[]{:S(2)}) collective-permute-start(f32[2,128,256]{2,1,0:T(8,128)} %get-tuple-element.58), channel_id=1, source_target_pairs={{16,32},{48,64},{80,96},{32,16},{64,48},{96,80},{17,33},{49,65},{8... | collective-permute-start | bytes 786440 | tf_op jit(solution)/shard_map/ppermute | solution.py:545
  151.6 10.0 %collective-permute-start.17 = (f32[64,8,128]{2,1,0:T(8,128)S(1)}, f32[64,8,128]{2,1,0:T(8,128)S(1)}, u32[]{:S(2)}, u32[]{:S(2)}) collective-permute-start(f32[64,8,128]{2,1,0:T(8,128)S(1)} %all-to-all-done.1.own_ref), channel_id=1, source_target_pairs={{0,1},{2,3},{4,5},{6,7},{8,9},{10,11},{12,13},{14,15},{1,0},{3,2},... | collective-permute-start | bytes 786440 | tf_op jit(solution)/shard_map/ppermute | solution.py:545
  (13 other events, 17.0 us)

commit v5 on v4

--- a/solution.py
+++ b/solution.py
@@ -486,12 +486,6 @@
     return pl.ds(pl.multiple_of(choice * half, half), half)
 
 
-def pack_edges(flags_ref, own_ref, a_ref, b_ref):
-    row_odd = flags_ref[0]
-    for out, rows in ((a_ref, half_at(1 - row_odd)), (b_ref, half_at(row_odd))):
-        out[...] = own_ref[:, rows, :]
-
-
 def pack_walls(flags_ref, two_ref, ra_ref, rb_ref, a_ref, b_ref):
     row_odd, col_odd = flags_ref[0], flags_ref[1]
     for out, lanes in ((a_ref, half_at(1 - col_odd)), (b_ref, half_at(col_odd))):
@@ -557,7 +551,8 @@
     edge, wall, tile = (2, half, win), (2, 2 * win, half), (2, win, win)
 
     def edges_of(own):
-        ra, rb = small_kernel(pack_edges, flags, (own,), (edge, edge))
+        zero = jnp.zeros((), jnp.int32)
+        ra, rb = (lax.dynamic_slice(own, (zero, half * at, zero), edge) for at in (1 - flags[0], flags[0]))
         return swapped(ra, "row", 0), swapped(rb, "row", 1)
 
     def walls_of(own, edges):

time: 164 us -> 163 us (level)
  local copies, waits for them, and re-layouts: 12.1 us -> 14.2 us
    dynamic_slice x0 -> x2, local copies, waits for them, and re-layouts: none -> 2.2 us  [edges_of(): lax.dynamic_slice(own, (zero, half * at, zero), edge)]
    pallas_call x11 -> x9, Pallas kernels: 15.7 us -> 15.1 us  [small_kernel(): pl.pallas_call(kernel, out_shape=[jax.ShapeDtypeStruct(shape, f32) for sh...]
  transfers between devices with their start and end apart: 20 -> 20, of which waited for: 10 -> 8; matrix products, arithmetic and copies ran while one was open for 0% -> 1% of each run, Pallas kernels for 18% -> 18%
where the time goes in v5:
time: 163 us; the launch traced here: 162 us
  Pallas kernels  57.4 us (35%)
  starting transfers between devices  52.1 us (32%)
  waiting for transfers between devices  37.6 us (23%)
  local copies, waits for them, and re-layouts  14.2 us (9%)
    ppermute x18, starting transfers between devices, swapped(): return lax.ppermute(block, axis, pairs + [(j, i) for i, j in pairs])  38.2 us
    ppermute x18, waiting for transfers between devices, swapped(): return lax.ppermute(block, axis, pairs + [(j, i) for i, j in pairs])  33.8 us
    pallas_call x3, Pallas kernels, position_kernel(): pl.pallas_call(body, out_shape=[jax.ShapeDtypeStruct(shape, f32) for shap...  33 us
    pallas_call x9, Pallas kernels, small_kernel(): pl.pallas_call(kernel, out_shape=[jax.ShapeDtypeStruct(shape, f32) for sh...  15.1 us
    all_to_all x2, starting transfers between devices, exchanged(): lax.all_to_all(parts, ('row', 'col'), 0, 0, axis_index_groups=groups, til...  14 us
    unnamed x50, local copies, waits for them, and re-layouts  11.9 us
    pallas_call x1, Pallas kernels, sort_patterns(): pl.pallas_call(sort_body, out_shape=jax.ShapeDtypeStruct((positions, win,...  5.46 us
    pallas_call x1, Pallas kernels, prepare(): pl.pallas_call(prepare_body, out_shape=(jax.ShapeDtypeStruct((positions,...  3.86 us
  transfers between devices with their start and end apart: 20, of which 8 were waited for; matrix products, arithmetic and copies ran while one was open for 1% of the time, Pallas kernels for 18%

profile of v5, /device:TPU:7, one launch (start us, length us, event | category | flops | bytes accessed | tf_op | source)
XLA Modules:
  0.0 162.3 jit_solution(4331638837397106305)
XLA Ops:
  1.8 5.5 %collective-permute-start.1 = (f32[2,128,256]{2,1,0:T(8,128)S(1)}, f32[2,128,256]{2,1,0:T(8,128)S(1)}, u32[]{:S(2)}, u32[]{:S(2)}) collective-permute-start(f32[2,128,256]{2,1,0:T(8,128)S(1)} %get-tuple-element.55), channel_id=1, source_target_pairs={{16,32},{48,64},{80,96},{32,16},{64,48},{96,80},{17,33},{49,65},{8... | collective-permute-start | bytes 786440 | tf_op jit(solution)/shard_map/ppermute | solution.py:539
  7.5 7.0 %collective-permute-done.1.rb_ref = f32[2,128,256]{2,1,0:T(8,128)S(1)} collective-permute-done((f32[2,128,256]{2,1,0:T(8,128)S(1)}, f32[2,128,256]{2,1,0:T(8,128)S(1)}, u32[]{:S(2)}, u32[]{:S(2)}) %collective-permute-start.1) | collective-permute-done | bytes 262176 | tf_op jit(solution)/shard_map/ppermute | solution.py:539
  15.5 1.6 %shard_map.103 = (f32[2,512,128]{2,1,0:T(8,128)}, f32[2,512,128]{2,1,0:T(8,128)}) custom-call(s32[2]{0:T(128)S(1)} %pad_add_fusion.flags_ref, f32[2,256,256]{2,1,0:T(8,128)S(1)} %copy-done.1, f32[2,128,256]{2,1,0:T(8,128)S(1)} %collective-permute-done.ra_ref, f32[2,128,256]{2,1,0:T(8,128)S(1)} %collective-permute-done.1.rb_ref), custom_call_target="tpu_custom_call" | custom-call | flops 524288 | bytes 2097152 | tf_op jit(solution)/shard_map/pallas_call | solution.py:471
  17.2 1.6 collective-permute-start.2
  18.8 3.6 %collective-permute-start.3 = (f32[2,512,128]{2,1,0:T(8,128)}, f32[2,512,128]{2,1,0:T(8,128)}, u32[]{:S(2)}, u32[]{:S(2)}) collective-permute-start(f32[2,512,128]{2,1,0:T(8,128)} %get-tuple-element.29), channel_id=1, source_target_pairs={{1,2},{3,4},{5,6},{7,8},{9,10},{11,12},{13,14},{2,1},{4,3},{6,5},{... | collective-permute-start | bytes 1572872 | tf_op jit(solution)/shard_map/ppermute | solution.py:539
  23.5 5.2 %collective-permute-start.5 = (f32[2,128,256]{2,1,0:T(8,128)S(1)}, f32[2,128,256]{2,1,0:T(8,128)S(1)}, u32[]{:S(2)}, u32[]{:S(2)}) collective-permute-start(f32[2,128,256]{2,1,0:T(8,128)S(1)} %get-tuple-element.53), channel_id=1, source_target_pairs={{16,32},{48,64},{80,96},{32,16},{64,48},{96,80},{17,33},{49,65},{8... | collective-permute-start | bytes 786440 | tf_op jit(solution)/shard_map/ppermute | solution.py:539
  28.8 14.2 %collective-permute-done.5.rb_ref = f32[2,128,256]{2,1,0:T(8,128)S(1)} collective-permute-done((f32[2,128,256]{2,1,0:T(8,128)S(1)}, f32[2,128,256]{2,1,0:T(8,128)S(1)}, u32[]{:S(2)}, u32[]{:S(2)}) %collective-permute-start.5) | collective-permute-done | bytes 262176 | tf_op jit(solution)/shard_map/ppermute | solution.py:539
  43.0 1.6 shard_map.105
  44.7 3.7 %collective-permute-start.7 = (f32[2,512,128]{2,1,0:T(8,128)}, f32[2,512,128]{2,1,0:T(8,128)}, u32[]{:S(2)}, u32[]{:S(2)}) collective-permute-start(f32[2,512,128]{2,1,0:T(8,128)} %get-tuple-element.35), channel_id=1, source_target_pairs={{1,2},{3,4},{5,6},{7,8},{9,10},{11,12},{13,14},{2,1},{4,3},{6,5},{... | collective-permute-start | bytes 1572872 | tf_op jit(solution)/shard_map/ppermute | solution.py:539
  48.5 1.6 copy-done.4
  51.1 3.9 %prepare.1 = (f32[8,2,256,256]{3,2,1,0:T(8,128)}, bf16[8,256,768]{2,1,0:T(8,128)(2,1)S(1)}, bf16[8,768,256]{2,1,0:T(8,128)(2,1)S(1)}) custom-call(s32[8,2]{1,0:T(8,128)S(1)} %copy.14.starts_ref, f32[2,256,256]{2,1,0:T(8,128)S(1)} %copy-done.13, bf16[8,2,256,256]{3,2,1,0:T(8,128)(2,1)S(1)} %copy-done.4), custom_call_target="tpu_custom_call" | custom-call | flops 134217728 | bytes 12582912 | tf_op jit(solution)/shard_map/prepare/pallas_call | solution.py:130
  55.0 1.6 copy-done
  56.6 5.5 %sort_patterns.1.sorted_ref = f32[8,256,256]{2,1,0:T(8,128)} custom-call(s32[8]{0:T(128)} %bitcast.8, f32[8,256,256]{2,1,0:T(8,128)} %bitcast.5, f32[8,256,256]{2,1,0:T(8,128)} %bitcast.6, bf16[256,256]{1,0:T(8,128)(2,1)} %constant.36.clone.order_ref), custom_call_target="tpu_custom_call" | custom-call | flops 805306368 | bytes 4194304 | tf_op jit(solution)/shard_map/sort_patterns/pallas_call | solution.py:86
  64.1 9.5 %shard_map.104 = (f32[8,2,256,256]{3,2,1,0:T(8,128)}, f32[2,520,512]{2,1,0:T(8,128)S(1)}, f32[256,256]{1,0:T(8,128)S(1)}) custom-call(s32[8,2]{1,0:T(8,128)S(1)} %copy.14.starts_ref, s32[2]{0:T(128)S(1)} %pad_add_fusion.flags_ref, f32[2,256,256]{2,1,0:T(8,128)S(1)} %copy-done.2, f32[2,128,256]{2,1,0:T(8,128)S(1)} %copy-done.12, ...), custom_call_target="tpu_custom_call" | custom-call | flops 3221225472 | bytes 8388608 | tf_op jit(solution)/shard_map/pallas_call | solution.py:448
  73.7 14.2 %shard_map.106 = (f32[8,2,256,256]{3,2,1,0:T(8,128)}, f32[2,512,128]{2,1,0:T(8,128)S(1)}, f32[2,512,128]{2,1,0:T(8,128)S(1)}, f32[2,512,256]{2,1,0:T(8,128)S(1)}) custom-call(s32[8,2]{1,0:T(8,128)S(1)} %copy.14.starts_ref, s32[2]{0:T(128)S(1)} %pad_add_fusion.flags_ref, f32[2,256,256]{2,1,0:T(8,128)S(1)} %copy-done.6, f32[2,128,256]{2,1,0:T(8,128)S(1)} %copy-done.19, ...), custom_call_target="tpu_custom_call" | custom-call | flops 6442450944 | bytes 16777216 | tf_op jit(solution)/shard_map/pallas_call | solution.py:448
  88.8 9.2 %shard_map.107 = (f32[2,512,128]{2,1,0:T(8,128)S(1)}, f32[2,512,128]{2,1,0:T(8,128)S(1)}, f32[2,512,256]{2,1,0:T(8,128)S(1)}, f32[3,128,256]{2,1,0:T(8,128)S(1)}, f32[3,128,256]{2,1,0:T(8,128)S(1)}) custom-call(s32[8,2]{1,0:T(8,128)S(1)} %copy.14.starts_ref, s32[2]{0:T(128)S(1)} %pad_add_fusion.flags_ref, f32[2,520,512]{2,1,0:T(8,128)S(1)} %get-tuple-element.33.wide, ...), custom_call_target="tpu_custom_call" | custom-call | flops 3221225472 | bytes 8388608 | tf_op jit(solution)/shard_map/pallas_call | solution.py:448
  100.7 1.7 %collective-permute-done.16.got_ref = f32[3,128,256]{2,1,0:T(8,128)S(1)} collective-permute-done((f32[3,128,256]{2,1,0:T(8,128)S(1)}, f32[3,128,256]{2,1,0:T(8,128)S(1)}, u32[]{:S(2)}, u32[]{:S(2)}) %collective-permute-start.16) | collective-permute-done | bytes 393248 | tf_op jit(solution)/shard_map/ppermute | solution.py:539
  103.8 8.0 %all-to-all-start = ((f32[64,16,128]{2,1,0:T(8,128)}), f32[64,16,128]{2,1,0:T(8,128)S(1)}, u32[]{:S(2)}, u32[]{:S(2)}) async-start(f32[64,16,128]{2,1,0:T(8,128)} %shard_map.112), calls=%async_computation | async-start | bytes 1048576 | tf_op jit(solution)/shard_map/all_to_all | solution.py:545
  112.6 3.3 %collective-permute-start.9 = (f32[2,512,128]{2,1,0:T(8,128)}, f32[2,512,128]{2,1,0:T(8,128)}, u32[]{:S(2)}, u32[]{:S(2)}) collective-permute-start(f32[2,512,128]{2,1,0:T(8,128)} %copy-done.22), channel_id=1, source_target_pairs={{1,2},{3,4},{5,6},{7,8},{9,10},{11,12},{13,14},{2,1},{4,3},{6,5},{... | collective-permute-start | bytes 1572872 | tf_op jit(solution)/shard_map/ppermute | solution.py:539
  116.0 3.2 %collective-permute-start.13 = (f32[2,512,128]{2,1,0:T(8,128)}, f32[2,512,128]{2,1,0:T(8,128)}, u32[]{:S(2)}, u32[]{:S(2)}) collective-permute-start(f32[2,512,128]{2,1,0:T(8,128)} %copy-done.20), channel_id=1, source_target_pairs={{1,2},{3,4},{5,6},{7,8},{9,10},{11,12},{13,14},{2,1},{4,3},{6,5},{... | collective-permute-start | bytes 1572872 | tf_op jit(solution)/shard_map/ppermute | solution.py:539
  119.2 3.8 %all-to-all-done.parts_ref = f32[64,16,128]{2,1,0:T(8,128)S(1)} async-done(((f32[64,16,128]{2,1,0:T(8,128)}), f32[64,16,128]{2,1,0:T(8,128)S(1)}, u32[]{:S(2)}, u32[]{:S(2)}) %all-to-all-start) | async-done | bytes 524320 | tf_op jit(solution)/shard_map/all_to_all | solution.py:545
  124.3 5.9 %all-to-all-start.1 = ((f32[64,8,128]{2,1,0:T(8,128)}), f32[64,8,128]{2,1,0:T(8,128)S(1)}, u32[]{:S(2)}, u32[]{:S(2)}) async-start(f32[64,8,128]{2,1,0:T(8,128)} %shard_map.113), calls=%async_computation.1 | async-start | bytes 524288 | tf_op jit(solution)/shard_map/all_to_all | solution.py:545
  130.3 1.6 %collective-permute-done.9.qb_ref = f32[2,512,128]{2,1,0:T(8,128)} collective-permute-done((f32[2,512,128]{2,1,0:T(8,128)}, f32[2,512,128]{2,1,0:T(8,128)}, u32[]{:S(2)}, u32[]{:S(2)}) %collective-permute-start.9) | collective-permute-done | bytes 524320 | tf_op jit(solution)/shard_map/ppermute | solution.py:539
  131.9 2.6 %shard_map.108 = (f32[2,128,256]{2,1,0:T(8,128)}, f32[2,128,256]{2,1,0:T(8,128)S(1)}, f32[2,256,256]{2,1,0:T(8,128)S(1)}) custom-call(s32[2]{0:T(128)S(1)} %pad_add_fusion.flags_ref, f32[2,512,256]{2,1,0:T(8,128)S(1)} %copy-done.10, f32[2,512,128]{2,1,0:T(8,128)} %collective-permute-done.8.qa_ref, f32[2,512,128]{2,1,0:T(8,128)} %collective-permute-done.9.qb_ref), custom_call_target="tpu_custom_call" | custom-call | flops 786432 | bytes 3145728 | tf_op jit(solution)/shard_map/pallas_call | solution.py:471
  135.7 4.1 %collective-permute-start.11 = (f32[2,128,256]{2,1,0:T(8,128)S(1)}, f32[2,128,256]{2,1,0:T(8,128)S(1)}, u32[]{:S(2)}, u32[]{:S(2)}) collective-permute-start(f32[2,128,256]{2,1,0:T(8,128)S(1)} %get-tuple-element.44), channel_id=1, source_target_pairs={{16,32},{48,64},{80,96},{32,16},{64,48},{96,80},{17,33},{49,65},{8... | collective-permute-start | bytes 786440 | tf_op jit(solution)/shard_map/ppermute | solution.py:539
  139.9 3.3 %collective-permute-done.13.qb_ref = f32[2,512,128]{2,1,0:T(8,128)} collective-permute-done((f32[2,512,128]{2,1,0:T(8,128)}, f32[2,512,128]{2,1,0:T(8,128)}, u32[]{:S(2)}, u32[]{:S(2)}) %collective-permute-start.13) | collective-permute-done | bytes 524320 | tf_op jit(solution)/shard_map/ppermute | solution.py:539
  143.2 2.4 %shard_map.110 = (f32[2,128,256]{2,1,0:T(8,128)}, f32[2,128,256]{2,1,0:T(8,128)S(1)}, f32[2,256,256]{2,1,0:T(8,128)S(1)}) custom-call(s32[2]{0:T(128)S(1)} %pad_add_fusion.flags_ref, f32[2,512,256]{2,1,0:T(8,128)S(1)} %copy-done.8, f32[2,512,128]{2,1,0:T(8,128)S(1)} %collective-permute-done.12.qa_ref, f32[2,512,128]{2,1,0:T(8,128)} %collective-permute-done.13.qb_ref), custom_call_target="tpu_custom_call" | custom-call | flops 786432 | bytes 3145728 | tf_op jit(solution)/shard_map/pallas_call | solution.py:471
  145.6 1.4 collective-permute-start.14
  147.0 4.1 %collective-permute-start.15 = (f32[2,128,256]{2,1,0:T(8,128)S(1)}, f32[2,128,256]{2,1,0:T(8,128)S(1)}, u32[]{:S(2)}, u32[]{:S(2)}) collective-permute-start(f32[2,128,256]{2,1,0:T(8,128)S(1)} %get-tuple-element.50), channel_id=1, source_target_pairs={{16,32},{48,64},{80,96},{32,16},{64,48},{96,80},{17,33},{49,65},{8... | collective-permute-start | bytes 786440 | tf_op jit(solution)/shard_map/ppermute | solution.py:539
  154.2 5.3 %collective-permute-done.15.b_ref = f32[2,128,256]{2,1,0:T(8,128)S(1)} collective-permute-done((f32[2,128,256]{2,1,0:T(8,128)S(1)}, f32[2,128,256]{2,1,0:T(8,128)S(1)}, u32[]{:S(2)}, u32[]{:S(2)}) %collective-permute-start.15) | collective-permute-done | bytes 262176 | tf_op jit(solution)/shard_map/ppermute | solution.py:539
  159.5 1.4 shard_map.111
  160.9 1.4 shard_map.114
  (76 shorter events, 18.1 us)
Async XLA Ops:
  0.6 42.4 %copy-start.5 = (f32[2,256,256]{2,1,0:T(8,128)S(1)}, f32[2,256,256]{2,1,0:T(8,128)}, u32[]{:S(2)}) copy-start(f32[2,256,256]{2,1,0:T(8,128)} %own_ref.3) | copy-start | bytes 1572868
  0.6 47.8 %copy-start.24 = (s32[1,1,8,2]{2,3,1,0:T(2,128)S(1)}, s32[1,1,8,2]{2,3,1,0:T(2,128)}, u32[]{:S(2)}) copy-start(s32[1,1,8,2]{2,3,1,0:T(2,128)} %param.11) | copy-start | bytes 196
  1.8 12.7 %collective-permute-start.1 = (f32[2,128,256]{2,1,0:T(8,128)S(1)}, f32[2,128,256]{2,1,0:T(8,128)S(1)}, u32[]{:S(2)}, u32[]{:S(2)}) collective-permute-start(f32[2,128,256]{2,1,0:T(8,128)S(1)} %get-tuple-element.55), channel_id=1, source_target_pairs={{16,32},{48,64},{80,96},{32,16},{64,48},{96,80},{17,33},{49,65},{8... | collective-permute-start | bytes 786440 | tf_op jit(solution)/shard_map/ppermute | solution.py:539
  7.3 7.2 %collective-permute-start = (f32[2,128,256]{2,1,0:T(8,128)S(1)}, f32[2,128,256]{2,1,0:T(8,128)S(1)}, u32[]{:S(2)}, u32[]{:S(2)}) collective-permute-start(f32[2,128,256]{2,1,0:T(8,128)S(1)} %get-tuple-element.56), channel_id=1, source_target_pairs={{0,16},{32,48},{64,80},{96,112},{16,0},{48,32},{80,64},{112,96},{1... | collective-permute-start | bytes 786440 | tf_op jit(solution)/shard_map/ppermute | solution.py:539
  15.5 32.9 %copy-start.11 = (f32[2,128,256]{2,1,0:T(8,128)}, f32[2,128,256]{2,1,0:T(8,128)S(1)}, u32[]{:S(2)}) copy-start(f32[2,128,256]{2,1,0:T(8,128)S(1)} %collective-permute-done.ra_ref) | copy-start | bytes 786436
  17.2 44.9 %collective-permute-start.2 = (f32[2,512,128]{2,1,0:T(8,128)}, f32[2,512,128]{2,1,0:T(8,128)}, u32[]{:S(2)}, u32[]{:S(2)}) collective-permute-start(f32[2,512,128]{2,1,0:T(8,128)} %get-tuple-element.28), channel_id=1, source_target_pairs={{0,1},{2,3},{4,5},{6,7},{8,9},{10,11},{12,13},{14,15},{1,0},{3,2},... | collective-permute-start | bytes 1572872 | tf_op jit(solution)/shard_map/ppermute | solution.py:539
  18.8 43.3 %collective-permute-start.3 = (f32[2,512,128]{2,1,0:T(8,128)}, f32[2,512,128]{2,1,0:T(8,128)}, u32[]{:S(2)}, u32[]{:S(2)}) collective-permute-start(f32[2,512,128]{2,1,0:T(8,128)} %get-tuple-element.29), channel_id=1, source_target_pairs={{1,2},{3,4},{5,6},{7,8},{9,10},{11,12},{13,14},{2,1},{4,3},{6,5},{... | collective-permute-start | bytes 1572872 | tf_op jit(solution)/shard_map/ppermute | solution.py:539
  23.5 19.5 %collective-permute-start.5 = (f32[2,128,256]{2,1,0:T(8,128)S(1)}, f32[2,128,256]{2,1,0:T(8,128)S(1)}, u32[]{:S(2)}, u32[]{:S(2)}) collective-permute-start(f32[2,128,256]{2,1,0:T(8,128)S(1)} %get-tuple-element.53), channel_id=1, source_target_pairs={{16,32},{48,64},{80,96},{32,16},{64,48},{96,80},{17,33},{49,65},{8... | collective-permute-start | bytes 786440 | tf_op jit(solution)/shard_map/ppermute | solution.py:539
  28.7 14.3 %collective-permute-start.4 = (f32[2,128,256]{2,1,0:T(8,128)S(1)}, f32[2,128,256]{2,1,0:T(8,128)S(1)}, u32[]{:S(2)}, u32[]{:S(2)}) collective-permute-start(f32[2,128,256]{2,1,0:T(8,128)S(1)} %get-tuple-element.54), channel_id=1, source_target_pairs={{0,16},{32,48},{64,80},{96,112},{16,0},{48,32},{80,64},{112,96},{1... | collective-permute-start | bytes 786440 | tf_op jit(solution)/shard_map/ppermute | solution.py:539
  44.6 29.0 %collective-permute-start.6 = (f32[2,512,128]{2,1,0:T(8,128)}, f32[2,512,128]{2,1,0:T(8,128)}, u32[]{:S(2)}, u32[]{:S(2)}) collective-permute-start(f32[2,512,128]{2,1,0:T(8,128)} %get-tuple-element.34), channel_id=1, source_target_pairs={{0,1},{2,3},{4,5},{6,7},{8,9},{10,11},{12,13},{14,15},{1,0},{3,2},... | collective-permute-start | bytes 1572872 | tf_op jit(solution)/shard_map/ppermute | solution.py:539
  44.7 29.0 %collective-permute-start.7 = (f32[2,512,128]{2,1,0:T(8,128)}, f32[2,512,128]{2,1,0:T(8,128)}, u32[]{:S(2)}, u32[]{:S(2)}) collective-permute-start(f32[2,512,128]{2,1,0:T(8,128)} %get-tuple-element.35), channel_id=1, source_target_pairs={{1,2},{3,4},{5,6},{7,8},{9,10},{11,12},{13,14},{2,1},{4,3},{6,5},{... | collective-permute-start | bytes 1572872 | tf_op jit(solution)/shard_map/ppermute | solution.py:539
  55.0 1.6 %copy-start = (bf16[8,768,256]{2,1,0:T(8,128)(2,1)}, bf16[8,768,256]{2,1,0:T(8,128)(2,1)S(1)}, u32[]{:S(2)}) copy-start(bf16[8,768,256]{2,1,0:T(8,128)(2,1)S(1)} %get-tuple-element.32.right_ref.right_back) | copy-start | bytes 9437188
  64.1 9.5 %copy-start.3 = (f32[8,256,256]{2,1,0:T(8,128)S(1)}, f32[8,256,256]{2,1,0:T(8,128)}, u32[]{:S(2)}) copy-start(f32[8,256,256]{2,1,0:T(8,128)} %sort_patterns.1.sorted_ref) | copy-start | bytes 6291460
  64.1 9.5 %copy-start.6 = (f32[2,256,256]{2,1,0:T(8,128)S(1)}, f32[2,256,256]{2,1,0:T(8,128)}, u32[]{:S(2)}) copy-start(f32[2,256,256]{2,1,0:T(8,128)} %own_ref.3) | copy-start | bytes 1572868
  64.1 9.6 %copy-start.17 = (f32[2,128,256]{2,1,0:T(8,128)S(1)}, f32[2,128,256]{2,1,0:T(8,128)}, u32[]{:S(2)}) copy-start(f32[2,128,256]{2,1,0:T(8,128)} %copy-done.16) | copy-start | bytes 786436
  64.1 9.6 %copy-start.19 = (f32[2,128,256]{2,1,0:T(8,128)S(1)}, f32[2,128,256]{2,1,0:T(8,128)}, u32[]{:S(2)}) copy-start(f32[2,128,256]{2,1,0:T(8,128)} %copy-done.18) | copy-start | bytes 786436
  87.9 10.2 %copy-start.7 = (f32[2,512,256]{2,1,0:T(8,128)}, f32[2,512,256]{2,1,0:T(8,128)S(1)}, u32[]{:S(2)}) copy-start(f32[2,512,256]{2,1,0:T(8,128)S(1)} %get-tuple-element.45.mid_ref) | copy-start | bytes 3145732
  100.7 31.2 %copy-start.10 = (f32[2,512,256]{2,1,0:T(8,128)S(1)}, f32[2,512,256]{2,1,0:T(8,128)}, u32[]{:S(2)}) copy-start(f32[2,512,256]{2,1,0:T(8,128)} %copy-done.9) | copy-start | bytes 3145732
  100.7 42.5 %copy-start.8 = (f32[2,512,256]{2,1,0:T(8,128)S(1)}, f32[2,512,256]{2,1,0:T(8,128)}, u32[]{:S(2)}) copy-start(f32[2,512,256]{2,1,0:T(8,128)} %copy-done.7) | copy-start | bytes 3145732
  100.7 1.7 %collective-permute-start.16 = (f32[3,128,256]{2,1,0:T(8,128)S(1)}, f32[3,128,256]{2,1,0:T(8,128)S(1)}, u32[]{:S(2)}, u32[]{:S(2)}) collective-permute-start(f32[3,128,256]{2,1,0:T(8,128)S(1)} %get-tuple-element.52), channel_id=1, source_target_pairs={{0,1},{2,3},{4,5},{6,7},{8,9},{10,11},{12,13},{14,15},{1,0},{3,2},... | collective-permute-start | bytes 1179656 | tf_op jit(solution)/shard_map/ppermute | solution.py:539
  103.8 19.2 %all-to-all-start = ((f32[64,16,128]{2,1,0:T(8,128)}), f32[64,16,128]{2,1,0:T(8,128)S(1)}, u32[]{:S(2)}, u32[]{:S(2)}) async-start(f32[64,16,128]{2,1,0:T(8,128)} %shard_map.112), calls=%async_computation | async-start | bytes 1048576 | tf_op jit(solution)/shard_map/all_to_all | solution.py:545
  111.8 18.4 %collective-permute-start.8 = (f32[2,512,128]{2,1,0:T(8,128)}, f32[2,512,128]{2,1,0:T(8,128)}, u32[]{:S(2)}, u32[]{:S(2)}) collective-permute-start(f32[2,512,128]{2,1,0:T(8,128)} %copy-done.23), channel_id=1, source_target_pairs={{0,1},{2,3},{4,5},{6,7},{8,9},{10,11},{12,13},{14,15},{1,0},{3,2},... | collective-permute-start | bytes 1572872 | tf_op jit(solution)/shard_map/ppermute | solution.py:539
  112.6 19.3 %collective-permute-start.9 = (f32[2,512,128]{2,1,0:T(8,128)}, f32[2,512,128]{2,1,0:T(8,128)}, u32[]{:S(2)}, u32[]{:S(2)}) collective-permute-start(f32[2,512,128]{2,1,0:T(8,128)} %copy-done.22), channel_id=1, source_target_pairs={{1,2},{3,4},{5,6},{7,8},{9,10},{11,12},{13,14},{2,1},{4,3},{6,5},{... | collective-permute-start | bytes 1572872 | tf_op jit(solution)/shard_map/ppermute | solution.py:539
  115.9 24.0 %collective-permute-start.12 = (f32[2,512,128]{2,1,0:T(8,128)}, f32[2,512,128]{2,1,0:T(8,128)S(1)}, u32[]{:S(2)}, u32[]{:S(2)}) collective-permute-start(f32[2,512,128]{2,1,0:T(8,128)} %copy-done.21), channel_id=1, source_target_pairs={{0,1},{2,3},{4,5},{6,7},{8,9},{10,11},{12,13},{14,15},{1,0},{3,2},... | collective-permute-start | bytes 1572872 | tf_op jit(solution)/shard_map/ppermute | solution.py:539
  116.0 27.2 %collective-permute-start.13 = (f32[2,512,128]{2,1,0:T(8,128)}, f32[2,512,128]{2,1,0:T(8,128)}, u32[]{:S(2)}, u32[]{:S(2)}) collective-permute-start(f32[2,512,128]{2,1,0:T(8,128)} %copy-done.20), channel_id=1, source_target_pairs={{1,2},{3,4},{5,6},{7,8},{9,10},{11,12},{13,14},{2,1},{4,3},{6,5},{... | collective-permute-start | bytes 1572872 | tf_op jit(solution)/shard_map/ppermute | solution.py:539
  124.3 26.8 %all-to-all-start.1 = ((f32[64,8,128]{2,1,0:T(8,128)}), f32[64,8,128]{2,1,0:T(8,128)S(1)}, u32[]{:S(2)}, u32[]{:S(2)}) async-start(f32[64,8,128]{2,1,0:T(8,128)} %shard_map.113), calls=%async_computation.1 | async-start | bytes 524288 | tf_op jit(solution)/shard_map/all_to_all | solution.py:545
  134.5 12.5 %copy-start.14 = (f32[2,256,256]{2,1,0:T(8,128)}, f32[2,256,256]{2,1,0:T(8,128)S(1)}, u32[]{:S(2)}) copy-start(f32[2,256,256]{2,1,0:T(8,128)S(1)} %get-tuple-element.42.center_ref) | copy-start | bytes 1572868
  134.5 16.7 %collective-permute-start.10 = (f32[2,128,256]{2,1,0:T(8,128)}, f32[2,128,256]{2,1,0:T(8,128)S(1)}, u32[]{:S(2)}, u32[]{:S(2)}) collective-permute-start(f32[2,128,256]{2,1,0:T(8,128)} %get-tuple-element.43), channel_id=1, source_target_pairs={{0,16},{32,48},{64,80},{96,112},{16,0},{48,32},{80,64},{112,96},{1... | collective-permute-start | bytes 786440 | tf_op jit(solution)/shard_map/ppermute | solution.py:539
  135.7 16.1 %collective-permute-start.11 = (f32[2,128,256]{2,1,0:T(8,128)S(1)}, f32[2,128,256]{2,1,0:T(8,128)S(1)}, u32[]{:S(2)}, u32[]{:S(2)}) collective-permute-start(f32[2,128,256]{2,1,0:T(8,128)S(1)} %get-tuple-element.44), channel_id=1, source_target_pairs={{16,32},{48,64},{80,96},{32,16},{64,48},{96,80},{17,33},{49,65},{8... | collective-permute-start | bytes 786440 | tf_op jit(solution)/shard_map/ppermute | solution.py:539
  145.6 8.6 %collective-permute-start.14 = (f32[2,128,256]{2,1,0:T(8,128)}, f32[2,128,256]{2,1,0:T(8,128)S(1)}, u32[]{:S(2)}, u32[]{:S(2)}) collective-permute-start(f32[2,128,256]{2,1,0:T(8,128)} %get-tuple-element.49), channel_id=1, source_target_pairs={{0,16},{32,48},{64,80},{96,112},{16,0},{48,32},{80,64},{112,96},{1... | collective-permute-start | bytes 786440 | tf_op jit(solution)/shard_map/ppermute | solution.py:539
  147.0 12.5 %collective-permute-start.15 = (f32[2,128,256]{2,1,0:T(8,128)S(1)}, f32[2,128,256]{2,1,0:T(8,128)S(1)}, u32[]{:S(2)}, u32[]{:S(2)}) collective-permute-start(f32[2,128,256]{2,1,0:T(8,128)S(1)} %get-tuple-element.50), channel_id=1, source_target_pairs={{16,32},{48,64},{80,96},{32,16},{64,48},{96,80},{17,33},{49,65},{8... | collective-permute-start | bytes 786440 | tf_op jit(solution)/shard_map/ppermute | solution.py:539
  151.1 9.8 %collective-permute-start.17 = (f32[64,8,128]{2,1,0:T(8,128)S(1)}, f32[64,8,128]{2,1,0:T(8,128)S(1)}, u32[]{:S(2)}, u32[]{:S(2)}) collective-permute-start(f32[64,8,128]{2,1,0:T(8,128)S(1)} %all-to-all-done.1.own_ref), channel_id=1, source_target_pairs={{0,1},{2,3},{4,5},{6,7},{8,9},{10,11},{12,13},{14,15},{1,0},{3,2},... | collective-permute-start | bytes 786440 | tf_op jit(solution)/shard_map/ppermute | solution.py:539
  (13 other events, 14.3 us)
